TPU v7x, 256 devices: a whole 4x4x8 slice. The times are simulated.
256 devices in a mesh: gx: 32 (over y_hi, z, core), gy: 8 (over y_lo, x).
Axes of the slice: x: 4, y: 4 (y_hi: 2, y_lo: 2; y = y_hi * 2 + y_lo), z: 8, core: 2. Of those that a mesh axis runs over, the one named last changes fastest.
Arguments:
- state_field: bfloat16 [1, 64, 2048, 2048], P(None, None, 'gx', 'gy'), may hold values from -6 to 6
- spectral_x: bfloat16 [2, 32, 2, 64, 64], P(None, 'gx'), may hold values from -2 to 2
- spectral_y: bfloat16 [2, 32, 2, 64, 64], P(None, 'gy'), may hold values from -2 to 2
- expand_weight: bfloat16 [2, 64, 256], replicated, may hold values from -0.75 to 0.75
- reduce_weight: bfloat16 [2, 256, 64], replicated, may hold values from -0.375 to 0.375
Outputs:
- next_state: bfloat16 [1, 64, 2048, 2048], P(None, None, 'gx', 'gy')
All inputs are finite; a program needn't handle non-finite values.
Results may differ from a plain program's by a relative error of at most 0.025.
Values may be sent and summed in bfloat16 or wider, within the bound.
No kernel may reach another device: no remote copies, remote signals or barrier semaphores. Data moves between devices by JAX's collectives and lax.ppermute only.
A program may use at most 64 MiB of HBM per device.

v0:
```python
import functools

import jax
import jax.numpy as jnp
import numpy as np
from jax import lax
from jax.experimental import pallas as pl
from jax.experimental.pallas import tpu as pltpu
from jax.sharding import PartitionSpec as P

F32 = jnp.float32
BF16 = jnp.bfloat16
NX = 2048
NY = 2048
CH = 64
HID = 256
MODES = 32
LAYERS = 2
RX = 10
RY = 20
RYP = 24
GROUP = 16
WIDE = GROUP * CH
LINE = 8


def window_tables(length, devices, rank):
    window = length // devices
    k = np.arange(MODES)[:, None]
    p = np.arange(length)[None, :]
    angle = 2.0 * np.pi * ((k * p) % length) / length
    scale = 1.0 / np.sqrt(length)
    weight = np.where(np.arange(MODES) == 0, 1.0, 2.0)[:, None]
    forward = np.concatenate([np.cos(angle), -np.sin(angle)], 0) * scale
    inverse = np.concatenate([weight * np.cos(angle), -weight * np.sin(angle)], 0) * scale
    _, _, vt = np.linalg.svd(forward[:, :window], full_matrices=False)
    basis = vt[:rank]
    basis = basis * np.sign(basis[np.arange(rank), np.abs(basis).argmax(1)])[:, None]
    fwd = np.stack([forward[:, d * window : (d + 1) * window] @ basis.T for d in range(devices)])
    inv = np.stack([inverse[:, d * window : (d + 1) * window] @ basis.T for d in range(devices)])
    return basis, fwd, inv


SHIFTS = ((1, 0), (0, 1), (0, 3), (1, 2), (0, 2), (1, 1), (1, 3))
UNROLL = 4
QUARTER = 16 * 64


def moved(me, flip, step):
    return (me // 4 ^ flip) * 4 + (me + step) % 4


def bf(x):
    return np.asarray(x, np.float32).astype(jnp.bfloat16)


def make_constants():
    bx, fx, ix = window_tables(NX, 32, RX)
    by, fy, iy = window_tables(NY, 8, RY)
    pairs = RX // 2
    ax = fx.reshape(32, 64, pairs, 2).transpose(3, 1, 2, 0).reshape(128, pairs * 32)
    gx = ix.reshape(32, 2, MODES, pairs, 2)
    u0 = gx[..., 0].transpose(3, 0, 1, 2).reshape(pairs * 32, 64)
    u1 = gx[..., 1].transpose(3, 0, 1, 2)[:, :, ::-1].reshape(pairs * 32, 64)
    mid_x = np.zeros((128 + pairs * 32, 256))
    mid_x[:128, : pairs * 32] = ax
    mid_x[128:, :64] = u0
    mid_x[128:, 64:128] = u1
    mid_y = np.zeros((2, 8, RYP, 128))
    mid_y[0, :, :RY, :64] = fy.transpose(0, 2, 1)
    mid_y[1, :, :RY, :64] = iy.transpose(0, 2, 1)
    cy = np.pad(by, ((0, RYP - RY), (0, 0)))
    bx = np.pad(bx, ((0, 16 - RX), (0, 128 - 64)))
    return dict(mid_x=bf(mid_x), mid_y=bf(mid_y), cy=bf(cy), bx=bf(bx))


def dot(a, b):
    return jnp.dot(a, b, preferred_element_type=F32)


def dot_nt(a, b):
    return lax.dot_general(a, b, (((1,), (1,)), ((), ())), preferred_element_type=F32)


def half_mask(rows):
    return lax.broadcasted_iota(jnp.int32, (rows, 128), 1) < 64


def dot_tn(a, b):
    return lax.dot_general(a, b, (((0,), (0,)), ((), ())), preferred_element_type=F32)


def estimate(us):
    return pl.CostEstimate(flops=int(us * 1e9), bytes_accessed=1 << 20, transcendentals=0)


def params(mib):
    return pltpu.CompilerParams(vmem_limit_bytes=mib << 20)


def fill_kron(bx_ref, kron_ref):
    lanes = lax.broadcasted_iota(jnp.int32, (CH, WIDE), 1)
    rows = lax.broadcasted_iota(jnp.int32, (CH, WIDE), 0)
    eye = (lanes % CH) == rows
    x = lax.broadcasted_iota(jnp.int32, (128, WIDE), 1) // CH + GROUP * pl.program_id(0)
    position = lax.broadcasted_iota(jnp.int32, (128, WIDE), 0)
    spread = dot(bx_ref[...], jnp.where(x == position, 1.0, 0.0).astype(BF16))
    for r in range(RX):
        row = jnp.broadcast_to(spread[r : r + 1, :], (CH, WIDE))
        kron_ref[r * CH : (r + 1) * CH, :] = jnp.where(eye, row, 0.0).astype(BF16)


def coefficients(g, state, kron_ref, cy_ref, acc_ref, zx_ref, zy_ref):
    part = dot_nt(state, kron_ref[...])

    @pl.when(g == 0)
    def _():
        acc_ref[...] = part

    @pl.when(g > 0)
    def _():
        acc_ref[...] += part

    zy_ref[0] = dot(cy_ref[...], state).astype(BF16)

    @pl.when(g == pl.num_programs(0) - 1)
    def _():
        zx_ref[...] = acc_ref[...].astype(BF16)


def first_kernel(field_ref, bx_ref, cy_ref, state_ref, zx_ref, zy_ref, t_ref, kron_ref, acc_ref):
    for h in range(2):
        part = field_ref[:, :, h * 128 : (h + 1) * 128].astype(F32)
        t_ref[h] = part.reshape(CH * GROUP, 128)
    for h in range(2):
        for p in range(GROUP // 2):
            two = [t_ref[h, pl.ds(2 * p + j, CH, stride=GROUP), :] for j in range(2)]
            block = jnp.concatenate(two, axis=0).T.astype(BF16)
            state_ref[h * 128 : (h + 1) * 128, p * 128 : (p + 1) * 128] = block
    fill_kron(bx_ref, kron_ref)
    coefficients(pl.program_id(0), state_ref[...], kron_ref, cy_ref, acc_ref, zx_ref, zy_ref)


def first_call(field, c):
    return pl.pallas_call(
        first_kernel,
        name="first",
        grid=(64 // GROUP,),
        in_specs=[
            pl.BlockSpec((CH, GROUP, 256), lambda g: (0, g, 0)),
            pl.BlockSpec((16, 128), lambda g: (0, 0)),
            pl.BlockSpec((RYP, 256), lambda g: (0, 0)),
        ],
        out_specs=[
            pl.BlockSpec((256, WIDE), lambda g: (0, g)),
            pl.BlockSpec((256, RX * CH), lambda g: (0, 0)),
            pl.BlockSpec((1, RYP, WIDE), lambda g: (g, 0, 0)),
        ],
        out_shape=[
            jax.ShapeDtypeStruct((256, 4096), BF16),
            jax.ShapeDtypeStruct((256, RX * CH), BF16),
            jax.ShapeDtypeStruct((4, RYP, QUARTER), BF16),
        ],
        scratch_shapes=[
            pltpu.VMEM((2, CH * GROUP, 128), F32),
            pltpu.VMEM((RX * CH, WIDE), BF16),
            pltpu.VMEM((256, RX * CH), F32),
        ],
        compiler_params=params(36),
        cost_estimate=estimate(10),
    )(field, c["bx"], c["cy"])


def mode_weights(w, sign):
    w = w.astype(F32)
    return jnp.concatenate([w * sign, pltpu.roll(w, 64, 1)], axis=0).astype(BF16)


def mix(xs_ref, ms_ref, lines, steps, weights):
    sign = jnp.where(half_mask(CH), 1.0, -1.0)

    def product(i, _):
        for mode, w in weights(i):
            rows = pl.ds(pl.multiple_of(mode * lines, lines), lines)
            ms_ref[rows, :] = dot_nt(xs_ref[rows, :].astype(BF16), mode_weights(w, sign))

    lax.fori_loop(0, steps, product, None, unroll=UNROLL)


def mid_x_kernel(core_ref, recv_ref, w0_ref, w1_ref, tab_ref, *refs):
    send_ref, r_ref, xs_ref, ms_ref, o_ref = refs
    pairs = RX // 2
    first = half_mask(MODES)
    for p in range(pairs):
        part = recv_ref[:, :, p * 128 : (p + 1) * 128]
        r_ref[p] = part.reshape(256, 128).astype(F32)
    cols = []
    for y in range(LINE):
        ry = [r_ref[p, pl.ds(y, 32, stride=LINE), :] for p in range(pairs)]
        cols.append(jnp.concatenate(ry, axis=0).astype(BF16))
    spec = dot(tab_ref[:128, : pairs * 32], jnp.concatenate(cols, axis=1))
    for y in range(LINE):
        s = spec[:, y * 128 : (y + 1) * 128]
        x = jnp.where(first, s[0:32], s[96:128])
        x = x + pltpu.roll(jnp.where(first, s[32:64], s[64:96]), 64, 1)
        xs_ref[pl.ds(y, MODES, stride=LINE), :] = x
    core = core_ref[0]
    weights = lambda t: [(t * 2 + core, w0_ref[t, 0]), (t * 2 + 1 - core, w1_ref[t, 0])]
    mix(xs_ref, ms_ref, LINE, 16, weights)
    cols = []
    for y in range(LINE):
        m = ms_ref[pl.ds(y, MODES, stride=LINE), :]
        cols.append(jnp.concatenate([m, pltpu.roll(m, 64, 1)], axis=0).astype(BF16))
    cols = jnp.concatenate(cols, axis=1)
    out0 = dot(tab_ref[128:, :64], cols)
    out1 = dot(tab_ref[128:, 64:128], cols)
    for y in range(LINE):
        for p in range(pairs):
            v0 = out0[p * 32 : (p + 1) * 32, y * 128 : (y + 1) * 128]
            v1 = out1[p * 32 : (p + 1) * 32, y * 128 : (y + 1) * 128]
            o_ref[p, pl.ds(y, 32, stride=LINE), :] = jnp.where(first, v0, v1)
    for p in range(pairs):
        part = o_ref[p].reshape(32, LINE, 128).astype(BF16)
        send_ref[:, :, p * 128 : (p + 1) * 128] = part


def whole(a):
    return pl.BlockSpec(a.shape, lambda *_: (0,) * a.ndim)


def mid_x(layer, core, recv, w0, w1, c):
    weights = pl.BlockSpec((16, 1, CH, 128), lambda i: (0, layer, 0, 0))
    return pl.pallas_call(
        mid_x_kernel,
        name="mid_x",
        grid=(1,),
        in_specs=[pl.BlockSpec(memory_space=pltpu.SMEM)]
        + [whole(recv), weights, weights, whole(c["mid_x"])],
        out_specs=whole(recv),
        out_shape=jax.ShapeDtypeStruct(recv.shape, BF16),
        scratch_shapes=[
            pltpu.VMEM((RX // 2, 256, 128), F32),
            pltpu.VMEM((MODES * LINE, 128), F32),
            pltpu.VMEM((MODES * LINE, 128), F32),
            pltpu.VMEM((RX // 2, 256, 128), F32),
        ],
        compiler_params=params(16),
        cost_estimate=estimate(3),
    )(core, recv, w0, w1, c["mid_x"])


def mid_y_kernel(me_ref, *refs):
    z_refs = refs[:8]
    w_ref, tab_ref = refs[8:10]
    out_refs = refs[10:14]
    xs_ref, ms_ref = refs[14:]
    first = half_mask(MODES)
    lines = 16
    half, quarter = me_ref[0] // 4, lax.rem(me_ref[0], 4)
    table = []
    for flip, step in ((0, 0),) + SHIFTS:
        near = half + flip - 2 * flip * half
        table.append(tab_ref[0, near * 4 + lax.rem(quarter + 4 - step, 4)].astype(F32))
    forward = jnp.concatenate(table, axis=0).T[:64].astype(BF16)
    table = [tab_ref[1, half * 4 + lax.rem(quarter + step, 4)].astype(F32) for step in range(4)]
    inverse = jnp.concatenate(table, axis=0)[:, :64].astype(BF16)
    for g in range(2):
        z = [ref[:, g * 512 : (g + 1) * 512].astype(F32) for ref in z_refs]
        z = jnp.concatenate(z, axis=0).astype(BF16)
        spec = dot(forward, z)
        for b in range(4):
            re = spec[0:32, b * 128 : (b + 1) * 128]
            im = spec[32:64, b * 128 : (b + 1) * 128]
            line = g * 8 + 2 * b
            xs_ref[pl.ds(line, MODES, stride=lines), :] = jnp.where(
                first, re, pltpu.roll(im, 64, 1)
            )
            xs_ref[pl.ds(line + 1, MODES, stride=lines), :] = jnp.where(
                first, pltpu.roll(re, 64, 1), im
            )
    weights = lambda src: [(src * 4 + j, w_ref[src, 0, j]) for j in range(4)]
    mix(xs_ref, ms_ref, lines, 8, weights)
    for g in range(2):
        cols = []
        for b in range(4):
            line = g * 8 + 2 * b
            m0 = ms_ref[pl.ds(line, MODES, stride=lines), :]
            m1 = ms_ref[pl.ds(line + 1, MODES, stride=lines), :]
            re = jnp.where(first, m0, pltpu.roll(m1, 64, 1))
            im = jnp.where(first, pltpu.roll(m0, 64, 1), m1)
            cols.append(jnp.concatenate([re, im], axis=0).astype(BF16))
        out = dot(inverse, jnp.concatenate(cols, axis=1)).astype(BF16)
        for step in range(4):
            out_refs[step][:, g * 512 : (g + 1) * 512] = out[step * RYP : (step + 1) * RYP]


def mid_y(layer, me, zs, w, c):
    table = c["mid_y"]
    return pl.pallas_call(
        mid_y_kernel,
        name="mid_y",
        grid_spec=pltpu.PrefetchScalarGridSpec(
            num_scalar_prefetch=1,
            grid=(1,),
            in_specs=[whole(z) for z in zs]
            + [
                pl.BlockSpec((8, 1, 4, CH, 128), lambda i, me: (0, layer, 0, 0, 0)),
                whole(table),
            ],
            out_specs=[pl.BlockSpec((RYP, QUARTER), lambda i, me: (0, 0))] * 4,
            scratch_shapes=[pltpu.VMEM((MODES * 16, 128), F32)] * 2,
        ),
        out_shape=[jax.ShapeDtypeStruct((RYP, QUARTER), BF16)] * 4,
        compiler_params=params(20),
        cost_estimate=estimate(2),
    )(me, *zs, w, table)


def gelu(x):
    x = x.astype(BF16)
    inner = x * (0.7978845608028654 + 0.035677408136300125 * (x * x))
    half = 0.5 * x
    return half + half * jnp.tanh(inner)


def last_kernel(more, *refs):
    me_ref, yx_ref, bx_ref = refs[:3]
    yy_refs = refs[3:7]
    cy_ref, state_ref, we_ref, wr_ref = refs[7:11]
    if more:
        out_ref, zx_ref, zy_ref, kron_ref, we4_ref, wr4_ref, yy_ref, acc_ref = refs[11:]
    else:
        out_ref, kron_ref, we4_ref, wr4_ref, yy_ref, t_ref = refs[11:]
    g = pl.program_id(0)

    @pl.when(g == 0)
    def _():
        we4_ref[...] = jnp.zeros_like(we4_ref)
        wr4_ref[...] = jnp.zeros_like(wr4_ref)
        for j in range(4):
            we4_ref[j * CH : (j + 1) * CH, j * HID : (j + 1) * HID] = we_ref[0]
            wr4_ref[j * CH : (j + 1) * CH, j * HID : (j + 1) * HID] = wr_ref[0]
        for step in range(4):
            yy_ref[lax.rem(me_ref[0] + 4 - step, 4)] = yy_refs[step][...]

    fill_kron(bx_ref, kron_ref)
    basis = cy_ref[...].astype(F32).T.astype(BF16)
    yy = yy_ref[g]
    for j in range(WIDE // 256):
        lanes = slice(j * 256, (j + 1) * 256)
        if j % 2 == 0:
            both = slice(j * 256, (j + 2) * 256)
            total = dot(yx_ref[...], kron_ref[:, both]) + dot(basis, yy[:, both])
            total = total.astype(BF16)
            total = jnp.concatenate([total[:, :256], total[:, 256:]], axis=0)
            hidden = gelu(dot(total, we4_ref[...])).astype(BF16)
            updates = dot_nt(hidden, wr4_ref[...])
        update = updates[(j % 2) * 256 : (j % 2 + 1) * 256]
        new = state_ref[:, lanes].astype(F32) + update
        if more:
            out_ref[:, lanes] = new.astype(BF16)
            continue
        for h in range(2):
            for p in range(2):
                block = new[h * 128 : (h + 1) * 128, p * 128 : (p + 1) * 128].T
                x = j * 4 + p * 2
                t_ref[h, pl.ds(x, CH, stride=GROUP), :] = block[:CH]
                t_ref[h, pl.ds(x + 1, CH, stride=GROUP), :] = block[CH:]
    if more:
        coefficients(g, out_ref[...], kron_ref, cy_ref, acc_ref, zx_ref, zy_ref)
    else:
        for h in range(2):
            part = t_ref[h].reshape(CH, GROUP, 128).astype(BF16)
            out_ref[:, :, h * 128 : (h + 1) * 128] = part


def last_call(layer, more, me, yx, yy, state, we, wr, c):
    in_specs = [
        pl.BlockSpec(memory_space=pltpu.SMEM),
        pl.BlockSpec((256, RX * CH), lambda g: (0, 0)),
        pl.BlockSpec((16, 128), lambda g: (0, 0)),
        *[pl.BlockSpec((RYP, QUARTER), lambda g: (0, 0))] * 4,
        pl.BlockSpec((RYP, 256), lambda g: (0, 0)),
        pl.BlockSpec((256, WIDE), lambda g: (0, g)),
        pl.BlockSpec((1, CH, HID), lambda g: (layer, 0, 0)),
        pl.BlockSpec((1, CH, HID), lambda g: (layer, 0, 0)),
    ]
    scratch = [pltpu.VMEM((RX * CH, WIDE), BF16)] + [pltpu.VMEM((256, 1024), BF16)] * 2
    scratch.append(pltpu.VMEM((4, RYP, QUARTER), BF16))
    if more:
        out_specs = [
            pl.BlockSpec((256, WIDE), lambda g: (0, g)),
            pl.BlockSpec((256, RX * CH), lambda g: (0, 0)),
            pl.BlockSpec((1, RYP, WIDE), lambda g: (g, 0, 0)),
        ]
        out_shape = [
            jax.ShapeDtypeStruct((256, 4096), BF16),
            jax.ShapeDtypeStruct((256, RX * CH), BF16),
            jax.ShapeDtypeStruct((4, RYP, QUARTER), BF16),
        ]
        scratch.append(pltpu.VMEM((256, RX * CH), F32))
    else:
        out_specs = [pl.BlockSpec((CH, GROUP, 256), lambda g: (0, g, 0))]
        out_shape = [jax.ShapeDtypeStruct((CH, 64, 256), BF16)]
        scratch.append(pltpu.VMEM((2, CH * GROUP, 128), F32))
    return pl.pallas_call(
        functools.partial(last_kernel, more),
        name="last",
        grid=(64 // GROUP,),
        in_specs=in_specs,
        out_specs=out_specs,
        out_shape=out_shape,
        scratch_shapes=scratch,
        compiler_params=params(40),
        cost_estimate=estimate(12),
    )(me, yx, c["bx"], *yy, c["cy"], state, we, wr)


def join(w):
    return jnp.concatenate([w[..., 0, :, :], w[..., 1, :, :]], axis=-1)


def exchange_weights(own):
    same_core = [list(range(s, 32, 2)) for s in range(2)]
    mine = jnp.broadcast_to(own[None], (16, LAYERS, CH, 128))
    mine = lax.all_to_all(mine, "gx", 0, 0, axis_index_groups=same_core, tiled=True)
    return mine, lax.ppermute(mine, "gx", [(i, i ^ 1) for i in range(32)])


def permute_y(x, flip, step):
    return lax.ppermute(x, "gy", [(i, moved(i, flip, step)) for i in range(8)])


def body(state_field, spectral_x, spectral_y, expand_weight, reduce_weight):
    c = {name: jnp.asarray(value) for name, value in make_constants().items()}
    core = lax.rem(lax.axis_index("gx"), 2).reshape(1).astype(jnp.int32)
    me = lax.axis_index("gy").reshape(1).astype(jnp.int32)
    own_x, own_y = join(spectral_x)[:, 0], join(spectral_y)
    own_x, own_y = lax.optimization_barrier((own_x, own_y))
    wy = lax.all_gather(own_y, "gy", axis=0)
    wx = exchange_weights(own_x)
    wr = jnp.swapaxes(reduce_weight, 1, 2)
    state, zx, zy = first_call(state_field[0], c)
    for l in range(LAYERS):
        recv = lax.all_to_all(zx.reshape(32, LINE, RX * CH), "gx", 0, 0, tiled=True)
        zs = []
        for flip, step in ((0, 0),) + SHIFTS:
            chunk = lax.dynamic_slice_in_dim(zy, lax.rem(me[0] + step, 4), 1, 0)[0]
            zs.append(permute_y(chunk, flip, step) if flip or step else chunk)
        zs, recv = lax.optimization_barrier((zs, recv))
        send = mid_x(l, core, recv, wx[0], wx[1], c)
        yx = lax.all_to_all(send, "gx", 0, 0, tiled=True).reshape(256, RX * CH)
        yy = mid_y(l, me, zs, wy, c)
        yy = [yy[0]] + [permute_y(yy[step], 0, step) for step in range(1, 4)]
        more = l + 1 < LAYERS
        got = last_call(l, more, me, yx, yy, state, expand_weight, wr, c)
        if more:
            state, zx, zy = got
    return got[0][None]


def solution(mesh):
    in_specs = (
        P(None, None, "gx", "gy"),
        P(None, "gx", None, None, None),
        P(None, "gy", None, None, None),
        P(),
        P(),
    )
    out_specs = P(None, None, "gx", "gy")
    return jax.shard_map(body, mesh=mesh, in_specs=in_specs, out_specs=out_specs, check_vma=False)
```

profile of v0, /device:TPU:1, one launch (start us, length us, event | category | flops | bytes accessed | tf_op | source)
XLA Modules:
  0.0 173.3 jit_solution(7800940485510870474)
XLA Ops:
  6.5 0.9 slice_bitcast_fusion.3
  7.5 1.0 slice_bitcast_fusion.1
  8.5 0.1 maximum_bitcast_fusion
  8.6 0.8 pad_maximum_fusion
  9.3 0.9 broadcast_in_dim.4
  10.2 11.7 %all-to-all-start.1 = ((bf16[16,2,64,128]{3,2,1,0:T(8,128)(2,1)}), bf16[16,2,64,128]{3,2,1,0:T(8,128)(2,1)S(1)}, u32[]{:S(2)}, u32[]{:S(2)}) async-start(bf16[16,2,64,128]{3,2,1,0:T(8,128)(2,1)} %broadcast_in_dim.4), calls=%async_computation.1 | async-start | bytes 1048576 | tf_op jit(solution)/shard_map/all_to_all | solution.py:426
  22.0 0.0 all-gather.3.cloned.1.call-start
  22.1 0.7 all-gather.3.cloned.1.call-update
  22.8 6.1 %first.1 = (bf16[256,4096]{1,0:T(8,128)(2,1)S(1)}, bf16[256,640]{1,0:T(8,128)(2,1)}, bf16[4,24,1024]{2,1,0:T(8,128)(2,1)S(1)}) custom-call(bf16[64,64,256]{2,1,0:T(8,128)(2,1)S(1)} %bitcast.44, bf16[16,128]{1,0:T(8,128)(2,1)S(1)} %copy-done.8, bf16[24,256]{1,0:T(8,128)(2,1)S(1)} %copy-done.7), custom_call_target="tpu_custom_call" | custom-call | flops 10000000000 | bytes 1048576 | tf_op jit(solution)/shard_map/first/pallas_call | solution.py:145
  28.9 1.3 copy-done.9
  30.2 7.1 %all-to-all-done.1.w0_ref = bf16[16,2,64,128]{3,2,1,0:T(8,128)(2,1)S(1)} async-done(((bf16[16,2,64,128]{3,2,1,0:T(8,128)(2,1)}), bf16[16,2,64,128]{3,2,1,0:T(8,128)(2,1)S(1)}, u32[]{:S(2)}, u32[]{:S(2)}) %all-to-all-start.1) | async-done | bytes 524320 | tf_op jit(solution)/shard_map/all_to_all | solution.py:426
  37.3 7.5 %all-to-all-start = ((bf16[32,8,640]{2,1,0:T(8,128)(2,1)}), bf16[32,8,640]{2,1,0:T(8,128)(2,1)S(1)}, u32[]{:S(2)}, u32[]{:S(2)}) async-start(bf16[32,8,640]{2,1,0:T(8,128)(2,1)} %bitcast.7), calls=%async_computation | async-start | bytes 655360 | tf_op jit(solution)/shard_map/all_to_all | solution.py:445
  44.8 0.3 collective-permute-start.7
  45.1 2.8 %collective-permute-start.4 = (bf16[24,1024]{1,0:T(8,128)(2,1)S(1)}, bf16[24,1024]{1,0:T(8,128)(2,1)S(1)}, u32[]{:S(2)}, u32[]{:S(2)}) collective-permute-start(bf16[24,1024]{1,0:T(8,128)(2,1)S(1)} %get-tuple-element.79), channel_id=1, source_target_pairs={{0,2},{1,3},{2,0},{3,1},{4,6},{5,7},{6,4},{7,5},{8,10},{9,11},{10,... | collective-permute-start | bytes 147464 | tf_op jit(solution)/shard_map/ppermute | solution.py:431
  47.9 0.3 collective-permute-start.3
  48.3 3.3 %collective-permute-start.6 = (bf16[24,1024]{1,0:T(8,128)(2,1)S(1)}, bf16[24,1024]{1,0:T(8,128)(2,1)S(1)}, u32[]{:S(2)}, u32[]{:S(2)}) collective-permute-start(bf16[24,1024]{1,0:T(8,128)(2,1)S(1)} %get-tuple-element.80), channel_id=1, source_target_pairs={{0,7},{1,4},{2,5},{3,6},{4,3},{5,0},{6,1},{7,2},{8,15},{9,12},{10,... | collective-permute-start | bytes 147464 | tf_op jit(solution)/shard_map/ppermute | solution.py:431
  51.5 0.5 collective-permute-start.2
  52.1 1.0 collective-permute-start.5
  53.1 1.4 collective-permute-done.3.refs_4_
  54.6 0.1 collective-permute-done.6.refs_7_
  54.6 1.2 collective-permute-start
  55.9 0.2 collective-permute-done.2.refs_3_
  56.1 2.2 %collective-permute-done.5.refs_6_ = bf16[24,1024]{1,0:T(8,128)(2,1)S(1)} collective-permute-done((bf16[24,1024]{1,0:T(8,128)(2,1)S(1)}, bf16[24,1024]{1,0:T(8,128)(2,1)S(1)}, u32[]{:S(2)}, u32[]{:S(2)}) %collective-permute-start.5) | collective-permute-done | bytes 49184 | tf_op jit(solution)/shard_map/ppermute | solution.py:431
  58.3 0.9 collective-permute-done.1.refs_2_
  59.2 0.4 collective-permute-done.refs_1_
  59.6 0.4 all-to-all-done.recv_ref
  60.0 2.8 %mid_x.2 = bf16[32,8,640]{2,1,0:T(8,128)(2,1)} custom-call(s32[1]{0:T(128)} %bitcast.1.core_ref, bf16[32,8,640]{2,1,0:T(8,128)(2,1)S(1)} %all-to-all-done.recv_ref, bf16[16,2,64,128]{3,2,1,0:T(8,128)(2,1)S(1)} %all-to-all-done.1.w0_ref, bf16[16,2,64,128]{3,2,1,0:T(8,128)(2,1)S(1)} %collective-permute-done.7.w1_ref, bf16[288,256]{1,0:T(8,128)(2,1)S(1)} %copy-done.5), custom_call_target="tpu_custom_call" | custom-call | flops 3000000000 | bytes 1048576 | tf_op jit(solution)/shard_map/mid_x/pallas_call | solution.py:233
  62.8 12.5 %all-to-all-start.2 = ((bf16[32,8,640]{2,1,0:T(8,128)(2,1)}), bf16[32,8,640]{2,1,0:T(8,128)(2,1)S(1)}, u32[]{:S(2)}, u32[]{:S(2)}) async-start(bf16[32,8,640]{2,1,0:T(8,128)(2,1)} %mid_x.2), calls=%async_computation.2 | async-start | bytes 655360 | tf_op jit(solution)/shard_map/all_to_all | solution.py:452
  75.3 0.0 all-gather.3.cloned.1.call-done
  75.4 1.2 copy-done.1
  76.6 1.6 mid_y.2
  78.1 0.1 collective-permute-start.8
  78.2 3.4 %collective-permute-start.9 = (bf16[24,1024]{1,0:T(8,128)(2,1)S(1)}, bf16[24,1024]{1,0:T(8,128)(2,1)S(1)}, u32[]{:S(2)}, u32[]{:S(2)}) collective-permute-start(bf16[24,1024]{1,0:T(8,128)(2,1)S(1)} %get-tuple-element.54), channel_id=1, source_target_pairs={{0,2},{1,3},{2,0},{3,1},{4,6},{5,7},{6,4},{7,5},{8,10},{9,11},{10,... | collective-permute-start | bytes 147464 | tf_op jit(solution)/shard_map/ppermute | solution.py:431
  81.6 1.1 collective-permute-done.8.refs_4_
  82.7 1.6 collective-permute-done.9.refs_5_
  84.3 0.5 collective-permute-done.10.refs_6_
  84.8 4.9 %all-to-all-done.2 = bf16[32,8,640]{2,1,0:T(8,128)(2,1)S(1)} async-done(((bf16[32,8,640]{2,1,0:T(8,128)(2,1)}), bf16[32,8,640]{2,1,0:T(8,128)(2,1)S(1)}, u32[]{:S(2)}, u32[]{:S(2)}) %all-to-all-start.2) | async-done | bytes 327712 | tf_op jit(solution)/shard_map/all_to_all | solution.py:452
  89.8 1.6 copy-done.10
  91.4 13.4 %last.2 = (bf16[256,4096]{1,0:T(8,128)(2,1)S(1)}, bf16[256,640]{1,0:T(8,128)(2,1)}, bf16[4,24,1024]{2,1,0:T(8,128)(2,1)S(1)}) custom-call(s32[1]{0:T(128)} %bitcast.me_ref.refs_0_, bf16[256,640]{1,0:T(8,128)(2,1)S(1)} %bitcast.42, bf16[16,128]{1,0:T(8,128)(2,1)S(1)} %copy-done.8, bf16[24,1024]{1,0:T(8,128)(2,1)S(1)} %get-tuple-element.52.refs_3_, ...), custom_call_target="tpu_custom_call" | custom-call | flops 12000000000 | bytes 1048576 | tf_op jit(solution)/shard_map/last/pallas_call | solution.py:406
  104.8 1.3 copy-done.11
  106.1 6.3 %all-to-all-start.3 = ((bf16[32,8,640]{2,1,0:T(8,128)(2,1)}), bf16[32,8,640]{2,1,0:T(8,128)(2,1)S(1)}, u32[]{:S(2)}, u32[]{:S(2)}) async-start(bf16[32,8,640]{2,1,0:T(8,128)(2,1)} %bitcast.20), calls=%async_computation.3 | async-start | bytes 655360 | tf_op jit(solution)/shard_map/all_to_all | solution.py:445
  112.4 1.3 collective-permute-start.15
  113.8 0.9 collective-permute-start.14
  114.7 2.9 %collective-permute-start.17 = (bf16[24,1024]{1,0:T(8,128)(2,1)S(1)}, bf16[24,1024]{1,0:T(8,128)(2,1)S(1)}, u32[]{:S(2)}, u32[]{:S(2)}) collective-permute-start(bf16[24,1024]{1,0:T(8,128)(2,1)S(1)} %get-tuple-element.76), channel_id=1, source_target_pairs={{0,7},{1,4},{2,5},{3,6},{4,3},{5,0},{6,1},{7,2},{8,15},{9,12},{10,... | collective-permute-start | bytes 147464 | tf_op jit(solution)/shard_map/ppermute | solution.py:431
  117.6 0.3 collective-permute-start.13
  117.9 0.7 collective-permute-start.16
  118.6 0.5 collective-permute-start.12
  119.1 0.4 collective-permute-done.14.refs_4_
  119.6 1.0 collective-permute-start.11
  120.5 0.9 collective-permute-done.13.refs_3_
  121.4 1.9 %collective-permute-done.16.refs_6_ = bf16[24,1024]{1,0:T(8,128)(2,1)S(1)} collective-permute-done((bf16[24,1024]{1,0:T(8,128)(2,1)S(1)}, bf16[24,1024]{1,0:T(8,128)(2,1)S(1)}, u32[]{:S(2)}, u32[]{:S(2)}) %collective-permute-start.16) | collective-permute-done | bytes 49184 | tf_op jit(solution)/shard_map/ppermute | solution.py:431
  123.3 3.6 %all-to-all-done.3.recv_ref = bf16[32,8,640]{2,1,0:T(8,128)(2,1)S(1)} async-done(((bf16[32,8,640]{2,1,0:T(8,128)(2,1)}), bf16[32,8,640]{2,1,0:T(8,128)(2,1)S(1)}, u32[]{:S(2)}, u32[]{:S(2)}) %all-to-all-start.3) | async-done | bytes 327712 | tf_op jit(solution)/shard_map/all_to_all | solution.py:445
  126.9 2.8 %mid_x.3 = bf16[32,8,640]{2,1,0:T(8,128)(2,1)} custom-call(s32[1]{0:T(128)} %bitcast.1.core_ref, bf16[32,8,640]{2,1,0:T(8,128)(2,1)S(1)} %all-to-all-done.3.recv_ref, bf16[16,2,64,128]{3,2,1,0:T(8,128)(2,1)S(1)} %all-to-all-done.1.w0_ref, bf16[16,2,64,128]{3,2,1,0:T(8,128)(2,1)S(1)} %collective-permute-done.7.w1_ref, bf16[288,256]{1,0:T(8,128)(2,1)S(1)} %copy-done.5), custom_call_target="tpu_custom_call" | custom-call | flops 3000000000 | bytes 1048576 | tf_op jit(solution)/shard_map/mid_x/pallas_call | solution.py:233
  129.7 8.9 %all-to-all-start.4 = ((bf16[32,8,640]{2,1,0:T(8,128)(2,1)}), bf16[32,8,640]{2,1,0:T(8,128)(2,1)S(1)}, u32[]{:S(2)}, u32[]{:S(2)}) async-start(bf16[32,8,640]{2,1,0:T(8,128)(2,1)} %mid_x.3), calls=%async_computation.4 | async-start | bytes 655360 | tf_op jit(solution)/shard_map/all_to_all | solution.py:452
  138.6 1.6 mid_y.3
  140.1 0.2 collective-permute-start.18
  140.4 2.8 %collective-permute-start.19 = (bf16[24,1024]{1,0:T(8,128)(2,1)S(1)}, bf16[24,1024]{1,0:T(8,128)(2,1)S(1)}, u32[]{:S(2)}, u32[]{:S(2)}) collective-permute-start(bf16[24,1024]{1,0:T(8,128)(2,1)S(1)} %get-tuple-element.70), channel_id=1, source_target_pairs={{0,2},{1,3},{2,0},{3,1},{4,6},{5,7},{6,4},{7,5},{8,10},{9,11},{10,... | collective-permute-start | bytes 147464 | tf_op jit(solution)/shard_map/ppermute | solution.py:431
  143.2 0.6 collective-permute-start.20
  143.7 0.9 collective-permute-done.18.refs_4_
  144.7 1.2 collective-permute-done.19.refs_5_
  145.8 0.9 collective-permute-done.20.refs_6_
  146.7 6.3 %all-to-all-done.4 = bf16[32,8,640]{2,1,0:T(8,128)(2,1)S(1)} async-done(((bf16[32,8,640]{2,1,0:T(8,128)(2,1)}), bf16[32,8,640]{2,1,0:T(8,128)(2,1)S(1)}, u32[]{:S(2)}, u32[]{:S(2)}) %all-to-all-start.4) | async-done | bytes 327712 | tf_op jit(solution)/shard_map/all_to_all | solution.py:452
  153.0 1.6 copy-done.12
  154.6 11.8 %last.3 = bf16[64,64,256]{2,1,0:T(8,128)(2,1)} custom-call(s32[1]{0:T(128)} %bitcast.me_ref.refs_0_, bf16[256,640]{1,0:T(8,128)(2,1)S(1)} %bitcast.43, bf16[16,128]{1,0:T(8,128)(2,1)S(1)} %copy-done.8, bf16[24,1024]{1,0:T(8,128)(2,1)S(1)} %get-tuple-element.68.refs_3_, bf16[24,1024]{1,0:T(8,128)(2,1)S(1)} %collective-permute-done.18.refs_4_, ...), custom_call_target="tpu_custom_call" | custom-call | flops 12000000000 | bytes 1048576 | tf_op jit(solution)/shard_map/last/pallas_call | solution.py:406
  (31 shorter events, 0.1 us)
Async XLA Ops:
  6.5 16.2 %copy-start.8 = (bf16[16,128]{1,0:T(8,128)(2,1)S(1)}, bf16[16,128]{1,0:T(8,128)(2,1)}, u32[]{:S(2)}) copy-start(bf16[16,128]{1,0:T(8,128)(2,1)} %constant.40.clone.bx_ref.refs_2_) | copy-start | bytes 12292
  6.5 16.2 %copy-start.7 = (bf16[24,256]{1,0:T(8,128)(2,1)S(1)}, bf16[24,256]{1,0:T(8,128)(2,1)}, u32[]{:S(2)}) copy-start(bf16[24,256]{1,0:T(8,128)(2,1)} %constant.39.clone.cy_ref.refs_7_) | copy-start | bytes 36868
  6.5 16.2 %copy-start = (bf16[1,64,64,256]{3,2,1,0:T(8,128)(2,1)S(1)}, bf16[1,64,64,256]{3,2,1,0:T(8,128)(2,1)}, u32[]{:S(2)}) copy-start(bf16[1,64,64,256]{3,2,1,0:T(8,128)(2,1)} %param.9) | copy-start | bytes 6291460
  10.2 27.0 %all-to-all-start.1 = ((bf16[16,2,64,128]{3,2,1,0:T(8,128)(2,1)}), bf16[16,2,64,128]{3,2,1,0:T(8,128)(2,1)S(1)}, u32[]{:S(2)}, u32[]{:S(2)}) async-start(bf16[16,2,64,128]{3,2,1,0:T(8,128)(2,1)} %broadcast_in_dim.4), calls=%async_computation.1 | async-start | bytes 1048576 | tf_op jit(solution)/shard_map/all_to_all | solution.py:426
  22.0 53.3 %all-gather.3.cloned.1.call-start = ((), (), s32[]{:S(2)}) async-start(), calls=%async_computation.5 | async-start | bytes 1179648 | tf_op jit(solution)/shard_map/all_gather | solution.py:440
  22.8 37.2 %copy-start.5 = (bf16[288,256]{1,0:T(8,128)(2,1)S(1)}, bf16[288,256]{1,0:T(8,128)(2,1)}, u32[]{:S(2)}) copy-start(bf16[288,256]{1,0:T(8,128)(2,1)} %constant.37.clone.tab_ref) | copy-start | bytes 442372
  28.9 1.3 copy-start.9
  37.3 22.7 %all-to-all-start = ((bf16[32,8,640]{2,1,0:T(8,128)(2,1)}), bf16[32,8,640]{2,1,0:T(8,128)(2,1)S(1)}, u32[]{:S(2)}, u32[]{:S(2)}) async-start(bf16[32,8,640]{2,1,0:T(8,128)(2,1)} %bitcast.7), calls=%async_computation | async-start | bytes 655360 | tf_op jit(solution)/shard_map/all_to_all | solution.py:445
  44.8 15.2 %collective-permute-start.7 = (bf16[16,2,64,128]{3,2,1,0:T(8,128)(2,1)S(1)}, bf16[16,2,64,128]{3,2,1,0:T(8,128)(2,1)S(1)}, u32[]{:S(2)}, u32[]{:S(2)}) collective-permute-start(bf16[16,2,64,128]{3,2,1,0:T(8,128)(2,1)S(1)} %all-to-all-done.1.w0_ref), channel_id=1, source_target_pairs={{0,8},{8,0},{16,24},{24,16},{32,40},{40,32},{48,56},{56,48},{64,72... | collective-permute-start | bytes 1572872 | tf_op jit(solution)/shard_map/ppermute | solution.py:427
  45.1 7.0 %collective-permute-start.4 = (bf16[24,1024]{1,0:T(8,128)(2,1)S(1)}, bf16[24,1024]{1,0:T(8,128)(2,1)S(1)}, u32[]{:S(2)}, u32[]{:S(2)}) collective-permute-start(bf16[24,1024]{1,0:T(8,128)(2,1)S(1)} %get-tuple-element.79), channel_id=1, source_target_pairs={{0,2},{1,3},{2,0},{3,1},{4,6},{5,7},{6,4},{7,5},{8,10},{9,11},{10,... | collective-permute-start | bytes 147464 | tf_op jit(solution)/shard_map/ppermute | solution.py:431
  47.9 6.6 %collective-permute-start.3 = (bf16[24,1024]{1,0:T(8,128)(2,1)S(1)}, bf16[24,1024]{1,0:T(8,128)(2,1)S(1)}, u32[]{:S(2)}, u32[]{:S(2)}) collective-permute-start(bf16[24,1024]{1,0:T(8,128)(2,1)S(1)} %get-tuple-element.79), channel_id=1, source_target_pairs={{0,6},{1,7},{2,4},{3,5},{4,2},{5,3},{6,0},{7,1},{8,14},{9,15},{10,... | collective-permute-start | bytes 147464 | tf_op jit(solution)/shard_map/ppermute | solution.py:431
  48.3 6.4 %collective-permute-start.6 = (bf16[24,1024]{1,0:T(8,128)(2,1)S(1)}, bf16[24,1024]{1,0:T(8,128)(2,1)S(1)}, u32[]{:S(2)}, u32[]{:S(2)}) collective-permute-start(bf16[24,1024]{1,0:T(8,128)(2,1)S(1)} %get-tuple-element.80), channel_id=1, source_target_pairs={{0,7},{1,4},{2,5},{3,6},{4,3},{5,0},{6,1},{7,2},{8,15},{9,12},{10,... | collective-permute-start | bytes 147464 | tf_op jit(solution)/shard_map/ppermute | solution.py:431
  51.5 4.6 %collective-permute-start.2 = (bf16[24,1024]{1,0:T(8,128)(2,1)S(1)}, bf16[24,1024]{1,0:T(8,128)(2,1)S(1)}, u32[]{:S(2)}, u32[]{:S(2)}) collective-permute-start(bf16[24,1024]{1,0:T(8,128)(2,1)S(1)} %get-tuple-element.80), channel_id=1, source_target_pairs={{0,3},{1,0},{2,1},{3,2},{4,7},{5,4},{6,5},{7,6},{8,11},{9,8},{10,9... | collective-permute-start | bytes 147464 | tf_op jit(solution)/shard_map/ppermute | solution.py:431
  52.1 6.2 %collective-permute-start.5 = (bf16[24,1024]{1,0:T(8,128)(2,1)S(1)}, bf16[24,1024]{1,0:T(8,128)(2,1)S(1)}, u32[]{:S(2)}, u32[]{:S(2)}) collective-permute-start(bf16[24,1024]{1,0:T(8,128)(2,1)S(1)} %get-tuple-element.81), channel_id=1, source_target_pairs={{0,5},{1,6},{2,7},{3,4},{4,1},{5,2},{6,3},{7,0},{8,13},{9,14},{10,... | collective-permute-start | bytes 147464 | tf_op jit(solution)/shard_map/ppermute | solution.py:431
  54.6 4.6 %collective-permute-start.1 = (bf16[24,1024]{1,0:T(8,128)(2,1)S(1)}, bf16[24,1024]{1,0:T(8,128)(2,1)S(1)}, u32[]{:S(2)}, u32[]{:S(2)}) collective-permute-start(bf16[24,1024]{1,0:T(8,128)(2,1)S(1)} %get-tuple-element.81), channel_id=1, source_target_pairs={{0,1},{1,2},{2,3},{3,0},{4,5},{5,6},{6,7},{7,4},{8,9},{9,10},{10,1... | collective-permute-start | bytes 147464 | tf_op jit(solution)/shard_map/ppermute | solution.py:431
  54.6 5.0 %collective-permute-start = (bf16[24,1024]{1,0:T(8,128)(2,1)S(1)}, bf16[24,1024]{1,0:T(8,128)(2,1)S(1)}, u32[]{:S(2)}, u32[]{:S(2)}) collective-permute-start(bf16[24,1024]{1,0:T(8,128)(2,1)S(1)} %get-tuple-element.43.refs_0_), channel_id=1, source_target_pairs={{0,4},{1,5},{2,6},{3,7},{4,0},{5,1},{6,2},{7,3},{8,12},{9,13},{10,... | collective-permute-start | bytes 147464 | tf_op jit(solution)/shard_map/ppermute | solution.py:431
  60.0 15.3 %copy-start.6 = (bf16[2,8,24,128]{3,2,1,0:T(8,128)(2,1)S(1)}, bf16[2,8,24,128]{3,2,1,0:T(8,128)(2,1)}, u32[]{:S(2)}) copy-start(bf16[2,8,24,128]{3,2,1,0:T(8,128)(2,1)} %constant.38.clone.refs_9_) | copy-start | bytes 294916
  62.8 27.0 %all-to-all-start.2 = ((bf16[32,8,640]{2,1,0:T(8,128)(2,1)}), bf16[32,8,640]{2,1,0:T(8,128)(2,1)S(1)}, u32[]{:S(2)}, u32[]{:S(2)}) async-start(bf16[32,8,640]{2,1,0:T(8,128)(2,1)} %mid_x.2), calls=%async_computation.2 | async-start | bytes 655360 | tf_op jit(solution)/shard_map/all_to_all | solution.py:452
  75.3 1.2 copy-start.1
  76.6 13.2 %copy-start.3 = (bf16[2,64,256]{2,1,0:T(8,128)(2,1)S(1)}, bf16[2,64,256]{2,1,0:T(8,128)(2,1)}, u32[]{:S(2)}) copy-start(bf16[2,64,256]{2,1,0:T(8,128)(2,1)} %refs_9_.5) | copy-start | bytes 196612
  76.6 13.2 %copy-start.4 = (bf16[2,256,64]{1,2,0:T(8,128)(2,1)S(1)}, bf16[2,256,64]{1,2,0:T(8,128)(2,1)}, u32[]{:S(2)}) copy-start(bf16[2,256,64]{1,2,0:T(8,128)(2,1)} %param.13) | copy-start | bytes 196612
  78.1 4.5 %collective-permute-start.8 = (bf16[24,1024]{1,0:T(8,128)(2,1)S(1)}, bf16[24,1024]{1,0:T(8,128)(2,1)S(1)}, u32[]{:S(2)}, u32[]{:S(2)}) collective-permute-start(bf16[24,1024]{1,0:T(8,128)(2,1)S(1)} %get-tuple-element.53), channel_id=1, source_target_pairs={{0,1},{1,2},{2,3},{3,0},{4,5},{5,6},{6,7},{7,4},{8,9},{9,10},{10,1... | collective-permute-start | bytes 147464 | tf_op jit(solution)/shard_map/ppermute | solution.py:431
  78.2 6.1 %collective-permute-start.9 = (bf16[24,1024]{1,0:T(8,128)(2,1)S(1)}, bf16[24,1024]{1,0:T(8,128)(2,1)S(1)}, u32[]{:S(2)}, u32[]{:S(2)}) collective-permute-start(bf16[24,1024]{1,0:T(8,128)(2,1)S(1)} %get-tuple-element.54), channel_id=1, source_target_pairs={{0,2},{1,3},{2,0},{3,1},{4,6},{5,7},{6,4},{7,5},{8,10},{9,11},{10,... | collective-permute-start | bytes 147464 | tf_op jit(solution)/shard_map/ppermute | solution.py:431
  81.6 3.2 %collective-permute-start.10 = (bf16[24,1024]{1,0:T(8,128)(2,1)S(1)}, bf16[24,1024]{1,0:T(8,128)(2,1)S(1)}, u32[]{:S(2)}, u32[]{:S(2)}) collective-permute-start(bf16[24,1024]{1,0:T(8,128)(2,1)S(1)} %get-tuple-element.55), channel_id=1, source_target_pairs={{0,3},{1,0},{2,1},{3,2},{4,7},{5,4},{6,5},{7,6},{8,11},{9,8},{10,9... | collective-permute-start | bytes 147464 | tf_op jit(solution)/shard_map/ppermute | solution.py:431
  89.8 1.6 copy-start.10
  104.8 1.3 copy-start.11
  106.1 20.8 %all-to-all-start.3 = ((bf16[32,8,640]{2,1,0:T(8,128)(2,1)}), bf16[32,8,640]{2,1,0:T(8,128)(2,1)S(1)}, u32[]{:S(2)}, u32[]{:S(2)}) async-start(bf16[32,8,640]{2,1,0:T(8,128)(2,1)} %bitcast.20), calls=%async_computation.3 | async-start | bytes 655360 | tf_op jit(solution)/shard_map/all_to_all | solution.py:445
  112.4 6.2 %collective-permute-start.15 = (bf16[24,1024]{1,0:T(8,128)(2,1)S(1)}, bf16[24,1024]{1,0:T(8,128)(2,1)S(1)}, u32[]{:S(2)}, u32[]{:S(2)}) collective-permute-start(bf16[24,1024]{1,0:T(8,128)(2,1)S(1)} %get-tuple-element.75), channel_id=1, source_target_pairs={{0,2},{1,3},{2,0},{3,1},{4,6},{5,7},{6,4},{7,5},{8,10},{9,11},{10,... | collective-permute-start | bytes 147464 | tf_op jit(solution)/shard_map/ppermute | solution.py:431
  113.8 5.8 %collective-permute-start.14 = (bf16[24,1024]{1,0:T(8,128)(2,1)S(1)}, bf16[24,1024]{1,0:T(8,128)(2,1)S(1)}, u32[]{:S(2)}, u32[]{:S(2)}) collective-permute-start(bf16[24,1024]{1,0:T(8,128)(2,1)S(1)} %get-tuple-element.75), channel_id=1, source_target_pairs={{0,6},{1,7},{2,4},{3,5},{4,2},{5,3},{6,0},{7,1},{8,14},{9,15},{10,... | collective-permute-start | bytes 147464 | tf_op jit(solution)/shard_map/ppermute | solution.py:431
  114.7 5.8 %collective-permute-start.17 = (bf16[24,1024]{1,0:T(8,128)(2,1)S(1)}, bf16[24,1024]{1,0:T(8,128)(2,1)S(1)}, u32[]{:S(2)}, u32[]{:S(2)}) collective-permute-start(bf16[24,1024]{1,0:T(8,128)(2,1)S(1)} %get-tuple-element.76), channel_id=1, source_target_pairs={{0,7},{1,4},{2,5},{3,6},{4,3},{5,0},{6,1},{7,2},{8,15},{9,12},{10,... | collective-permute-start | bytes 147464 | tf_op jit(solution)/shard_map/ppermute | solution.py:431
  117.6 3.7 %collective-permute-start.13 = (bf16[24,1024]{1,0:T(8,128)(2,1)S(1)}, bf16[24,1024]{1,0:T(8,128)(2,1)S(1)}, u32[]{:S(2)}, u32[]{:S(2)}) collective-permute-start(bf16[24,1024]{1,0:T(8,128)(2,1)S(1)} %get-tuple-element.76), channel_id=1, source_target_pairs={{0,3},{1,0},{2,1},{3,2},{4,7},{5,4},{6,5},{7,6},{8,11},{9,8},{10,9... | collective-permute-start | bytes 147464 | tf_op jit(solution)/shard_map/ppermute | solution.py:431
  117.9 5.3 %collective-permute-start.16 = (bf16[24,1024]{1,0:T(8,128)(2,1)S(1)}, bf16[24,1024]{1,0:T(8,128)(2,1)S(1)}, u32[]{:S(2)}, u32[]{:S(2)}) collective-permute-start(bf16[24,1024]{1,0:T(8,128)(2,1)S(1)} %get-tuple-element.77), channel_id=1, source_target_pairs={{0,5},{1,6},{2,7},{3,4},{4,1},{5,2},{6,3},{7,0},{8,13},{9,14},{10,... | collective-permute-start | bytes 147464 | tf_op jit(solution)/shard_map/ppermute | solution.py:431
  118.6 4.7 %collective-permute-start.12 = (bf16[24,1024]{1,0:T(8,128)(2,1)S(1)}, bf16[24,1024]{1,0:T(8,128)(2,1)S(1)}, u32[]{:S(2)}, u32[]{:S(2)}) collective-permute-start(bf16[24,1024]{1,0:T(8,128)(2,1)S(1)} %get-tuple-element.77), channel_id=1, source_target_pairs={{0,1},{1,2},{2,3},{3,0},{4,5},{5,6},{6,7},{7,4},{8,9},{9,10},{10,1... | collective-permute-start | bytes 147464 | tf_op jit(solution)/shard_map/ppermute | solution.py:431
  119.5 19.0 %copy-start.2 = (bf16[16,4,64,128]{3,2,1,0:T(8,128)(2,1)S(1)}, bf16[16,4,64,128]{3,2,1,0:T(8,128)(2,1)}, u32[]{:S(2)}) copy-start(bf16[16,4,64,128]{3,2,1,0:T(8,128)(2,1)} %all-gather.3.cloned.1.call-done) | copy-start | bytes 3145732
  119.6 3.7 %collective-permute-start.11 = (bf16[24,1024]{1,0:T(8,128)(2,1)S(1)}, bf16[24,1024]{1,0:T(8,128)(2,1)S(1)}, u32[]{:S(2)}, u32[]{:S(2)}) collective-permute-start(bf16[24,1024]{1,0:T(8,128)(2,1)S(1)} %get-tuple-element.60.refs_0_), channel_id=1, source_target_pairs={{0,4},{1,5},{2,6},{3,7},{4,0},{5,1},{6,2},{7,3},{8,12},{9,13},{10,... | collective-permute-start | bytes 147464 | tf_op jit(solution)/shard_map/ppermute | solution.py:431
  129.7 23.3 %all-to-all-start.4 = ((bf16[32,8,640]{2,1,0:T(8,128)(2,1)}), bf16[32,8,640]{2,1,0:T(8,128)(2,1)S(1)}, u32[]{:S(2)}, u32[]{:S(2)}) async-start(bf16[32,8,640]{2,1,0:T(8,128)(2,1)} %mid_x.3), calls=%async_computation.4 | async-start | bytes 655360 | tf_op jit(solution)/shard_map/all_to_all | solution.py:452
  140.1 4.5 %collective-permute-start.18 = (bf16[24,1024]{1,0:T(8,128)(2,1)S(1)}, bf16[24,1024]{1,0:T(8,128)(2,1)S(1)}, u32[]{:S(2)}, u32[]{:S(2)}) collective-permute-start(bf16[24,1024]{1,0:T(8,128)(2,1)S(1)} %get-tuple-element.69), channel_id=1, source_target_pairs={{0,1},{1,2},{2,3},{3,0},{4,5},{5,6},{6,7},{7,4},{8,9},{9,10},{10,1... | collective-permute-start | bytes 147464 | tf_op jit(solution)/shard_map/ppermute | solution.py:431
  140.4 5.5 %collective-permute-start.19 = (bf16[24,1024]{1,0:T(8,128)(2,1)S(1)}, bf16[24,1024]{1,0:T(8,128)(2,1)S(1)}, u32[]{:S(2)}, u32[]{:S(2)}) collective-permute-start(bf16[24,1024]{1,0:T(8,128)(2,1)S(1)} %get-tuple-element.70), channel_id=1, source_target_pairs={{0,2},{1,3},{2,0},{3,1},{4,6},{5,7},{6,4},{7,5},{8,10},{9,11},{10,... | collective-permute-start | bytes 147464 | tf_op jit(solution)/shard_map/ppermute | solution.py:431
  143.2 3.6 %collective-permute-start.20 = (bf16[24,1024]{1,0:T(8,128)(2,1)S(1)}, bf16[24,1024]{1,0:T(8,128)(2,1)S(1)}, u32[]{:S(2)}, u32[]{:S(2)}) collective-permute-start(bf16[24,1024]{1,0:T(8,128)(2,1)S(1)} %get-tuple-element.71), channel_id=1, source_target_pairs={{0,3},{1,0},{2,1},{3,2},{4,7},{5,4},{6,5},{7,6},{8,11},{9,8},{10,9... | collective-permute-start | bytes 147464 | tf_op jit(solution)/shard_map/ppermute | solution.py:431
  153.0 1.6 copy-start.12
Sparse Core Ops, SparseCore 0:
  24.6 40.3 all-gather.2
where the time goes:
time: 174 us; the launch traced here: 173 us
  starting transfers between devices  71.2 us (41%)
  Pallas kernels  40.1 us (23%)
  waiting for transfers between devices  37.6 us (22%)
  between operations  13.6 us (8%)
  local copies, waits for them, and re-layouts  9.96 us (6%)
    pallas_call x2, Pallas kernels, last_call(): pl.pallas_call(functools.partial(last_kernel, more), name='last', grid=(6...  25.3 us
    ppermute x20, starting transfers between devices, permute_y(): return lax.ppermute(x, 'gy', [(i, moved(i, flip, step)) for i in range(8)])  24 us
    all_to_all x2, starting transfers between devices, body(): yx = lax.all_to_all(send, 'gx', 0, 0, tiled=True).reshape(256, RX * CH)  21.3 us
    ppermute x20, waiting for transfers between devices, permute_y(): return lax.ppermute(x, 'gy', [(i, moved(i, flip, step)) for i in range(8)])  14.7 us
    all_to_all x2, starting transfers between devices, body(): recv = lax.all_to_all(zx.reshape(32, LINE, RX * CH), 'gx', 0, 0, tiled=True)  13.8 us
    all_to_all x1, starting transfers between devices, exchange_weights(): lax.all_to_all(mine, 'gx', 0, 0, axis_index_groups=same_core, tiled=True)  11.7 us
    all_to_all x2, waiting for transfers between devices, body(): yx = lax.all_to_all(send, 'gx', 0, 0, tiled=True).reshape(256, RX * CH)  11.2 us
    unnamed x26, local copies, waits for them, and re-layouts  7.07 us
  transfers between devices with their start and end apart: 27, of which 20 were waited for; matrix products, arithmetic and copies ran while one was open for 0% of the time, Pallas kernels for 7%

commit v1 on v0

--- a/solution.py
+++ b/solution.py
@@ -187,7 +187,9 @@
     lax.fori_loop(0, steps, product, None, unroll=UNROLL)
 
 
-def mid_x_kernel(core_ref, recv_ref, w0_ref, w1_ref, tab_ref, *refs):
+def mid_x_kernel(
+    core_ref, layer_ref, recv_ref, near0_ref, near1_ref, far0_ref, far1_ref, tab_ref, *refs
+):
     send_ref, r_ref, xs_ref, ms_ref, o_ref = refs
     pairs = RX // 2
     first = half_mask(MODES)
@@ -205,7 +207,13 @@
         x = x + pltpu.roll(jnp.where(first, s[32:64], s[64:96]), 64, 1)
         xs_ref[pl.ds(y, MODES, stride=LINE), :] = x
     core = core_ref[0]
-    weights = lambda t: [(t * 2 + core, w0_ref[t, 0]), (t * 2 + 1 - core, w1_ref[t, 0])]
+    layer = layer_ref[0]
+
+    def weights(t):
+        mine = jnp.where(layer == 0, near0_ref[t].astype(F32), far0_ref[t].astype(F32))
+        swapped = jnp.where(layer == 0, near1_ref[t].astype(F32), far1_ref[t].astype(F32))
+        return [(t * 2 + core, mine), (t * 2 + 1 - core, swapped)]
+
     mix(xs_ref, ms_ref, LINE, 16, weights)
     cols = []
     for y in range(LINE):
@@ -228,14 +236,13 @@
     return pl.BlockSpec(a.shape, lambda *_: (0,) * a.ndim)
 
 
-def mid_x(layer, core, recv, w0, w1, c):
-    weights = pl.BlockSpec((16, 1, CH, 128), lambda i: (0, layer, 0, 0))
+def mid_x(core, layer, recv, w, c):
     return pl.pallas_call(
         mid_x_kernel,
         name="mid_x",
         grid=(1,),
-        in_specs=[pl.BlockSpec(memory_space=pltpu.SMEM)]
-        + [whole(recv), weights, weights, whole(c["mid_x"])],
+        in_specs=[pl.BlockSpec(memory_space=pltpu.SMEM)] * 2
+        + [whole(a) for a in (recv, *w, c["mid_x"])],
         out_specs=whole(recv),
         out_shape=jax.ShapeDtypeStruct(recv.shape, BF16),
         scratch_shapes=[
@@ -246,21 +253,22 @@
         ],
         compiler_params=params(16),
         cost_estimate=estimate(3),
-    )(core, recv, w0, w1, c["mid_x"])
+    )(core, layer, recv, *w, c["mid_x"])
 
 
 def mid_y_kernel(me_ref, *refs):
-    z_refs = refs[:8]
-    w_ref, tab_ref = refs[8:10]
-    out_refs = refs[10:14]
-    xs_ref, ms_ref = refs[14:]
+    z_refs, w_refs = refs[:8], refs[8:16]
+    tab_ref = refs[16]
+    out_refs = refs[17:21]
+    xs_ref, ms_ref, w_ref = refs[21:]
     first = half_mask(MODES)
     lines = 16
     half, quarter = me_ref[0] // 4, lax.rem(me_ref[0], 4)
-    table = []
+    sources = []
     for flip, step in ((0, 0),) + SHIFTS:
         near = half + flip - 2 * flip * half
-        table.append(tab_ref[0, near * 4 + lax.rem(quarter + 4 - step, 4)].astype(F32))
+        sources.append(near * 4 + lax.rem(quarter + 4 - step, 4))
+    table = [tab_ref[0, src].astype(F32) for src in sources]
     forward = jnp.concatenate(table, axis=0).T[:64].astype(BF16)
     table = [tab_ref[1, half * 4 + lax.rem(quarter + step, 4)].astype(F32) for step in range(4)]
     inverse = jnp.concatenate(table, axis=0)[:, :64].astype(BF16)
@@ -278,7 +286,9 @@
             xs_ref[pl.ds(line + 1, MODES, stride=lines), :] = jnp.where(
                 first, pltpu.roll(re, 64, 1), im
             )
-    weights = lambda src: [(src * 4 + j, w_ref[src, 0, j]) for j in range(4)]
+    for slot, src in enumerate(sources):
+        w_ref[src] = w_refs[slot][0]
+    weights = lambda src: [(src * 4 + j, w_ref[src, j]) for j in range(4)]
     mix(xs_ref, ms_ref, lines, 8, weights)
     for g in range(2):
         cols = []
@@ -295,25 +305,21 @@
 
 
 def mid_y(layer, me, zs, w, c):
-    table = c["mid_y"]
     return pl.pallas_call(
         mid_y_kernel,
         name="mid_y",
-        grid_spec=pltpu.PrefetchScalarGridSpec(
-            num_scalar_prefetch=1,
-            grid=(1,),
-            in_specs=[whole(z) for z in zs]
-            + [
-                pl.BlockSpec((8, 1, 4, CH, 128), lambda i, me: (0, layer, 0, 0, 0)),
-                whole(table),
-            ],
-            out_specs=[pl.BlockSpec((RYP, QUARTER), lambda i, me: (0, 0))] * 4,
-            scratch_shapes=[pltpu.VMEM((MODES * 16, 128), F32)] * 2,
-        ),
+        grid=(1,),
+        in_specs=[pl.BlockSpec(memory_space=pltpu.SMEM)]
+        + [whole(z) for z in zs]
+        + [pl.BlockSpec((1, 4, CH, 128), lambda i: (layer, 0, 0, 0))] * 8
+        + [whole(c["mid_y"])],
+        out_specs=[pl.BlockSpec((RYP, QUARTER), lambda i: (0, 0))] * 4,
+        scratch_shapes=[pltpu.VMEM((MODES * 16, 128), F32)] * 2
+        + [pltpu.VMEM((8, 4, CH, 128), BF16)],
         out_shape=[jax.ShapeDtypeStruct((RYP, QUARTER), BF16)] * 4,
         compiler_params=params(20),
         cost_estimate=estimate(2),
-    )(me, *zs, w, table)
+    )(me, *zs, *w, c["mid_y"])
 
 
 def gelu(x):
@@ -416,15 +422,36 @@
     )(me, yx, c["bx"], *yy, c["cy"], state, we, wr)
 
 
-def join(w):
-    return jnp.concatenate([w[..., 0, :, :], w[..., 1, :, :]], axis=-1)
-
-
-def exchange_weights(own):
-    same_core = [list(range(s, 32, 2)) for s in range(2)]
-    mine = jnp.broadcast_to(own[None], (16, LAYERS, CH, 128))
-    mine = lax.all_to_all(mine, "gx", 0, 0, axis_index_groups=same_core, tiled=True)
-    return mine, lax.ppermute(mine, "gx", [(i, i ^ 1) for i in range(32)])
+def pack_kernel(half_ref, wx_ref, wy_ref, x_ref, y_ref):
+    def join(parts):
+        return jnp.concatenate([part.astype(F32) for part in parts], axis=1)
+
+    for layer in range(LAYERS):
+        for j in range(4):
+            y_ref[layer, j] = join([wy_ref[layer, j, i] for i in range(2)]).astype(BF16)
+    own = [join([wx_ref[layer, 0, i] for i in range(2)]) for layer in range(LAYERS)]
+    mode = jnp.where(half_ref[0] == 0, own[0], own[1]).astype(BF16)
+    for i in range(16):
+        x_ref[i] = mode
+
+
+def pack_call(half, spectral_x, spectral_y):
+    shapes = (16, CH, 128), (LAYERS, 4, CH, 128)
+    out_shape = [jax.ShapeDtypeStruct(shape, BF16) for shape in shapes]
+    return pl.pallas_call(
+        pack_kernel,
+        name="pack",
+        grid=(1,),
+        in_specs=[pl.BlockSpec(memory_space=pltpu.SMEM), whole(spectral_x), whole(spectral_y)],
+        out_specs=[whole(a) for a in out_shape],
+        out_shape=out_shape,
+        compiler_params=params(16),
+        cost_estimate=estimate(2),
+    )(half, spectral_x, spectral_y)
+
+
+def swap_cores(x):
+    return lax.ppermute(x, "gx", [(i, i ^ 1) for i in range(32)])
 
 
 def permute_y(x, flip, step):
@@ -435,20 +462,26 @@
     c = {name: jnp.asarray(value) for name, value in make_constants().items()}
     core = lax.rem(lax.axis_index("gx"), 2).reshape(1).astype(jnp.int32)
     me = lax.axis_index("gy").reshape(1).astype(jnp.int32)
-    own_x, own_y = join(spectral_x)[:, 0], join(spectral_y)
-    own_x, own_y = lax.optimization_barrier((own_x, own_y))
-    wy = lax.all_gather(own_y, "gy", axis=0)
-    wx = exchange_weights(own_x)
+    half = me // 4
+    own_x, own_y = pack_call(half, spectral_x, spectral_y)
+    same_core = [list(range(s, 32, 2)) for s in range(2)]
+    mine = lax.all_to_all(own_x, "gx", 0, 0, axis_index_groups=same_core, tiled=True)
+    wy = [own_y] + [permute_y(own_y, flip, step) for flip, step in SHIFTS]
     wr = jnp.swapaxes(reduce_weight, 1, 2)
     state, zx, zy = first_call(state_field[0], c)
+    state = pltpu.with_memory_space_constraint(state, pltpu.HBM)
+    zx, wy = lax.optimization_barrier((zx, wy))
     for l in range(LAYERS):
         recv = lax.all_to_all(zx.reshape(32, LINE, RX * CH), "gx", 0, 0, tiled=True)
         zs = []
         for flip, step in ((0, 0),) + SHIFTS:
             chunk = lax.dynamic_slice_in_dim(zy, lax.rem(me[0] + step, 4), 1, 0)[0]
             zs.append(permute_y(chunk, flip, step) if flip or step else chunk)
+        if l == 0:
+            other = permute_y(mine, 1, 0)
+            wx = [mine, swap_cores(mine), other, swap_cores(other)]
         zs, recv = lax.optimization_barrier((zs, recv))
-        send = mid_x(l, core, recv, wx[0], wx[1], c)
+        send = mid_x(core, lax.rem(half + l, 2), recv, wx, c)
         yx = lax.all_to_all(send, "gx", 0, 0, tiled=True).reshape(256, RX * CH)
         yy = mid_y(l, me, zs, wy, c)
         yy = [yy[0]] + [permute_y(yy[step], 0, step) for step in range(1, 4)]
@@ -456,6 +489,7 @@
         got = last_call(l, more, me, yx, yy, state, expand_weight, wr, c)
         if more:
             state, zx, zy = got
+            state = pltpu.with_memory_space_constraint(state, pltpu.HBM)
     return got[0][None]
 
 

time: 174 us -> 179 us (1.029)
  starting transfers between devices: 71.2 us -> 92 us
  between operations: 13.6 us -> 0.25 us
  local copies, waits for them, and re-layouts: 9.96 us -> 7.4 us
  Pallas kernels: 40.1 us -> 42.6 us
    ppermute x20 -> x28, starting transfers between devices: 24 us -> 38.8 us  [permute_y(): return lax.ppermute(x, 'gy', [(i, moved(i, flip, step)) for i in range(8)])]
    all_to_all x1, waiting for transfers between devices: 7.06 us -> 0.01 us  [body(): lax.all_to_all(own_x, 'gx', 0, 0, axis_index_groups=same_core, tiled=True)]
    ppermute x20 -> x28, waiting for transfers between devices: 14.7 us -> 21.5 us  [permute_y(): return lax.ppermute(x, 'gy', [(i, moved(i, flip, step)) for i in range(8)])]
    all_to_all x2, starting transfers between devices: 13.8 us -> 18.1 us  [body(): recv = lax.all_to_all(zx.reshape(32, LINE, RX * CH), 'gx', 0, 0, tiled=True)]
    squeeze x2 -> x0, local copies, waits for them, and re-layouts: 1.92 us -> none  [join(): return jnp.concatenate([w[..., 0, :, :], w[..., 1, :, :]], axis=-1)]
    all_to_all x2, waiting for transfers between devices: 3.98 us -> 2.16 us  [body(): recv = lax.all_to_all(zx.reshape(32, LINE, RX * CH), 'gx', 0, 0, tiled=True)]
    pallas_call x2 -> x3, Pallas kernels: 3.11 us -> 4.01 us  [the longest x2 3.17 us: mid_y(): pl.pallas_call(mid_y_kernel, name='mid_y', grid=(1,), in_specs=[pl.BlockS...]
    unnamed x26 -> x36, local copies, waits for them, and re-layouts: 7.07 us -> 7.36 us
  transfers between devices with their start and end apart: 27 -> 35, of which waited for: 20 -> 16; matrix products, arithmetic and copies ran while one was open for 0% -> 0% of each run, Pallas kernels for 7% -> 5%
where the time goes in v1:
time: 179 us; the launch traced here: 178 us
  starting transfers between devices  92 us (51%)
  Pallas kernels  42.6 us (24%)
  waiting for transfers between devices  36.2 us (20%)
  local copies, waits for them, and re-layouts  7.4 us (4%)
    ppermute x28, starting transfers between devices, permute_y(): return lax.ppermute(x, 'gy', [(i, moved(i, flip, step)) for i in range(8)])  38.8 us
    pallas_call x2, Pallas kernels, last_call(): pl.pallas_call(functools.partial(last_kernel, more), name='last', grid=(6...  27 us
    all_to_all x2, starting transfers between devices, body(): yx = lax.all_to_all(send, 'gx', 0, 0, tiled=True).reshape(256, RX * CH)  23 us
    ppermute x28, waiting for transfers between devices, permute_y(): return lax.ppermute(x, 'gy', [(i, moved(i, flip, step)) for i in range(8)])  21.5 us
    all_to_all x2, starting transfers between devices, body(): recv = lax.all_to_all(zx.reshape(32, LINE, RX * CH), 'gx', 0, 0, tiled=True)  18.1 us
    all_to_all x2, waiting for transfers between devices, body(): yx = lax.all_to_all(send, 'gx', 0, 0, tiled=True).reshape(256, RX * CH)  12.5 us
    all_to_all x1, starting transfers between devices, body(): lax.all_to_all(own_x, 'gx', 0, 0, axis_index_groups=same_core, tiled=True)  10.6 us
    unnamed x36, local copies, waits for them, and re-layouts  7.36 us
  transfers between devices with their start and end apart: 35, of which 16 were waited for; matrix products, arithmetic and copies ran while one was open for 0% of the time, Pallas kernels for 5%

profile of v1, /device:TPU:1, one launch (start us, length us, event | category | flops | bytes accessed | tf_op | source)
XLA Modules:
  0.0 178.5 jit_solution(3907551369999861024)
XLA Ops:
  0.0 0.9 copy-done.1
  1.0 0.8 copy-done.8
  1.8 0.8 pack.1
  2.6 4.3 %collective-permute-start.13 = (bf16[2,4,64,128]{3,2,1,0:T(8,128)(2,1)S(1)}, bf16[2,4,64,128]{3,2,1,0:T(8,128)(2,1)S(1)}, u32[]{:S(2)}, u32[]{:S(2)}) collective-permute-start(bf16[2,4,64,128]{3,2,1,0:T(8,128)(2,1)S(1)} %get-tuple-element.62.refs_8_), channel_id=1, source_target_pairs={{0,7},{1,4},{2,5},{3,6},{4,3},{5,0},{6,1},{7,2},{8,15},{9,12},{10,... | collective-permute-start | bytes 393224 | tf_op jit(solution)/shard_map/ppermute | solution.py:458
  7.0 1.6 collective-permute-start.11
  8.6 1.2 collective-permute-start.10
  9.8 3.7 %collective-permute-start.9 = (bf16[2,4,64,128]{3,2,1,0:T(8,128)(2,1)S(1)}, bf16[2,4,64,128]{3,2,1,0:T(8,128)(2,1)S(1)}, u32[]{:S(2)}, u32[]{:S(2)}) collective-permute-start(bf16[2,4,64,128]{3,2,1,0:T(8,128)(2,1)S(1)} %get-tuple-element.62.refs_8_), channel_id=1, source_target_pairs={{0,3},{1,0},{2,1},{3,2},{4,7},{5,4},{6,5},{7,6},{8,11},{9,8},{10,9... | collective-permute-start | bytes 393224 | tf_op jit(solution)/shard_map/ppermute | solution.py:458
  13.5 10.6 %all-to-all-start.1 = ((bf16[16,64,128]{2,1,0:T(8,128)(2,1)}), bf16[16,64,128]{2,1,0:T(8,128)(2,1)S(1)}, u32[]{:S(2)}, u32[]{:S(2)}) async-start(bf16[16,64,128]{2,1,0:T(8,128)(2,1)} %get-tuple-element.53), calls=%async_computation.1 | async-start | bytes 524288 | tf_op jit(solution)/shard_map/all_to_all | solution.py:468
  24.2 0.1 collective-permute-start.8
  24.3 0.1 collective-permute-start.7
  24.4 6.1 %first.1 = (bf16[256,4096]{1,0:T(8,128)(2,1)S(1)}, bf16[256,640]{1,0:T(8,128)(2,1)}, bf16[4,24,1024]{2,1,0:T(8,128)(2,1)S(1)}) custom-call(bf16[64,64,256]{2,1,0:T(8,128)(2,1)S(1)} %bitcast.27, bf16[16,128]{1,0:T(8,128)(2,1)S(1)} %copy-done.15, bf16[24,256]{1,0:T(8,128)(2,1)S(1)} %copy-done.14), custom_call_target="tpu_custom_call" | custom-call | flops 10000000000 | bytes 1048576 | tf_op jit(solution)/shard_map/first/pallas_call | solution.py:145
  30.5 1.3 copy-done.16
  31.8 0.7 copy-done.2
  32.5 0.6 copy-done.4
  33.1 0.7 copy-done.6
  33.8 12.7 %all-to-all-start = ((bf16[32,8,640]{2,1,0:T(8,128)(2,1)}), bf16[32,8,640]{2,1,0:T(8,128)(2,1)S(1)}, u32[]{:S(2)}, u32[]{:S(2)}) async-start(bf16[32,8,640]{2,1,0:T(8,128)(2,1)} %bitcast.7), calls=%async_computation | async-start | bytes 655360 | tf_op jit(solution)/shard_map/all_to_all | solution.py:475
  46.5 0.5 collective-permute-start.15
  47.0 0.5 collective-permute-start.14
  47.5 9.7 %collective-permute-done.15.far0_ref = bf16[16,64,128]{2,1,0:T(8,128)(2,1)S(1)} collective-permute-done((bf16[16,64,128]{2,1,0:T(8,128)(2,1)S(1)}, bf16[16,64,128]{2,1,0:T(8,128)(2,1)S(1)}, u32[]{:S(2)}, u32[]{:S(2)}) %collective-permute-start.15) | collective-permute-done | bytes 262176 | tf_op jit(solution)/shard_map/ppermute | solution.py:458
  57.2 1.0 collective-permute-start.16
  58.2 1.2 collective-permute-start.4
  59.4 2.2 %collective-permute-start.3 = (bf16[24,1024]{1,0:T(8,128)(2,1)S(1)}, bf16[24,1024]{1,0:T(8,128)(2,1)S(1)}, u32[]{:S(2)}, u32[]{:S(2)}) collective-permute-start(bf16[24,1024]{1,0:T(8,128)(2,1)S(1)} %get-tuple-element.95), channel_id=1, source_target_pairs={{0,6},{1,7},{2,4},{3,5},{4,2},{5,3},{6,0},{7,1},{8,14},{9,15},{10,... | collective-permute-start | bytes 147464 | tf_op jit(solution)/shard_map/ppermute | solution.py:458
  61.6 3.4 %collective-permute-start.6 = (bf16[24,1024]{1,0:T(8,128)(2,1)S(1)}, bf16[24,1024]{1,0:T(8,128)(2,1)S(1)}, u32[]{:S(2)}, u32[]{:S(2)}) collective-permute-start(bf16[24,1024]{1,0:T(8,128)(2,1)S(1)} %get-tuple-element.96), channel_id=1, source_target_pairs={{0,7},{1,4},{2,5},{3,6},{4,3},{5,0},{6,1},{7,2},{8,15},{9,12},{10,... | collective-permute-start | bytes 147464 | tf_op jit(solution)/shard_map/ppermute | solution.py:458
  65.0 1.0 collective-permute-start.2
  66.0 1.5 collective-permute-start.5
  67.5 0.5 collective-permute-done.2.refs_3_
  67.9 0.6 collective-permute-start
  68.5 2.6 %collective-permute-done.5.refs_6_ = bf16[24,1024]{1,0:T(8,128)(2,1)S(1)} collective-permute-done((bf16[24,1024]{1,0:T(8,128)(2,1)S(1)}, bf16[24,1024]{1,0:T(8,128)(2,1)S(1)}, u32[]{:S(2)}, u32[]{:S(2)}) %collective-permute-start.5) | collective-permute-done | bytes 49184 | tf_op jit(solution)/shard_map/ppermute | solution.py:458
  71.2 0.5 collective-permute-done.1.refs_2_
  71.7 0.9 copy-done.11
  72.6 2.8 %mid_x.2 = bf16[32,8,640]{2,1,0:T(8,128)(2,1)} custom-call(s32[1]{0:T(128)} %bitcast.1.core_ref, s32[1]{0:T(128)S(6)} %rem.142.layer_ref, bf16[32,8,640]{2,1,0:T(8,128)(2,1)S(1)} %all-to-all-done.recv_ref, bf16[16,64,128]{2,1,0:T(8,128)(2,1)S(1)} %all-to-all-done.1.near0_ref, bf16[16,64,128]{2,1,0:T(8,128)(2,1)S(1)} %collective-permute-done.14.near1_ref, ...), custom_call_target="tpu_custom_call" | custom-call | flops 3000000000 | bytes 1048576 | tf_op jit(solution)/shard_map/mid_x/pallas_call | solution.py:240
  75.3 12.7 %all-to-all-start.2 = ((bf16[32,8,640]{2,1,0:T(8,128)(2,1)}), bf16[32,8,640]{2,1,0:T(8,128)(2,1)S(1)}, u32[]{:S(2)}, u32[]{:S(2)}) async-start(bf16[32,8,640]{2,1,0:T(8,128)(2,1)} %mid_x.2), calls=%async_computation.2 | async-start | bytes 655360 | tf_op jit(solution)/shard_map/all_to_all | solution.py:485
  88.1 1.6 mid_y.2
  89.7 0.1 collective-permute-start.17
  89.8 3.1 %collective-permute-start.18 = (bf16[24,1024]{1,0:T(8,128)(2,1)S(1)}, bf16[24,1024]{1,0:T(8,128)(2,1)S(1)}, u32[]{:S(2)}, u32[]{:S(2)}) collective-permute-start(bf16[24,1024]{1,0:T(8,128)(2,1)S(1)} %get-tuple-element.72), channel_id=1, source_target_pairs={{0,2},{1,3},{2,0},{3,1},{4,6},{5,7},{6,4},{7,5},{8,10},{9,11},{10,... | collective-permute-start | bytes 147464 | tf_op jit(solution)/shard_map/ppermute | solution.py:458
  92.9 1.7 collective-permute-start.19
  94.5 1.0 collective-permute-done.18.refs_5_
  95.6 0.8 collective-permute-done.19.refs_6_
  96.3 6.2 %all-to-all-done.2 = bf16[32,8,640]{2,1,0:T(8,128)(2,1)S(1)} async-done(((bf16[32,8,640]{2,1,0:T(8,128)(2,1)}), bf16[32,8,640]{2,1,0:T(8,128)(2,1)S(1)}, u32[]{:S(2)}, u32[]{:S(2)}) %all-to-all-start.2) | async-done | bytes 327712 | tf_op jit(solution)/shard_map/all_to_all | solution.py:485
  102.5 14.3 %last.2 = (bf16[256,4096]{1,0:T(8,128)(2,1)S(1)}, bf16[256,640]{1,0:T(8,128)(2,1)}, bf16[4,24,1024]{2,1,0:T(8,128)(2,1)S(1)}) custom-call(s32[1]{0:T(128)} %bitcast.me_ref.refs_0_, bf16[256,640]{1,0:T(8,128)(2,1)S(1)} %bitcast.26, bf16[16,128]{1,0:T(8,128)(2,1)S(1)} %copy-done.15, bf16[24,1024]{1,0:T(8,128)(2,1)S(1)} %get-tuple-element.70.refs_3_, ...), custom_call_target="tpu_custom_call" | custom-call | flops 12000000000 | bytes 1048576 | tf_op jit(solution)/shard_map/last/pallas_call | solution.py:412
  116.9 1.3 copy-done.17
  118.2 5.3 %all-to-all-start.3 = ((bf16[32,8,640]{2,1,0:T(8,128)(2,1)}), bf16[32,8,640]{2,1,0:T(8,128)(2,1)S(1)}, u32[]{:S(2)}, u32[]{:S(2)}) async-start(bf16[32,8,640]{2,1,0:T(8,128)(2,1)} %bitcast.14), calls=%async_computation.3 | async-start | bytes 655360 | tf_op jit(solution)/shard_map/all_to_all | solution.py:475
  123.6 2.8 %collective-permute-start.24 = (bf16[24,1024]{1,0:T(8,128)(2,1)S(1)}, bf16[24,1024]{1,0:T(8,128)(2,1)S(1)}, u32[]{:S(2)}, u32[]{:S(2)}) collective-permute-start(bf16[24,1024]{1,0:T(8,128)(2,1)S(1)} %get-tuple-element.91), channel_id=1, source_target_pairs={{0,2},{1,3},{2,0},{3,1},{4,6},{5,7},{6,4},{7,5},{8,10},{9,11},{10,... | collective-permute-start | bytes 147464 | tf_op jit(solution)/shard_map/ppermute | solution.py:458
  126.4 0.5 collective-permute-start.23
  126.9 3.1 %collective-permute-start.26 = (bf16[24,1024]{1,0:T(8,128)(2,1)S(1)}, bf16[24,1024]{1,0:T(8,128)(2,1)S(1)}, u32[]{:S(2)}, u32[]{:S(2)}) collective-permute-start(bf16[24,1024]{1,0:T(8,128)(2,1)S(1)} %get-tuple-element.92), channel_id=1, source_target_pairs={{0,7},{1,4},{2,5},{3,6},{4,3},{5,0},{6,1},{7,2},{8,15},{9,12},{10,... | collective-permute-start | bytes 147464 | tf_op jit(solution)/shard_map/ppermute | solution.py:458
  129.9 0.6 collective-permute-start.22
  130.5 0.9 collective-permute-start.25
  131.4 0.8 collective-permute-done.23.refs_4_
  132.2 0.4 collective-permute-start.20
  132.7 0.5 collective-permute-done.22.refs_3_
  133.2 2.7 %collective-permute-done.25.refs_6_ = bf16[24,1024]{1,0:T(8,128)(2,1)S(1)} collective-permute-done((bf16[24,1024]{1,0:T(8,128)(2,1)S(1)}, bf16[24,1024]{1,0:T(8,128)(2,1)S(1)}, u32[]{:S(2)}, u32[]{:S(2)}) %collective-permute-start.25) | collective-permute-done | bytes 49184 | tf_op jit(solution)/shard_map/ppermute | solution.py:458
  135.9 0.2 collective-permute-done.20.refs_1_
  136.1 2.2 %all-to-all-done.3.recv_ref = bf16[32,8,640]{2,1,0:T(8,128)(2,1)S(1)} async-done(((bf16[32,8,640]{2,1,0:T(8,128)(2,1)}), bf16[32,8,640]{2,1,0:T(8,128)(2,1)S(1)}, u32[]{:S(2)}, u32[]{:S(2)}) %all-to-all-start.3) | async-done | bytes 327712 | tf_op jit(solution)/shard_map/all_to_all | solution.py:475
  138.2 2.8 %mid_x.3 = bf16[32,8,640]{2,1,0:T(8,128)(2,1)} custom-call(s32[1]{0:T(128)} %bitcast.1.core_ref, s32[1]{0:T(128)S(6)} %rem.136.layer_ref, bf16[32,8,640]{2,1,0:T(8,128)(2,1)S(1)} %all-to-all-done.3.recv_ref, bf16[16,64,128]{2,1,0:T(8,128)(2,1)S(1)} %all-to-all-done.1.near0_ref, bf16[16,64,128]{2,1,0:T(8,128)(2,1)S(1)} %collective-permute-done.14.near1_ref, ...), custom_call_target="tpu_custom_call" | custom-call | flops 3000000000 | bytes 1048576 | tf_op jit(solution)/shard_map/mid_x/pallas_call | solution.py:240
  141.0 10.3 %all-to-all-start.4 = ((bf16[32,8,640]{2,1,0:T(8,128)(2,1)}), bf16[32,8,640]{2,1,0:T(8,128)(2,1)S(1)}, u32[]{:S(2)}, u32[]{:S(2)}) async-start(bf16[32,8,640]{2,1,0:T(8,128)(2,1)} %mid_x.3), calls=%async_computation.4 | async-start | bytes 655360 | tf_op jit(solution)/shard_map/all_to_all | solution.py:485
  151.3 1.6 mid_y.3
  152.9 0.1 collective-permute-start.27
  153.0 2.9 %collective-permute-start.28 = (bf16[24,1024]{1,0:T(8,128)(2,1)S(1)}, bf16[24,1024]{1,0:T(8,128)(2,1)S(1)}, u32[]{:S(2)}, u32[]{:S(2)}) collective-permute-start(bf16[24,1024]{1,0:T(8,128)(2,1)S(1)} %get-tuple-element.88), channel_id=1, source_target_pairs={{0,2},{1,3},{2,0},{3,1},{4,6},{5,7},{6,4},{7,5},{8,10},{9,11},{10,... | collective-permute-start | bytes 147464 | tf_op jit(solution)/shard_map/ppermute | solution.py:458
  155.9 1.3 collective-permute-start.29
  157.2 0.2 collective-permute-done.27.refs_4_
  157.4 1.2 collective-permute-done.28.refs_5_
  158.6 0.9 collective-permute-done.29.refs_6_
  159.5 6.3 %all-to-all-done.4 = bf16[32,8,640]{2,1,0:T(8,128)(2,1)S(1)} async-done(((bf16[32,8,640]{2,1,0:T(8,128)(2,1)}), bf16[32,8,640]{2,1,0:T(8,128)(2,1)S(1)}, u32[]{:S(2)}, u32[]{:S(2)}) %all-to-all-start.4) | async-done | bytes 327712 | tf_op jit(solution)/shard_map/all_to_all | solution.py:485
  165.8 12.7 %last.3 = bf16[64,64,256]{2,1,0:T(8,128)(2,1)} custom-call(s32[1]{0:T(128)} %bitcast.me_ref.refs_0_, bf16[256,640]{1,0:T(8,128)(2,1)S(1)} %bitcast.25, bf16[16,128]{1,0:T(8,128)(2,1)S(1)} %copy-done.15, bf16[24,1024]{1,0:T(8,128)(2,1)S(1)} %get-tuple-element.86.refs_3_, bf16[24,1024]{1,0:T(8,128)(2,1)S(1)} %collective-permute-done.27.refs_4_, ...), custom_call_target="tpu_custom_call" | custom-call | flops 12000000000 | bytes 1048576 | tf_op jit(solution)/shard_map/last/pallas_call | solution.py:412
  (52 shorter events, 0.2 us)
Async XLA Ops:
  0.0 0.9 copy-start.1
  1.0 0.8 copy-start.8
  1.8 22.6 %copy-start = (bf16[1,64,64,256]{3,2,1,0:T(8,128)(2,1)S(1)}, bf16[1,64,64,256]{3,2,1,0:T(8,128)(2,1)}, u32[]{:S(2)}) copy-start(bf16[1,64,64,256]{3,2,1,0:T(8,128)(2,1)} %param.9) | copy-start | bytes 6291460
  1.8 22.6 %copy-start.14 = (bf16[24,256]{1,0:T(8,128)(2,1)S(1)}, bf16[24,256]{1,0:T(8,128)(2,1)}, u32[]{:S(2)}) copy-start(bf16[24,256]{1,0:T(8,128)(2,1)} %constant.70.clone.cy_ref.refs_7_) | copy-start | bytes 36868
  1.8 22.6 %copy-start.15 = (bf16[16,128]{1,0:T(8,128)(2,1)S(1)}, bf16[16,128]{1,0:T(8,128)(2,1)}, u32[]{:S(2)}) copy-start(bf16[16,128]{1,0:T(8,128)(2,1)} %constant.71.clone.bx_ref.refs_2_) | copy-start | bytes 12292
  2.6 21.5 %collective-permute-start.13 = (bf16[2,4,64,128]{3,2,1,0:T(8,128)(2,1)S(1)}, bf16[2,4,64,128]{3,2,1,0:T(8,128)(2,1)S(1)}, u32[]{:S(2)}, u32[]{:S(2)}) collective-permute-start(bf16[2,4,64,128]{3,2,1,0:T(8,128)(2,1)S(1)} %get-tuple-element.62.refs_8_), channel_id=1, source_target_pairs={{0,7},{1,4},{2,5},{3,6},{4,3},{5,0},{6,1},{7,2},{8,15},{9,12},{10,... | collective-permute-start | bytes 393224 | tf_op jit(solution)/shard_map/ppermute | solution.py:458
  7.0 17.3 %collective-permute-start.12 = (bf16[2,4,64,128]{3,2,1,0:T(8,128)(2,1)S(1)}, bf16[2,4,64,128]{3,2,1,0:T(8,128)(2,1)S(1)}, u32[]{:S(2)}, u32[]{:S(2)}) collective-permute-start(bf16[2,4,64,128]{3,2,1,0:T(8,128)(2,1)S(1)} %get-tuple-element.62.refs_8_), channel_id=1, source_target_pairs={{0,5},{1,6},{2,7},{3,4},{4,1},{5,2},{6,3},{7,0},{8,13},{9,14},{10,... | collective-permute-start | bytes 393224 | tf_op jit(solution)/shard_map/ppermute | solution.py:458
  7.0 24.8 %collective-permute-start.11 = (bf16[2,4,64,128]{3,2,1,0:T(8,128)(2,1)S(1)}, bf16[2,4,64,128]{3,2,1,0:T(8,128)(2,1)S(1)}, u32[]{:S(2)}, u32[]{:S(2)}) collective-permute-start(bf16[2,4,64,128]{3,2,1,0:T(8,128)(2,1)S(1)} %get-tuple-element.62.refs_8_), channel_id=1, source_target_pairs={{0,2},{1,3},{2,0},{3,1},{4,6},{5,7},{6,4},{7,5},{8,10},{9,11},{10,... | collective-permute-start | bytes 393224 | tf_op jit(solution)/shard_map/ppermute | solution.py:458
  8.6 23.2 %collective-permute-start.10 = (bf16[2,4,64,128]{3,2,1,0:T(8,128)(2,1)S(1)}, bf16[2,4,64,128]{3,2,1,0:T(8,128)(2,1)S(1)}, u32[]{:S(2)}, u32[]{:S(2)}) collective-permute-start(bf16[2,4,64,128]{3,2,1,0:T(8,128)(2,1)S(1)} %get-tuple-element.62.refs_8_), channel_id=1, source_target_pairs={{0,6},{1,7},{2,4},{3,5},{4,2},{5,3},{6,0},{7,1},{8,14},{9,15},{10,... | collective-permute-start | bytes 393224 | tf_op jit(solution)/shard_map/ppermute | solution.py:458
  9.8 22.0 %collective-permute-start.9 = (bf16[2,4,64,128]{3,2,1,0:T(8,128)(2,1)S(1)}, bf16[2,4,64,128]{3,2,1,0:T(8,128)(2,1)S(1)}, u32[]{:S(2)}, u32[]{:S(2)}) collective-permute-start(bf16[2,4,64,128]{3,2,1,0:T(8,128)(2,1)S(1)} %get-tuple-element.62.refs_8_), channel_id=1, source_target_pairs={{0,3},{1,0},{2,1},{3,2},{4,7},{5,4},{6,5},{7,6},{8,11},{9,8},{10,9... | collective-permute-start | bytes 393224 | tf_op jit(solution)/shard_map/ppermute | solution.py:458
  13.5 20.3 %all-to-all-start.1 = ((bf16[16,64,128]{2,1,0:T(8,128)(2,1)}), bf16[16,64,128]{2,1,0:T(8,128)(2,1)S(1)}, u32[]{:S(2)}, u32[]{:S(2)}) async-start(bf16[16,64,128]{2,1,0:T(8,128)(2,1)} %get-tuple-element.53), calls=%async_computation.1 | async-start | bytes 524288 | tf_op jit(solution)/shard_map/all_to_all | solution.py:468
  24.2 8.3 %collective-permute-start.8 = (bf16[2,4,64,128]{3,2,1,0:T(8,128)(2,1)S(1)}, bf16[2,4,64,128]{3,2,1,0:T(8,128)(2,1)S(1)}, u32[]{:S(2)}, u32[]{:S(2)}) collective-permute-start(bf16[2,4,64,128]{3,2,1,0:T(8,128)(2,1)S(1)} %get-tuple-element.62.refs_8_), channel_id=1, source_target_pairs={{0,1},{1,2},{2,3},{3,0},{4,5},{5,6},{6,7},{7,4},{8,9},{9,10},{10,1... | collective-permute-start | bytes 393224 | tf_op jit(solution)/shard_map/ppermute | solution.py:458
  24.3 8.9 %collective-permute-start.7 = (bf16[2,4,64,128]{3,2,1,0:T(8,128)(2,1)S(1)}, bf16[2,4,64,128]{3,2,1,0:T(8,128)(2,1)S(1)}, u32[]{:S(2)}, u32[]{:S(2)}) collective-permute-start(bf16[2,4,64,128]{3,2,1,0:T(8,128)(2,1)S(1)} %get-tuple-element.62.refs_8_), channel_id=1, source_target_pairs={{0,4},{1,5},{2,6},{3,7},{4,0},{5,1},{6,2},{7,3},{8,12},{9,13},{10,... | collective-permute-start | bytes 393224 | tf_op jit(solution)/shard_map/ppermute | solution.py:458
  30.5 1.3 copy-start.16
  31.8 0.7 copy-start.2
  32.5 0.6 copy-start.4
  33.1 0.7 copy-start.6
  33.8 37.9 %all-to-all-start = ((bf16[32,8,640]{2,1,0:T(8,128)(2,1)}), bf16[32,8,640]{2,1,0:T(8,128)(2,1)S(1)}, u32[]{:S(2)}, u32[]{:S(2)}) async-start(bf16[32,8,640]{2,1,0:T(8,128)(2,1)} %bitcast.7), calls=%async_computation | async-start | bytes 655360 | tf_op jit(solution)/shard_map/all_to_all | solution.py:475
  46.5 10.7 %collective-permute-start.15 = (bf16[16,64,128]{2,1,0:T(8,128)(2,1)S(1)}, bf16[16,64,128]{2,1,0:T(8,128)(2,1)S(1)}, u32[]{:S(2)}, u32[]{:S(2)}) collective-permute-start(bf16[16,64,128]{2,1,0:T(8,128)(2,1)S(1)} %all-to-all-done.1.near0_ref), channel_id=1, source_target_pairs={{0,4},{1,5},{2,6},{3,7},{4,0},{5,1},{6,2},{7,3},{8,12},{9,13},{10,... | collective-permute-start | bytes 786440 | tf_op jit(solution)/shard_map/ppermute | solution.py:458
  47.0 24.6 %collective-permute-start.14 = (bf16[16,64,128]{2,1,0:T(8,128)(2,1)S(1)}, bf16[16,64,128]{2,1,0:T(8,128)(2,1)S(1)}, u32[]{:S(2)}, u32[]{:S(2)}) collective-permute-start(bf16[16,64,128]{2,1,0:T(8,128)(2,1)S(1)} %all-to-all-done.1.near0_ref), channel_id=1, source_target_pairs={{0,8},{8,0},{16,24},{24,16},{32,40},{40,32},{48,56},{56,48},{64,72... | collective-permute-start | bytes 786440 | tf_op jit(solution)/shard_map/ppermute | solution.py:454
  57.2 14.5 %collective-permute-start.16 = (bf16[16,64,128]{2,1,0:T(8,128)(2,1)S(1)}, bf16[16,64,128]{2,1,0:T(8,128)(2,1)S(1)}, u32[]{:S(2)}, u32[]{:S(2)}) collective-permute-start(bf16[16,64,128]{2,1,0:T(8,128)(2,1)S(1)} %collective-permute-done.15.far0_ref), channel_id=1, source_target_pairs={{0,8},{8,0},{16,24},{24,16},{32,40},{40,32},{48,56},{56,48},{64,72... | collective-permute-start | bytes 786440 | tf_op jit(solution)/shard_map/ppermute | solution.py:454
  58.2 6.8 %collective-permute-start.4 = (bf16[24,1024]{1,0:T(8,128)(2,1)S(1)}, bf16[24,1024]{1,0:T(8,128)(2,1)S(1)}, u32[]{:S(2)}, u32[]{:S(2)}) collective-permute-start(bf16[24,1024]{1,0:T(8,128)(2,1)S(1)} %get-tuple-element.95), channel_id=1, source_target_pairs={{0,2},{1,3},{2,0},{3,1},{4,6},{5,7},{6,4},{7,5},{8,10},{9,11},{10,... | collective-permute-start | bytes 147464 | tf_op jit(solution)/shard_map/ppermute | solution.py:458
  59.4 6.7 %collective-permute-start.3 = (bf16[24,1024]{1,0:T(8,128)(2,1)S(1)}, bf16[24,1024]{1,0:T(8,128)(2,1)S(1)}, u32[]{:S(2)}, u32[]{:S(2)}) collective-permute-start(bf16[24,1024]{1,0:T(8,128)(2,1)S(1)} %get-tuple-element.95), channel_id=1, source_target_pairs={{0,6},{1,7},{2,4},{3,5},{4,2},{5,3},{6,0},{7,1},{8,14},{9,15},{10,... | collective-permute-start | bytes 147464 | tf_op jit(solution)/shard_map/ppermute | solution.py:458
  61.6 5.9 %collective-permute-start.6 = (bf16[24,1024]{1,0:T(8,128)(2,1)S(1)}, bf16[24,1024]{1,0:T(8,128)(2,1)S(1)}, u32[]{:S(2)}, u32[]{:S(2)}) collective-permute-start(bf16[24,1024]{1,0:T(8,128)(2,1)S(1)} %get-tuple-element.96), channel_id=1, source_target_pairs={{0,7},{1,4},{2,5},{3,6},{4,3},{5,0},{6,1},{7,2},{8,15},{9,12},{10,... | collective-permute-start | bytes 147464 | tf_op jit(solution)/shard_map/ppermute | solution.py:458
  65.0 2.9 %collective-permute-start.2 = (bf16[24,1024]{1,0:T(8,128)(2,1)S(1)}, bf16[24,1024]{1,0:T(8,128)(2,1)S(1)}, u32[]{:S(2)}, u32[]{:S(2)}) collective-permute-start(bf16[24,1024]{1,0:T(8,128)(2,1)S(1)} %get-tuple-element.96), channel_id=1, source_target_pairs={{0,3},{1,0},{2,1},{3,2},{4,7},{5,4},{6,5},{7,6},{8,11},{9,8},{10,9... | collective-permute-start | bytes 147464 | tf_op jit(solution)/shard_map/ppermute | solution.py:458
  66.0 5.2 %collective-permute-start.5 = (bf16[24,1024]{1,0:T(8,128)(2,1)S(1)}, bf16[24,1024]{1,0:T(8,128)(2,1)S(1)}, u32[]{:S(2)}, u32[]{:S(2)}) collective-permute-start(bf16[24,1024]{1,0:T(8,128)(2,1)S(1)} %get-tuple-element.97), channel_id=1, source_target_pairs={{0,5},{1,6},{2,7},{3,4},{4,1},{5,2},{6,3},{7,0},{8,13},{9,14},{10,... | collective-permute-start | bytes 147464 | tf_op jit(solution)/shard_map/ppermute | solution.py:458
  67.5 4.2 %collective-permute-start.1 = (bf16[24,1024]{1,0:T(8,128)(2,1)S(1)}, bf16[24,1024]{1,0:T(8,128)(2,1)S(1)}, u32[]{:S(2)}, u32[]{:S(2)}) collective-permute-start(bf16[24,1024]{1,0:T(8,128)(2,1)S(1)} %get-tuple-element.97), channel_id=1, source_target_pairs={{0,1},{1,2},{2,3},{3,0},{4,5},{5,6},{6,7},{7,4},{8,9},{9,10},{10,1... | collective-permute-start | bytes 147464 | tf_op jit(solution)/shard_map/ppermute | solution.py:458
  67.9 3.7 %collective-permute-start = (bf16[24,1024]{1,0:T(8,128)(2,1)S(1)}, bf16[24,1024]{1,0:T(8,128)(2,1)S(1)}, u32[]{:S(2)}, u32[]{:S(2)}) collective-permute-start(bf16[24,1024]{1,0:T(8,128)(2,1)S(1)} %get-tuple-element.54.refs_0_), channel_id=1, source_target_pairs={{0,4},{1,5},{2,6},{3,7},{4,0},{5,1},{6,2},{7,3},{8,12},{9,13},{10,... | collective-permute-start | bytes 147464 | tf_op jit(solution)/shard_map/ppermute | solution.py:458
  71.7 0.9 copy-start.11
  72.6 15.5 %copy-start.3 = (bf16[2,4,64,128]{3,2,1,0:T(8,128)(2,1)S(1)}, bf16[2,4,64,128]{3,2,1,0:T(8,128)(2,1)}, u32[]{:S(2)}) copy-start(bf16[2,4,64,128]{3,2,1,0:T(8,128)(2,1)} %copy-done.2) | copy-start | bytes 393220
  72.6 15.5 %copy-start.5 = (bf16[2,4,64,128]{3,2,1,0:T(8,128)(2,1)S(1)}, bf16[2,4,64,128]{3,2,1,0:T(8,128)(2,1)}, u32[]{:S(2)}) copy-start(bf16[2,4,64,128]{3,2,1,0:T(8,128)(2,1)} %copy-done.4) | copy-start | bytes 393220
  72.6 15.5 %copy-start.7 = (bf16[2,4,64,128]{3,2,1,0:T(8,128)(2,1)S(1)}, bf16[2,4,64,128]{3,2,1,0:T(8,128)(2,1)}, u32[]{:S(2)}) copy-start(bf16[2,4,64,128]{3,2,1,0:T(8,128)(2,1)} %copy-done.6) | copy-start | bytes 393220
  72.6 15.5 %copy-start.13 = (bf16[2,8,24,128]{3,2,1,0:T(8,128)(2,1)S(1)}, bf16[2,8,24,128]{3,2,1,0:T(8,128)(2,1)}, u32[]{:S(2)}) copy-start(bf16[2,8,24,128]{3,2,1,0:T(8,128)(2,1)} %constant.69.clone.refs_16_) | copy-start | bytes 294916
  75.3 27.2 %all-to-all-start.2 = ((bf16[32,8,640]{2,1,0:T(8,128)(2,1)}), bf16[32,8,640]{2,1,0:T(8,128)(2,1)S(1)}, u32[]{:S(2)}, u32[]{:S(2)}) async-start(bf16[32,8,640]{2,1,0:T(8,128)(2,1)} %mid_x.2), calls=%async_computation.2 | async-start | bytes 655360 | tf_op jit(solution)/shard_map/all_to_all | solution.py:485
  88.1 14.4 %copy-start.9 = (bf16[2,64,256]{2,1,0:T(8,128)(2,1)S(1)}, bf16[2,64,256]{2,1,0:T(8,128)(2,1)}, u32[]{:S(2)}) copy-start(bf16[2,64,256]{2,1,0:T(8,128)(2,1)} %refs_9_.3) | copy-start | bytes 196612
  88.1 14.4 %copy-start.10 = (bf16[2,256,64]{1,2,0:T(8,128)(2,1)S(1)}, bf16[2,256,64]{1,2,0:T(8,128)(2,1)}, u32[]{:S(2)}) copy-start(bf16[2,256,64]{1,2,0:T(8,128)(2,1)} %param.13) | copy-start | bytes 196612
  89.7 4.8 %collective-permute-start.17 = (bf16[24,1024]{1,0:T(8,128)(2,1)S(1)}, bf16[24,1024]{1,0:T(8,128)(2,1)S(1)}, u32[]{:S(2)}, u32[]{:S(2)}) collective-permute-start(bf16[24,1024]{1,0:T(8,128)(2,1)S(1)} %get-tuple-element.71), channel_id=1, source_target_pairs={{0,1},{1,2},{2,3},{3,0},{4,5},{5,6},{6,7},{7,4},{8,9},{9,10},{10,1... | collective-permute-start | bytes 147464 | tf_op jit(solution)/shard_map/ppermute | solution.py:458
  89.8 5.8 %collective-permute-start.18 = (bf16[24,1024]{1,0:T(8,128)(2,1)S(1)}, bf16[24,1024]{1,0:T(8,128)(2,1)S(1)}, u32[]{:S(2)}, u32[]{:S(2)}) collective-permute-start(bf16[24,1024]{1,0:T(8,128)(2,1)S(1)} %get-tuple-element.72), channel_id=1, source_target_pairs={{0,2},{1,3},{2,0},{3,1},{4,6},{5,7},{6,4},{7,5},{8,10},{9,11},{10,... | collective-permute-start | bytes 147464 | tf_op jit(solution)/shard_map/ppermute | solution.py:458
  92.9 3.5 %collective-permute-start.19 = (bf16[24,1024]{1,0:T(8,128)(2,1)S(1)}, bf16[24,1024]{1,0:T(8,128)(2,1)S(1)}, u32[]{:S(2)}, u32[]{:S(2)}) collective-permute-start(bf16[24,1024]{1,0:T(8,128)(2,1)S(1)} %get-tuple-element.73), channel_id=1, source_target_pairs={{0,3},{1,0},{2,1},{3,2},{4,7},{5,4},{6,5},{7,6},{8,11},{9,8},{10,9... | collective-permute-start | bytes 147464 | tf_op jit(solution)/shard_map/ppermute | solution.py:458
  102.5 35.7 %copy-start.12 = (bf16[288,256]{1,0:T(8,128)(2,1)S(1)}, bf16[288,256]{1,0:T(8,128)(2,1)}, u32[]{:S(2)}) copy-start(bf16[288,256]{1,0:T(8,128)(2,1)} %constant.68.clone.tab_ref) | copy-start | bytes 442372
  116.9 1.3 copy-start.17
  118.2 20.0 %all-to-all-start.3 = ((bf16[32,8,640]{2,1,0:T(8,128)(2,1)}), bf16[32,8,640]{2,1,0:T(8,128)(2,1)S(1)}, u32[]{:S(2)}, u32[]{:S(2)}) async-start(bf16[32,8,640]{2,1,0:T(8,128)(2,1)} %bitcast.14), calls=%async_computation.3 | async-start | bytes 655360 | tf_op jit(solution)/shard_map/all_to_all | solution.py:475
  123.6 7.8 %collective-permute-start.24 = (bf16[24,1024]{1,0:T(8,128)(2,1)S(1)}, bf16[24,1024]{1,0:T(8,128)(2,1)S(1)}, u32[]{:S(2)}, u32[]{:S(2)}) collective-permute-start(bf16[24,1024]{1,0:T(8,128)(2,1)S(1)} %get-tuple-element.91), channel_id=1, source_target_pairs={{0,2},{1,3},{2,0},{3,1},{4,6},{5,7},{6,4},{7,5},{8,10},{9,11},{10,... | collective-permute-start | bytes 147464 | tf_op jit(solution)/shard_map/ppermute | solution.py:458
  126.4 5.9 %collective-permute-start.23 = (bf16[24,1024]{1,0:T(8,128)(2,1)S(1)}, bf16[24,1024]{1,0:T(8,128)(2,1)S(1)}, u32[]{:S(2)}, u32[]{:S(2)}) collective-permute-start(bf16[24,1024]{1,0:T(8,128)(2,1)S(1)} %get-tuple-element.91), channel_id=1, source_target_pairs={{0,6},{1,7},{2,4},{3,5},{4,2},{5,3},{6,0},{7,1},{8,14},{9,15},{10,... | collective-permute-start | bytes 147464 | tf_op jit(solution)/shard_map/ppermute | solution.py:458
  126.9 5.8 %collective-permute-start.26 = (bf16[24,1024]{1,0:T(8,128)(2,1)S(1)}, bf16[24,1024]{1,0:T(8,128)(2,1)S(1)}, u32[]{:S(2)}, u32[]{:S(2)}) collective-permute-start(bf16[24,1024]{1,0:T(8,128)(2,1)S(1)} %get-tuple-element.92), channel_id=1, source_target_pairs={{0,7},{1,4},{2,5},{3,6},{4,3},{5,0},{6,1},{7,2},{8,15},{9,12},{10,... | collective-permute-start | bytes 147464 | tf_op jit(solution)/shard_map/ppermute | solution.py:458
  129.9 3.2 %collective-permute-start.22 = (bf16[24,1024]{1,0:T(8,128)(2,1)S(1)}, bf16[24,1024]{1,0:T(8,128)(2,1)S(1)}, u32[]{:S(2)}, u32[]{:S(2)}) collective-permute-start(bf16[24,1024]{1,0:T(8,128)(2,1)S(1)} %get-tuple-element.92), channel_id=1, source_target_pairs={{0,3},{1,0},{2,1},{3,2},{4,7},{5,4},{6,5},{7,6},{8,11},{9,8},{10,9... | collective-permute-start | bytes 147464 | tf_op jit(solution)/shard_map/ppermute | solution.py:458
  130.5 5.3 %collective-permute-start.25 = (bf16[24,1024]{1,0:T(8,128)(2,1)S(1)}, bf16[24,1024]{1,0:T(8,128)(2,1)S(1)}, u32[]{:S(2)}, u32[]{:S(2)}) collective-permute-start(bf16[24,1024]{1,0:T(8,128)(2,1)S(1)} %get-tuple-element.93), channel_id=1, source_target_pairs={{0,5},{1,6},{2,7},{3,4},{4,1},{5,2},{6,3},{7,0},{8,13},{9,14},{10,... | collective-permute-start | bytes 147464 | tf_op jit(solution)/shard_map/ppermute | solution.py:458
  131.4 4.4 %collective-permute-start.21 = (bf16[24,1024]{1,0:T(8,128)(2,1)S(1)}, bf16[24,1024]{1,0:T(8,128)(2,1)S(1)}, u32[]{:S(2)}, u32[]{:S(2)}) collective-permute-start(bf16[24,1024]{1,0:T(8,128)(2,1)S(1)} %get-tuple-element.93), channel_id=1, source_target_pairs={{0,1},{1,2},{2,3},{3,0},{4,5},{5,6},{6,7},{7,4},{8,9},{9,10},{10,1... | collective-permute-start | bytes 147464 | tf_op jit(solution)/shard_map/ppermute | solution.py:458
  132.2 3.8 %collective-permute-start.20 = (bf16[24,1024]{1,0:T(8,128)(2,1)S(1)}, bf16[24,1024]{1,0:T(8,128)(2,1)S(1)}, u32[]{:S(2)}, u32[]{:S(2)}) collective-permute-start(bf16[24,1024]{1,0:T(8,128)(2,1)S(1)} %get-tuple-element.78.refs_0_), channel_id=1, source_target_pairs={{0,4},{1,5},{2,6},{3,7},{4,0},{5,1},{6,2},{7,3},{8,12},{9,13},{10,... | collective-permute-start | bytes 147464 | tf_op jit(solution)/shard_map/ppermute | solution.py:458
  141.0 24.8 %all-to-all-start.4 = ((bf16[32,8,640]{2,1,0:T(8,128)(2,1)}), bf16[32,8,640]{2,1,0:T(8,128)(2,1)S(1)}, u32[]{:S(2)}, u32[]{:S(2)}) async-start(bf16[32,8,640]{2,1,0:T(8,128)(2,1)} %mid_x.3), calls=%async_computation.4 | async-start | bytes 655360 | tf_op jit(solution)/shard_map/all_to_all | solution.py:485
  152.9 4.5 %collective-permute-start.27 = (bf16[24,1024]{1,0:T(8,128)(2,1)S(1)}, bf16[24,1024]{1,0:T(8,128)(2,1)S(1)}, u32[]{:S(2)}, u32[]{:S(2)}) collective-permute-start(bf16[24,1024]{1,0:T(8,128)(2,1)S(1)} %get-tuple-element.87), channel_id=1, source_target_pairs={{0,1},{1,2},{2,3},{3,0},{4,5},{5,6},{6,7},{7,4},{8,9},{9,10},{10,1... | collective-permute-start | bytes 147464 | tf_op jit(solution)/shard_map/ppermute | solution.py:458
  153.0 5.6 %collective-permute-start.28 = (bf16[24,1024]{1,0:T(8,128)(2,1)S(1)}, bf16[24,1024]{1,0:T(8,128)(2,1)S(1)}, u32[]{:S(2)}, u32[]{:S(2)}) collective-permute-start(bf16[24,1024]{1,0:T(8,128)(2,1)S(1)} %get-tuple-element.88), channel_id=1, source_target_pairs={{0,2},{1,3},{2,0},{3,1},{4,6},{5,7},{6,4},{7,5},{8,10},{9,11},{10,... | collective-permute-start | bytes 147464 | tf_op jit(solution)/shard_map/ppermute | solution.py:458
  155.9 3.6 %collective-permute-start.29 = (bf16[24,1024]{1,0:T(8,128)(2,1)S(1)}, bf16[24,1024]{1,0:T(8,128)(2,1)S(1)}, u32[]{:S(2)}, u32[]{:S(2)}) collective-permute-start(bf16[24,1024]{1,0:T(8,128)(2,1)S(1)} %get-tuple-element.89), channel_id=1, source_target_pairs={{0,3},{1,0},{2,1},{3,2},{4,7},{5,4},{6,5},{7,6},{8,11},{9,8},{10,9... | collective-permute-start | bytes 147464 | tf_op jit(solution)/shard_map/ppermute | solution.py:458

commit v2 on v1

--- a/solution.py
+++ b/solution.py
@@ -19,6 +19,7 @@
 RX = 10
 RY = 20
 RYP = 24
+ROWS = RYP + 32
 GROUP = 16
 WIDE = GROUP * CH
 LINE = 8
@@ -110,7 +111,7 @@
         kron_ref[r * CH : (r + 1) * CH, :] = jnp.where(eye, row, 0.0).astype(BF16)
 
 
-def coefficients(g, state, kron_ref, cy_ref, acc_ref, zx_ref, zy_ref):
+def coefficients(g, state, kron_ref, cy_ref, wy_ref, acc_ref, zx_ref, zy_ref):
     part = dot_nt(state, kron_ref[...])
 
     @pl.when(g == 0)
@@ -121,14 +122,17 @@
     def _():
         acc_ref[...] += part
 
-    zy_ref[0] = dot(cy_ref[...], state).astype(BF16)
+    zy_ref[0, :RYP] = dot(cy_ref[...], state).astype(BF16)
+    zy_ref[0, RYP:] = wy_ref[0]
 
     @pl.when(g == pl.num_programs(0) - 1)
     def _():
         zx_ref[...] = acc_ref[...].astype(BF16)
 
 
-def first_kernel(field_ref, bx_ref, cy_ref, state_ref, zx_ref, zy_ref, t_ref, kron_ref, acc_ref):
+def first_kernel(
+    field_ref, bx_ref, cy_ref, wy_ref, state_ref, zx_ref, zy_ref, t_ref, kron_ref, acc_ref
+):
     for h in range(2):
         part = field_ref[:, :, h * 128 : (h + 1) * 128].astype(F32)
         t_ref[h] = part.reshape(CH * GROUP, 128)
@@ -138,10 +142,11 @@
             block = jnp.concatenate(two, axis=0).T.astype(BF16)
             state_ref[h * 128 : (h + 1) * 128, p * 128 : (p + 1) * 128] = block
     fill_kron(bx_ref, kron_ref)
-    coefficients(pl.program_id(0), state_ref[...], kron_ref, cy_ref, acc_ref, zx_ref, zy_ref)
-
-
-def first_call(field, c):
+    g = pl.program_id(0)
+    coefficients(g, state_ref[...], kron_ref, cy_ref, wy_ref, acc_ref, zx_ref, zy_ref)
+
+
+def first_call(field, wy, c):
     return pl.pallas_call(
         first_kernel,
         name="first",
@@ -150,16 +155,17 @@
             pl.BlockSpec((CH, GROUP, 256), lambda g: (0, g, 0)),
             pl.BlockSpec((16, 128), lambda g: (0, 0)),
             pl.BlockSpec((RYP, 256), lambda g: (0, 0)),
+            pl.BlockSpec((1, ROWS - RYP, QUARTER), lambda g: (0, 0, 0)),
         ],
         out_specs=[
             pl.BlockSpec((256, WIDE), lambda g: (0, g)),
             pl.BlockSpec((256, RX * CH), lambda g: (0, 0)),
-            pl.BlockSpec((1, RYP, WIDE), lambda g: (g, 0, 0)),
+            pl.BlockSpec((1, ROWS, WIDE), lambda g: (g, 0, 0)),
         ],
         out_shape=[
             jax.ShapeDtypeStruct((256, 4096), BF16),
             jax.ShapeDtypeStruct((256, RX * CH), BF16),
-            jax.ShapeDtypeStruct((4, RYP, QUARTER), BF16),
+            jax.ShapeDtypeStruct((4, ROWS, QUARTER), BF16),
         ],
         scratch_shapes=[
             pltpu.VMEM((2, CH * GROUP, 128), F32),
@@ -168,7 +174,7 @@
         ],
         compiler_params=params(36),
         cost_estimate=estimate(10),
-    )(field, c["bx"], c["cy"])
+    )(field, c["bx"], c["cy"], wy)
 
 
 def mode_weights(w, sign):
@@ -188,7 +194,7 @@
 
 
 def mid_x_kernel(
-    core_ref, layer_ref, recv_ref, near0_ref, near1_ref, far0_ref, far1_ref, tab_ref, *refs
+    core_ref, recv_ref, w0_ref, w1_ref, tab_ref, *refs
 ):
     send_ref, r_ref, xs_ref, ms_ref, o_ref = refs
     pairs = RX // 2
@@ -207,13 +213,7 @@
         x = x + pltpu.roll(jnp.where(first, s[32:64], s[64:96]), 64, 1)
         xs_ref[pl.ds(y, MODES, stride=LINE), :] = x
     core = core_ref[0]
-    layer = layer_ref[0]
-
-    def weights(t):
-        mine = jnp.where(layer == 0, near0_ref[t].astype(F32), far0_ref[t].astype(F32))
-        swapped = jnp.where(layer == 0, near1_ref[t].astype(F32), far1_ref[t].astype(F32))
-        return [(t * 2 + core, mine), (t * 2 + 1 - core, swapped)]
-
+    weights = lambda t: [(t * 2 + core, w0_ref[t, 0]), (t * 2 + 1 - core, w1_ref[t, 0])]
     mix(xs_ref, ms_ref, LINE, 16, weights)
     cols = []
     for y in range(LINE):
@@ -236,13 +236,14 @@
     return pl.BlockSpec(a.shape, lambda *_: (0,) * a.ndim)
 
 
-def mid_x(core, layer, recv, w, c):
+def mid_x(layer, core, recv, w0, w1, c):
+    weights = pl.BlockSpec((16, 1, CH, 128), lambda i: (0, layer, 0, 0))
     return pl.pallas_call(
         mid_x_kernel,
         name="mid_x",
         grid=(1,),
-        in_specs=[pl.BlockSpec(memory_space=pltpu.SMEM)] * 2
-        + [whole(a) for a in (recv, *w, c["mid_x"])],
+        in_specs=[pl.BlockSpec(memory_space=pltpu.SMEM)]
+        + [whole(recv), weights, weights, whole(c["mid_x"])],
         out_specs=whole(recv),
         out_shape=jax.ShapeDtypeStruct(recv.shape, BF16),
         scratch_shapes=[
@@ -253,14 +254,12 @@
         ],
         compiler_params=params(16),
         cost_estimate=estimate(3),
-    )(core, layer, recv, *w, c["mid_x"])
+    )(core, recv, w0, w1, c["mid_x"])
 
 
 def mid_y_kernel(me_ref, *refs):
-    z_refs, w_refs = refs[:8], refs[8:16]
-    tab_ref = refs[16]
-    out_refs = refs[17:21]
-    xs_ref, ms_ref, w_ref = refs[21:]
+    z_refs, tab_ref, out_refs = refs[:8], refs[8], refs[9:13]
+    xs_ref, ms_ref, w_ref = refs[13:]
     first = half_mask(MODES)
     lines = 16
     half, quarter = me_ref[0] // 4, lax.rem(me_ref[0], 4)
@@ -273,7 +272,7 @@
     table = [tab_ref[1, half * 4 + lax.rem(quarter + step, 4)].astype(F32) for step in range(4)]
     inverse = jnp.concatenate(table, axis=0)[:, :64].astype(BF16)
     for g in range(2):
-        z = [ref[:, g * 512 : (g + 1) * 512].astype(F32) for ref in z_refs]
+        z = [ref[:RYP, g * 512 : (g + 1) * 512].astype(F32) for ref in z_refs]
         z = jnp.concatenate(z, axis=0).astype(BF16)
         spec = dot(forward, z)
         for b in range(4):
@@ -286,8 +285,11 @@
             xs_ref[pl.ds(line + 1, MODES, stride=lines), :] = jnp.where(
                 first, pltpu.roll(re, 64, 1), im
             )
-    for slot, src in enumerate(sources):
-        w_ref[src] = w_refs[slot][0]
+    for ref, src in zip(z_refs, sources):
+        packed = ref[RYP:, :].astype(F32)
+        for j in range(4):
+            tiles = [packed[j * 8 : (j + 1) * 8, t * 128 : (t + 1) * 128] for t in range(8)]
+            w_ref[src, j] = jnp.concatenate(tiles, axis=0).astype(BF16)
     weights = lambda src: [(src * 4 + j, w_ref[src, j]) for j in range(4)]
     mix(xs_ref, ms_ref, lines, 8, weights)
     for g in range(2):
@@ -304,14 +306,13 @@
             out_refs[step][:, g * 512 : (g + 1) * 512] = out[step * RYP : (step + 1) * RYP]
 
 
-def mid_y(layer, me, zs, w, c):
+def mid_y(me, zs, c):
     return pl.pallas_call(
         mid_y_kernel,
         name="mid_y",
         grid=(1,),
         in_specs=[pl.BlockSpec(memory_space=pltpu.SMEM)]
         + [whole(z) for z in zs]
-        + [pl.BlockSpec((1, 4, CH, 128), lambda i: (layer, 0, 0, 0))] * 8
         + [whole(c["mid_y"])],
         out_specs=[pl.BlockSpec((RYP, QUARTER), lambda i: (0, 0))] * 4,
         scratch_shapes=[pltpu.VMEM((MODES * 16, 128), F32)] * 2
@@ -319,7 +320,7 @@
         out_shape=[jax.ShapeDtypeStruct((RYP, QUARTER), BF16)] * 4,
         compiler_params=params(20),
         cost_estimate=estimate(2),
-    )(me, *zs, *w, c["mid_y"])
+    )(me, *zs, c["mid_y"])
 
 
 def gelu(x):
@@ -334,7 +335,7 @@
     yy_refs = refs[3:7]
     cy_ref, state_ref, we_ref, wr_ref = refs[7:11]
     if more:
-        out_ref, zx_ref, zy_ref, kron_ref, we4_ref, wr4_ref, yy_ref, acc_ref = refs[11:]
+        wy_ref, out_ref, zx_ref, zy_ref, kron_ref, we4_ref, wr4_ref, yy_ref, acc_ref = refs[11:]
     else:
         out_ref, kron_ref, we4_ref, wr4_ref, yy_ref, t_ref = refs[11:]
     g = pl.program_id(0)
@@ -373,14 +374,14 @@
                 t_ref[h, pl.ds(x, CH, stride=GROUP), :] = block[:CH]
                 t_ref[h, pl.ds(x + 1, CH, stride=GROUP), :] = block[CH:]
     if more:
-        coefficients(g, out_ref[...], kron_ref, cy_ref, acc_ref, zx_ref, zy_ref)
+        coefficients(g, out_ref[...], kron_ref, cy_ref, wy_ref, acc_ref, zx_ref, zy_ref)
     else:
         for h in range(2):
             part = t_ref[h].reshape(CH, GROUP, 128).astype(BF16)
             out_ref[:, :, h * 128 : (h + 1) * 128] = part
 
 
-def last_call(layer, more, me, yx, yy, state, we, wr, c):
+def last_call(layer, more, me, yx, yy, state, we, wr, wy, c):
     in_specs = [
         pl.BlockSpec(memory_space=pltpu.SMEM),
         pl.BlockSpec((256, RX * CH), lambda g: (0, 0)),
@@ -393,16 +394,21 @@
     ]
     scratch = [pltpu.VMEM((RX * CH, WIDE), BF16)] + [pltpu.VMEM((256, 1024), BF16)] * 2
     scratch.append(pltpu.VMEM((4, RYP, QUARTER), BF16))
+    args = [me, yx, c["bx"], *yy, c["cy"], state, we, wr]
     if more:
+        in_specs.append(
+            pl.BlockSpec((1, ROWS - RYP, QUARTER), lambda g: (layer + 1, 0, 0))
+        )
+        args.append(wy)
         out_specs = [
             pl.BlockSpec((256, WIDE), lambda g: (0, g)),
             pl.BlockSpec((256, RX * CH), lambda g: (0, 0)),
-            pl.BlockSpec((1, RYP, WIDE), lambda g: (g, 0, 0)),
+            pl.BlockSpec((1, ROWS, WIDE), lambda g: (g, 0, 0)),
         ]
         out_shape = [
             jax.ShapeDtypeStruct((256, 4096), BF16),
             jax.ShapeDtypeStruct((256, RX * CH), BF16),
-            jax.ShapeDtypeStruct((4, RYP, QUARTER), BF16),
+            jax.ShapeDtypeStruct((4, ROWS, QUARTER), BF16),
         ]
         scratch.append(pltpu.VMEM((256, RX * CH), F32))
     else:
@@ -419,35 +425,37 @@
         scratch_shapes=scratch,
         compiler_params=params(40),
         cost_estimate=estimate(12),
-    )(me, yx, c["bx"], *yy, c["cy"], state, we, wr)
-
-
-def pack_kernel(half_ref, wx_ref, wy_ref, x_ref, y_ref):
+    )(*args)
+
+
+def pack_kernel(wx_ref, wy_ref, x_ref, y_ref):
     def join(parts):
         return jnp.concatenate([part.astype(F32) for part in parts], axis=1)
 
     for layer in range(LAYERS):
+        own = join([wx_ref[layer, 0, i] for i in range(2)]).astype(BF16)
+        for i in range(16):
+            x_ref[i, layer] = own
+        rows = []
         for j in range(4):
-            y_ref[layer, j] = join([wy_ref[layer, j, i] for i in range(2)]).astype(BF16)
-    own = [join([wx_ref[layer, 0, i] for i in range(2)]) for layer in range(LAYERS)]
-    mode = jnp.where(half_ref[0] == 0, own[0], own[1]).astype(BF16)
-    for i in range(16):
-        x_ref[i] = mode
-
-
-def pack_call(half, spectral_x, spectral_y):
-    shapes = (16, CH, 128), (LAYERS, 4, CH, 128)
+            own = join([wy_ref[layer, j, i] for i in range(2)])
+            rows.append(join([own[t * 8 : (t + 1) * 8] for t in range(8)]))
+        y_ref[layer] = jnp.concatenate(rows, axis=0).astype(BF16)
+
+
+def pack_call(spectral_x, spectral_y):
+    shapes = (16, LAYERS, CH, 128), (LAYERS, ROWS - RYP, QUARTER)
     out_shape = [jax.ShapeDtypeStruct(shape, BF16) for shape in shapes]
     return pl.pallas_call(
         pack_kernel,
         name="pack",
         grid=(1,),
-        in_specs=[pl.BlockSpec(memory_space=pltpu.SMEM), whole(spectral_x), whole(spectral_y)],
+        in_specs=[whole(spectral_x), whole(spectral_y)],
         out_specs=[whole(a) for a in out_shape],
         out_shape=out_shape,
         compiler_params=params(16),
         cost_estimate=estimate(2),
-    )(half, spectral_x, spectral_y)
+    )(spectral_x, spectral_y)
 
 
 def swap_cores(x):
@@ -462,34 +470,28 @@
     c = {name: jnp.asarray(value) for name, value in make_constants().items()}
     core = lax.rem(lax.axis_index("gx"), 2).reshape(1).astype(jnp.int32)
     me = lax.axis_index("gy").reshape(1).astype(jnp.int32)
-    half = me // 4
-    own_x, own_y = pack_call(half, spectral_x, spectral_y)
+    own_x, wy = pack_call(spectral_x, spectral_y)
     same_core = [list(range(s, 32, 2)) for s in range(2)]
     mine = lax.all_to_all(own_x, "gx", 0, 0, axis_index_groups=same_core, tiled=True)
-    wy = [own_y] + [permute_y(own_y, flip, step) for flip, step in SHIFTS]
+    swapped = swap_cores(mine)
     wr = jnp.swapaxes(reduce_weight, 1, 2)
-    state, zx, zy = first_call(state_field[0], c)
-    state = pltpu.with_memory_space_constraint(state, pltpu.HBM)
-    zx, wy = lax.optimization_barrier((zx, wy))
+    state, zx, zy = first_call(state_field[0], wy, c)
     for l in range(LAYERS):
+        state = pltpu.with_memory_space_constraint(state, pltpu.HBM)
         recv = lax.all_to_all(zx.reshape(32, LINE, RX * CH), "gx", 0, 0, tiled=True)
         zs = []
         for flip, step in ((0, 0),) + SHIFTS:
             chunk = lax.dynamic_slice_in_dim(zy, lax.rem(me[0] + step, 4), 1, 0)[0]
             zs.append(permute_y(chunk, flip, step) if flip or step else chunk)
-        if l == 0:
-            other = permute_y(mine, 1, 0)
-            wx = [mine, swap_cores(mine), other, swap_cores(other)]
         zs, recv = lax.optimization_barrier((zs, recv))
-        send = mid_x(core, lax.rem(half + l, 2), recv, wx, c)
+        send = mid_x(l, core, recv, mine, swapped, c)
         yx = lax.all_to_all(send, "gx", 0, 0, tiled=True).reshape(256, RX * CH)
-        yy = mid_y(l, me, zs, wy, c)
+        yy = mid_y(me, zs, c)
         yy = [yy[0]] + [permute_y(yy[step], 0, step) for step in range(1, 4)]
         more = l + 1 < LAYERS
-        got = last_call(l, more, me, yx, yy, state, expand_weight, wr, c)
+        got = last_call(l, more, me, yx, yy, state, expand_weight, wr, wy, c)
         if more:
             state, zx, zy = got
-            state = pltpu.with_memory_space_constraint(state, pltpu.HBM)
     return got[0][None]
 
 

time: 179 us -> 164 us (0.916)
  starting transfers between devices: 92 us -> 71 us
  waiting for transfers between devices: 36.2 us -> 44.8 us
  local copies, waits for them, and re-layouts: 7.4 us -> 4.7 us
    ppermute x28 -> x20, starting transfers between devices: 38.8 us -> 25.8 us  [permute_y(): return lax.ppermute(x, 'gy', [(i, moved(i, flip, step)) for i in range(8)])]
    all_to_all x1, waiting for transfers between devices: 0.01 us -> 7.78 us  [body(): lax.all_to_all(own_x, 'gx', 0, 0, axis_index_groups=same_core, tiled=True)]
    all_to_all x2, starting transfers between devices: 18.1 us -> 13 us  [body(): recv = lax.all_to_all(zx.reshape(32, LINE, RX * CH), 'gx', 0, 0, tiled=True)]
    ppermute x28 -> x20, waiting for transfers between devices: 21.5 us -> 24.9 us  [permute_y(): return lax.ppermute(x, 'gy', [(i, moved(i, flip, step)) for i in range(8)])]
    all_to_all x2, starting transfers between devices: 23 us -> 20.2 us  [body(): yx = lax.all_to_all(send, 'gx', 0, 0, tiled=True).reshape(256, RX * CH)]
    unnamed x36 -> x22, local copies, waits for them, and re-layouts: 7.36 us -> 4.63 us
    all_to_all x2, waiting for transfers between devices: 2.16 us -> 0.01 us  [body(): recv = lax.all_to_all(zx.reshape(32, LINE, RX * CH), 'gx', 0, 0, tiled=True)]
  transfers between devices with their start and end apart: 35 -> 26, of which waited for: 16 -> 16; matrix products, arithmetic and copies ran while one was open for 0% -> 0% of each run, Pallas kernels for 5% -> 6%
where the time goes in v2:
time: 164 us; the launch traced here: 163 us
  starting transfers between devices  71 us (43%)
  waiting for transfers between devices  44.8 us (27%)
  Pallas kernels  42.8 us (26%)
  local copies, waits for them, and re-layouts  4.7 us (3%)
    pallas_call x2, Pallas kernels, last_call(): pl.pallas_call(functools.partial(last_kernel, more), name='last', grid=(6...  27 us
    ppermute x20, starting transfers between devices, permute_y(): return lax.ppermute(x, 'gy', [(i, moved(i, flip, step)) for i in range(8)])  25.8 us
    ppermute x20, waiting for transfers between devices, permute_y(): return lax.ppermute(x, 'gy', [(i, moved(i, flip, step)) for i in range(8)])  24.9 us
    all_to_all x2, starting transfers between devices, body(): yx = lax.all_to_all(send, 'gx', 0, 0, tiled=True).reshape(256, RX * CH)  20.2 us
    all_to_all x2, starting transfers between devices, body(): recv = lax.all_to_all(zx.reshape(32, LINE, RX * CH), 'gx', 0, 0, tiled=True)  13 us
    all_to_all x2, waiting for transfers between devices, body(): yx = lax.all_to_all(send, 'gx', 0, 0, tiled=True).reshape(256, RX * CH)  12.1 us
    all_to_all x1, starting transfers between devices, body(): lax.all_to_all(own_x, 'gx', 0, 0, axis_index_groups=same_core, tiled=True)  11.7 us
    all_to_all x1, waiting for transfers between devices, body(): lax.all_to_all(own_x, 'gx', 0, 0, axis_index_groups=same_core, tiled=True)  7.78 us
  transfers between devices with their start and end apart: 26, of which 16 were waited for; matrix products, arithmetic and copies ran while one was open for 0% of the time, Pallas kernels for 6%

profile of v2, /device:TPU:1, one launch (start us, length us, event | category | flops | bytes accessed | tf_op | source)
XLA Modules:
  0.0 163.5 jit_solution(16739546822640536850)
XLA Ops:
  0.0 1.1 copy-done.1
  1.1 0.8 copy-done.2
  1.9 0.9 pack.1
  2.9 11.7 %all-to-all-start.1 = ((bf16[16,2,64,128]{3,2,1,0:T(8,128)(2,1)}), bf16[16,2,64,128]{3,2,1,0:T(8,128)(2,1)S(1)}, u32[]{:S(2)}, u32[]{:S(2)}) async-start(bf16[16,2,64,128]{3,2,1,0:T(8,128)(2,1)} %get-tuple-element.43), calls=%async_computation.1 | async-start | bytes 1048576 | tf_op jit(solution)/shard_map/all_to_all | solution.py:475
  14.7 0.0 copy-start.5
  14.7 6.1 %first.1 = (bf16[256,4096]{1,0:T(8,128)(2,1)S(1)}, bf16[256,640]{1,0:T(8,128)(2,1)}, bf16[4,56,1024]{2,1,0:T(8,128)(2,1)S(1)}) custom-call(bf16[64,64,256]{2,1,0:T(8,128)(2,1)S(1)} %bitcast.27, bf16[16,128]{1,0:T(8,128)(2,1)S(1)} %copy-done.8, bf16[24,256]{1,0:T(8,128)(2,1)S(1)} %copy-done.7, bf16[2,32,1024]{2,1,0:T(8,128)(2,1)S(1)} %get-tuple-element.39.wy_ref.refs_11_), custom_call_target="tpu_custom_call" | custom-call | flops 10000000000 | bytes 1048576 | tf_op jit(solution)/shard_map/first/pallas_call | solution.py:150
  20.8 1.3 copy-done.9
  22.1 7.8 %all-to-all-done.1.w0_ref = bf16[16,2,64,128]{3,2,1,0:T(8,128)(2,1)S(1)} async-done(((bf16[16,2,64,128]{3,2,1,0:T(8,128)(2,1)}), bf16[16,2,64,128]{3,2,1,0:T(8,128)(2,1)S(1)}, u32[]{:S(2)}, u32[]{:S(2)}) %all-to-all-start.1) | async-done | bytes 524320 | tf_op jit(solution)/shard_map/all_to_all | solution.py:475
  29.9 7.5 %all-to-all-start = ((bf16[32,8,640]{2,1,0:T(8,128)(2,1)}), bf16[32,8,640]{2,1,0:T(8,128)(2,1)S(1)}, u32[]{:S(2)}, u32[]{:S(2)}) async-start(bf16[32,8,640]{2,1,0:T(8,128)(2,1)} %bitcast.7), calls=%async_computation | async-start | bytes 655360 | tf_op jit(solution)/shard_map/all_to_all | solution.py:481
  37.4 0.3 collective-permute-start.7
  37.8 2.8 %collective-permute-start.4 = (bf16[56,1024]{1,0:T(8,128)(2,1)S(1)}, bf16[56,1024]{1,0:T(8,128)(2,1)S(1)}, u32[]{:S(2)}, u32[]{:S(2)}) collective-permute-start(bf16[56,1024]{1,0:T(8,128)(2,1)S(1)} %get-tuple-element.77), channel_id=1, source_target_pairs={{0,2},{1,3},{2,0},{3,1},{4,6},{5,7},{6,4},{7,5},{8,10},{9,11},{10,... | collective-permute-start | bytes 344072 | tf_op jit(solution)/shard_map/ppermute | solution.py:466
  40.6 0.3 collective-permute-start.3
  40.9 3.3 %collective-permute-start.6 = (bf16[56,1024]{1,0:T(8,128)(2,1)S(1)}, bf16[56,1024]{1,0:T(8,128)(2,1)S(1)}, u32[]{:S(2)}, u32[]{:S(2)}) collective-permute-start(bf16[56,1024]{1,0:T(8,128)(2,1)S(1)} %get-tuple-element.78), channel_id=1, source_target_pairs={{0,7},{1,4},{2,5},{3,6},{4,3},{5,0},{6,1},{7,2},{8,15},{9,12},{10,... | collective-permute-start | bytes 344072 | tf_op jit(solution)/shard_map/ppermute | solution.py:466
  44.2 0.6 collective-permute-start.2
  44.7 0.0 collective-permute-done.4.refs_5_
  44.7 1.0 collective-permute-start.5
  45.8 1.9 %collective-permute-done.3.refs_4_ = bf16[56,1024]{1,0:T(8,128)(2,1)S(1)} collective-permute-done((bf16[56,1024]{1,0:T(8,128)(2,1)S(1)}, bf16[56,1024]{1,0:T(8,128)(2,1)S(1)}, u32[]{:S(2)}, u32[]{:S(2)}) %collective-permute-start.3) | collective-permute-done | bytes 114720 | tf_op jit(solution)/shard_map/ppermute | solution.py:466
  47.7 0.7 collective-permute-start.1
  48.4 3.8 %collective-permute-done.6.refs_7_ = bf16[56,1024]{1,0:T(8,128)(2,1)S(1)} collective-permute-done((bf16[56,1024]{1,0:T(8,128)(2,1)S(1)}, bf16[56,1024]{1,0:T(8,128)(2,1)S(1)}, u32[]{:S(2)}, u32[]{:S(2)}) %collective-permute-start.6) | collective-permute-done | bytes 114720 | tf_op jit(solution)/shard_map/ppermute | solution.py:466
  52.2 0.6 collective-permute-start
  52.8 0.8 collective-permute-done.2.refs_3_
  53.6 2.5 %collective-permute-done.refs_1_ = bf16[56,1024]{1,0:T(8,128)(2,1)S(1)} collective-permute-done((bf16[56,1024]{1,0:T(8,128)(2,1)S(1)}, bf16[56,1024]{1,0:T(8,128)(2,1)S(1)}, u32[]{:S(2)}, u32[]{:S(2)}) %collective-permute-start) | collective-permute-done | bytes 114720 | tf_op jit(solution)/shard_map/ppermute | solution.py:466
  56.1 0.0 all-to-all-done.recv_ref
  56.1 0.0 collective-permute-done.7.w1_ref
  56.1 0.0 copy-start.6
  56.1 2.8 %mid_x.2 = bf16[32,8,640]{2,1,0:T(8,128)(2,1)} custom-call(s32[1]{0:T(128)} %bitcast.1.core_ref, bf16[32,8,640]{2,1,0:T(8,128)(2,1)S(1)} %all-to-all-done.recv_ref, bf16[16,2,64,128]{3,2,1,0:T(8,128)(2,1)S(1)} %all-to-all-done.1.w0_ref, bf16[16,2,64,128]{3,2,1,0:T(8,128)(2,1)S(1)} %collective-permute-done.7.w1_ref, bf16[288,256]{1,0:T(8,128)(2,1)S(1)} %copy-done.5), custom_call_target="tpu_custom_call" | custom-call | flops 3000000000 | bytes 1048576 | tf_op jit(solution)/shard_map/mid_x/pallas_call | solution.py:241
  58.9 11.0 %all-to-all-start.2 = ((bf16[32,8,640]{2,1,0:T(8,128)(2,1)}), bf16[32,8,640]{2,1,0:T(8,128)(2,1)S(1)}, u32[]{:S(2)}, u32[]{:S(2)}) async-start(bf16[32,8,640]{2,1,0:T(8,128)(2,1)} %mid_x.2), calls=%async_computation.2 | async-start | bytes 655360 | tf_op jit(solution)/shard_map/all_to_all | solution.py:488
  69.9 0.0 copy-start.3
  69.9 0.0 copy-start.4
  69.9 1.6 mid_y.2
  71.5 1.5 collective-permute-start.8
  73.0 2.3 %collective-permute-start.9 = (bf16[24,1024]{1,0:T(8,128)(2,1)S(1)}, bf16[24,1024]{1,0:T(8,128)(2,1)S(1)}, u32[]{:S(2)}, u32[]{:S(2)}) collective-permute-start(bf16[24,1024]{1,0:T(8,128)(2,1)S(1)} %get-tuple-element.54), channel_id=1, source_target_pairs={{0,2},{1,3},{2,0},{3,1},{4,6},{5,7},{6,4},{7,5},{8,10},{9,11},{10,... | collective-permute-start | bytes 147464 | tf_op jit(solution)/shard_map/ppermute | solution.py:466
  75.3 1.1 collective-permute-start.10
  76.4 0.0 collective-permute-done.8.refs_4_
  76.4 1.9 %collective-permute-done.9.refs_5_ = bf16[24,1024]{1,0:T(8,128)(2,1)S(1)} collective-permute-done((bf16[24,1024]{1,0:T(8,128)(2,1)S(1)}, bf16[24,1024]{1,0:T(8,128)(2,1)S(1)}, u32[]{:S(2)}, u32[]{:S(2)}) %collective-permute-start.9) | collective-permute-done | bytes 49184 | tf_op jit(solution)/shard_map/ppermute | solution.py:466
  78.3 0.3 collective-permute-done.10.refs_6_
  78.6 5.8 %all-to-all-done.2 = bf16[32,8,640]{2,1,0:T(8,128)(2,1)S(1)} async-done(((bf16[32,8,640]{2,1,0:T(8,128)(2,1)}), bf16[32,8,640]{2,1,0:T(8,128)(2,1)S(1)}, u32[]{:S(2)}, u32[]{:S(2)}) %all-to-all-start.2) | async-done | bytes 327712 | tf_op jit(solution)/shard_map/all_to_all | solution.py:488
  84.4 14.3 %last.2 = (bf16[256,4096]{1,0:T(8,128)(2,1)S(1)}, bf16[256,640]{1,0:T(8,128)(2,1)}, bf16[4,56,1024]{2,1,0:T(8,128)(2,1)S(1)}) custom-call(s32[1]{0:T(128)} %bitcast.me_ref.refs_0_, bf16[256,640]{1,0:T(8,128)(2,1)S(1)} %bitcast.25, bf16[16,128]{1,0:T(8,128)(2,1)S(1)} %copy-done.8, bf16[24,1024]{1,0:T(8,128)(2,1)S(1)} %get-tuple-element.52.refs_3_, ...), custom_call_target="tpu_custom_call" | custom-call | flops 12000000000 | bytes 1048576 | tf_op jit(solution)/shard_map/last/pallas_call | solution.py:418
  98.7 1.3 copy-done.10
  100.0 5.4 %all-to-all-start.3 = ((bf16[32,8,640]{2,1,0:T(8,128)(2,1)}), bf16[32,8,640]{2,1,0:T(8,128)(2,1)S(1)}, u32[]{:S(2)}, u32[]{:S(2)}) async-start(bf16[32,8,640]{2,1,0:T(8,128)(2,1)} %bitcast.14), calls=%async_computation.3 | async-start | bytes 655360 | tf_op jit(solution)/shard_map/all_to_all | solution.py:481
  105.5 2.7 %collective-permute-start.15 = (bf16[56,1024]{1,0:T(8,128)(2,1)S(1)}, bf16[56,1024]{1,0:T(8,128)(2,1)S(1)}, u32[]{:S(2)}, u32[]{:S(2)}) collective-permute-start(bf16[56,1024]{1,0:T(8,128)(2,1)S(1)} %get-tuple-element.73), channel_id=1, source_target_pairs={{0,2},{1,3},{2,0},{3,1},{4,6},{5,7},{6,4},{7,5},{8,10},{9,11},{10,... | collective-permute-start | bytes 344072 | tf_op jit(solution)/shard_map/ppermute | solution.py:466
  108.2 0.1 collective-permute-start.14
  108.3 3.6 %collective-permute-start.17 = (bf16[56,1024]{1,0:T(8,128)(2,1)S(1)}, bf16[56,1024]{1,0:T(8,128)(2,1)S(1)}, u32[]{:S(2)}, u32[]{:S(2)}) collective-permute-start(bf16[56,1024]{1,0:T(8,128)(2,1)S(1)} %get-tuple-element.74), channel_id=1, source_target_pairs={{0,7},{1,4},{2,5},{3,6},{4,3},{5,0},{6,1},{7,2},{8,15},{9,12},{10,... | collective-permute-start | bytes 344072 | tf_op jit(solution)/shard_map/ppermute | solution.py:466
  111.9 0.5 collective-permute-start.13
  112.4 0.3 collective-permute-start.16
  112.7 0.0 collective-permute-done.15.refs_5_
  112.7 0.7 collective-permute-start.12
  113.4 2.2 %collective-permute-done.14.refs_4_ = bf16[56,1024]{1,0:T(8,128)(2,1)S(1)} collective-permute-done((bf16[56,1024]{1,0:T(8,128)(2,1)S(1)}, bf16[56,1024]{1,0:T(8,128)(2,1)S(1)}, u32[]{:S(2)}, u32[]{:S(2)}) %collective-permute-start.14) | collective-permute-done | bytes 114720 | tf_op jit(solution)/shard_map/ppermute | solution.py:466
  115.6 0.2 collective-permute-start.11
  115.9 2.2 %collective-permute-done.17.refs_7_ = bf16[56,1024]{1,0:T(8,128)(2,1)S(1)} collective-permute-done((bf16[56,1024]{1,0:T(8,128)(2,1)S(1)}, bf16[56,1024]{1,0:T(8,128)(2,1)S(1)}, u32[]{:S(2)}, u32[]{:S(2)}) %collective-permute-start.17) | collective-permute-done | bytes 114720 | tf_op jit(solution)/shard_map/ppermute | solution.py:466
  118.0 2.9 %collective-permute-done.13.refs_3_ = bf16[56,1024]{1,0:T(8,128)(2,1)S(1)} collective-permute-done((bf16[56,1024]{1,0:T(8,128)(2,1)S(1)}, bf16[56,1024]{1,0:T(8,128)(2,1)S(1)}, u32[]{:S(2)}, u32[]{:S(2)}) %collective-permute-start.13) | collective-permute-done | bytes 114720 | tf_op jit(solution)/shard_map/ppermute | solution.py:466
  120.9 0.0 collective-permute-done.16.refs_6_
  120.9 3.4 %collective-permute-done.11.refs_1_ = bf16[56,1024]{1,0:T(8,128)(2,1)S(1)} collective-permute-done((bf16[56,1024]{1,0:T(8,128)(2,1)S(1)}, bf16[56,1024]{1,0:T(8,128)(2,1)S(1)}, u32[]{:S(2)}, u32[]{:S(2)}) %collective-permute-start.11) | collective-permute-done | bytes 114720 | tf_op jit(solution)/shard_map/ppermute | solution.py:466
  124.3 2.8 %mid_x.3 = bf16[32,8,640]{2,1,0:T(8,128)(2,1)} custom-call(s32[1]{0:T(128)} %bitcast.1.core_ref, bf16[32,8,640]{2,1,0:T(8,128)(2,1)S(1)} %all-to-all-done.3.recv_ref, bf16[16,2,64,128]{3,2,1,0:T(8,128)(2,1)S(1)} %all-to-all-done.1.w0_ref, bf16[16,2,64,128]{3,2,1,0:T(8,128)(2,1)S(1)} %collective-permute-done.7.w1_ref, bf16[288,256]{1,0:T(8,128)(2,1)S(1)} %copy-done.5), custom_call_target="tpu_custom_call" | custom-call | flops 3000000000 | bytes 1048576 | tf_op jit(solution)/shard_map/mid_x/pallas_call | solution.py:241
  127.1 9.2 %all-to-all-start.4 = ((bf16[32,8,640]{2,1,0:T(8,128)(2,1)}), bf16[32,8,640]{2,1,0:T(8,128)(2,1)S(1)}, u32[]{:S(2)}, u32[]{:S(2)}) async-start(bf16[32,8,640]{2,1,0:T(8,128)(2,1)} %mid_x.3), calls=%async_computation.4 | async-start | bytes 655360 | tf_op jit(solution)/shard_map/all_to_all | solution.py:488
  136.3 1.6 mid_y.3
  137.9 0.5 collective-permute-start.18
  138.4 2.4 %collective-permute-start.19 = (bf16[24,1024]{1,0:T(8,128)(2,1)S(1)}, bf16[24,1024]{1,0:T(8,128)(2,1)S(1)}, u32[]{:S(2)}, u32[]{:S(2)}) collective-permute-start(bf16[24,1024]{1,0:T(8,128)(2,1)S(1)} %get-tuple-element.70), channel_id=1, source_target_pairs={{0,2},{1,3},{2,0},{3,1},{4,6},{5,7},{6,4},{7,5},{8,10},{9,11},{10,... | collective-permute-start | bytes 147464 | tf_op jit(solution)/shard_map/ppermute | solution.py:466
  140.8 0.7 collective-permute-start.20
  141.5 0.9 collective-permute-done.18.refs_4_
  142.4 1.1 collective-permute-done.19.refs_5_
  143.5 1.0 collective-permute-done.20.refs_6_
  144.5 6.3 %all-to-all-done.4 = bf16[32,8,640]{2,1,0:T(8,128)(2,1)S(1)} async-done(((bf16[32,8,640]{2,1,0:T(8,128)(2,1)}), bf16[32,8,640]{2,1,0:T(8,128)(2,1)S(1)}, u32[]{:S(2)}, u32[]{:S(2)}) %all-to-all-start.4) | async-done | bytes 327712 | tf_op jit(solution)/shard_map/all_to_all | solution.py:488
  150.8 12.7 %last.3 = bf16[64,64,256]{2,1,0:T(8,128)(2,1)} custom-call(s32[1]{0:T(128)} %bitcast.me_ref.refs_0_, bf16[256,640]{1,0:T(8,128)(2,1)S(1)} %bitcast.26, bf16[16,128]{1,0:T(8,128)(2,1)S(1)} %copy-done.8, bf16[24,1024]{1,0:T(8,128)(2,1)S(1)} %get-tuple-element.68.refs_3_, bf16[24,1024]{1,0:T(8,128)(2,1)S(1)} %collective-permute-done.18.refs_4_, ...), custom_call_target="tpu_custom_call" | custom-call | flops 12000000000 | bytes 1048576 | tf_op jit(solution)/shard_map/last/pallas_call | solution.py:418
  (20 shorter events, 0.1 us)
Async XLA Ops:
  0.0 14.6 %copy-start.8 = (bf16[16,128]{1,0:T(8,128)(2,1)S(1)}, bf16[16,128]{1,0:T(8,128)(2,1)}, u32[]{:S(2)}) copy-start(bf16[16,128]{1,0:T(8,128)(2,1)} %constant.40.clone.bx_ref.refs_2_) | copy-start | bytes 12292
  0.0 14.6 %copy-start = (bf16[1,64,64,256]{3,2,1,0:T(8,128)(2,1)S(1)}, bf16[1,64,64,256]{3,2,1,0:T(8,128)(2,1)}, u32[]{:S(2)}) copy-start(bf16[1,64,64,256]{3,2,1,0:T(8,128)(2,1)} %param.9) | copy-start | bytes 6291460
  0.0 1.1 copy-start.1
  1.1 0.8 copy-start.2
  1.9 12.7 %copy-start.7 = (bf16[24,256]{1,0:T(8,128)(2,1)S(1)}, bf16[24,256]{1,0:T(8,128)(2,1)}, u32[]{:S(2)}) copy-start(bf16[24,256]{1,0:T(8,128)(2,1)} %constant.39.clone.cy_ref.refs_7_) | copy-start | bytes 36868
  2.9 27.0 %all-to-all-start.1 = ((bf16[16,2,64,128]{3,2,1,0:T(8,128)(2,1)}), bf16[16,2,64,128]{3,2,1,0:T(8,128)(2,1)S(1)}, u32[]{:S(2)}, u32[]{:S(2)}) async-start(bf16[16,2,64,128]{3,2,1,0:T(8,128)(2,1)} %get-tuple-element.43), calls=%async_computation.1 | async-start | bytes 1048576 | tf_op jit(solution)/shard_map/all_to_all | solution.py:475
  14.7 41.4 %copy-start.5 = (bf16[288,256]{1,0:T(8,128)(2,1)S(1)}, bf16[288,256]{1,0:T(8,128)(2,1)}, u32[]{:S(2)}) copy-start(bf16[288,256]{1,0:T(8,128)(2,1)} %constant.37.clone.tab_ref) | copy-start | bytes 442372
  20.8 1.3 copy-start.9
  29.9 26.2 %all-to-all-start = ((bf16[32,8,640]{2,1,0:T(8,128)(2,1)}), bf16[32,8,640]{2,1,0:T(8,128)(2,1)S(1)}, u32[]{:S(2)}, u32[]{:S(2)}) async-start(bf16[32,8,640]{2,1,0:T(8,128)(2,1)} %bitcast.7), calls=%async_computation | async-start | bytes 655360 | tf_op jit(solution)/shard_map/all_to_all | solution.py:481
  37.4 18.7 %collective-permute-start.7 = (bf16[16,2,64,128]{3,2,1,0:T(8,128)(2,1)S(1)}, bf16[16,2,64,128]{3,2,1,0:T(8,128)(2,1)S(1)}, u32[]{:S(2)}, u32[]{:S(2)}) collective-permute-start(bf16[16,2,64,128]{3,2,1,0:T(8,128)(2,1)S(1)} %all-to-all-done.1.w0_ref), channel_id=1, source_target_pairs={{0,8},{8,0},{16,24},{24,16},{32,40},{40,32},{48,56},{56,48},{64,72... | collective-permute-start | bytes 1572872 | tf_op jit(solution)/shard_map/ppermute | solution.py:462
  37.8 7.0 %collective-permute-start.4 = (bf16[56,1024]{1,0:T(8,128)(2,1)S(1)}, bf16[56,1024]{1,0:T(8,128)(2,1)S(1)}, u32[]{:S(2)}, u32[]{:S(2)}) collective-permute-start(bf16[56,1024]{1,0:T(8,128)(2,1)S(1)} %get-tuple-element.77), channel_id=1, source_target_pairs={{0,2},{1,3},{2,0},{3,1},{4,6},{5,7},{6,4},{7,5},{8,10},{9,11},{10,... | collective-permute-start | bytes 344072 | tf_op jit(solution)/shard_map/ppermute | solution.py:466
  40.6 7.1 %collective-permute-start.3 = (bf16[56,1024]{1,0:T(8,128)(2,1)S(1)}, bf16[56,1024]{1,0:T(8,128)(2,1)S(1)}, u32[]{:S(2)}, u32[]{:S(2)}) collective-permute-start(bf16[56,1024]{1,0:T(8,128)(2,1)S(1)} %get-tuple-element.77), channel_id=1, source_target_pairs={{0,6},{1,7},{2,4},{3,5},{4,2},{5,3},{6,0},{7,1},{8,14},{9,15},{10,... | collective-permute-start | bytes 344072 | tf_op jit(solution)/shard_map/ppermute | solution.py:466
  40.9 11.2 %collective-permute-start.6 = (bf16[56,1024]{1,0:T(8,128)(2,1)S(1)}, bf16[56,1024]{1,0:T(8,128)(2,1)S(1)}, u32[]{:S(2)}, u32[]{:S(2)}) collective-permute-start(bf16[56,1024]{1,0:T(8,128)(2,1)S(1)} %get-tuple-element.78), channel_id=1, source_target_pairs={{0,7},{1,4},{2,5},{3,6},{4,3},{5,0},{6,1},{7,2},{8,15},{9,12},{10,... | collective-permute-start | bytes 344072 | tf_op jit(solution)/shard_map/ppermute | solution.py:466
  44.2 9.4 %collective-permute-start.2 = (bf16[56,1024]{1,0:T(8,128)(2,1)S(1)}, bf16[56,1024]{1,0:T(8,128)(2,1)S(1)}, u32[]{:S(2)}, u32[]{:S(2)}) collective-permute-start(bf16[56,1024]{1,0:T(8,128)(2,1)S(1)} %get-tuple-element.78), channel_id=1, source_target_pairs={{0,3},{1,0},{2,1},{3,2},{4,7},{5,4},{6,5},{7,6},{8,11},{9,8},{10,9... | collective-permute-start | bytes 344072 | tf_op jit(solution)/shard_map/ppermute | solution.py:466
  44.7 8.8 %collective-permute-start.5 = (bf16[56,1024]{1,0:T(8,128)(2,1)S(1)}, bf16[56,1024]{1,0:T(8,128)(2,1)S(1)}, u32[]{:S(2)}, u32[]{:S(2)}) collective-permute-start(bf16[56,1024]{1,0:T(8,128)(2,1)S(1)} %get-tuple-element.79), channel_id=1, source_target_pairs={{0,5},{1,6},{2,7},{3,4},{4,1},{5,2},{6,3},{7,0},{8,13},{9,14},{10,... | collective-permute-start | bytes 344072 | tf_op jit(solution)/shard_map/ppermute | solution.py:466
  47.7 5.9 %collective-permute-start.1 = (bf16[56,1024]{1,0:T(8,128)(2,1)S(1)}, bf16[56,1024]{1,0:T(8,128)(2,1)S(1)}, u32[]{:S(2)}, u32[]{:S(2)}) collective-permute-start(bf16[56,1024]{1,0:T(8,128)(2,1)S(1)} %get-tuple-element.79), channel_id=1, source_target_pairs={{0,1},{1,2},{2,3},{3,0},{4,5},{5,6},{6,7},{7,4},{8,9},{9,10},{10,1... | collective-permute-start | bytes 344072 | tf_op jit(solution)/shard_map/ppermute | solution.py:466
  52.2 3.9 %collective-permute-start = (bf16[56,1024]{1,0:T(8,128)(2,1)S(1)}, bf16[56,1024]{1,0:T(8,128)(2,1)S(1)}, u32[]{:S(2)}, u32[]{:S(2)}) collective-permute-start(bf16[56,1024]{1,0:T(8,128)(2,1)S(1)} %get-tuple-element.44.refs_0_), channel_id=1, source_target_pairs={{0,4},{1,5},{2,6},{3,7},{4,0},{5,1},{6,2},{7,3},{8,12},{9,13},{10,... | collective-permute-start | bytes 344072 | tf_op jit(solution)/shard_map/ppermute | solution.py:466
  56.1 13.8 %copy-start.6 = (bf16[2,8,24,128]{3,2,1,0:T(8,128)(2,1)S(1)}, bf16[2,8,24,128]{3,2,1,0:T(8,128)(2,1)}, u32[]{:S(2)}) copy-start(bf16[2,8,24,128]{3,2,1,0:T(8,128)(2,1)} %constant.38.clone.refs_8_) | copy-start | bytes 294916
  58.9 25.4 %all-to-all-start.2 = ((bf16[32,8,640]{2,1,0:T(8,128)(2,1)}), bf16[32,8,640]{2,1,0:T(8,128)(2,1)S(1)}, u32[]{:S(2)}, u32[]{:S(2)}) async-start(bf16[32,8,640]{2,1,0:T(8,128)(2,1)} %mid_x.2), calls=%async_computation.2 | async-start | bytes 655360 | tf_op jit(solution)/shard_map/all_to_all | solution.py:488
  69.9 14.5 %copy-start.3 = (bf16[2,64,256]{2,1,0:T(8,128)(2,1)S(1)}, bf16[2,64,256]{2,1,0:T(8,128)(2,1)}, u32[]{:S(2)}) copy-start(bf16[2,64,256]{2,1,0:T(8,128)(2,1)} %refs_9_.3) | copy-start | bytes 196612
  69.9 14.5 %copy-start.4 = (bf16[2,256,64]{1,2,0:T(8,128)(2,1)S(1)}, bf16[2,256,64]{1,2,0:T(8,128)(2,1)}, u32[]{:S(2)}) copy-start(bf16[2,256,64]{1,2,0:T(8,128)(2,1)} %param.13) | copy-start | bytes 196612
  71.5 4.9 %collective-permute-start.8 = (bf16[24,1024]{1,0:T(8,128)(2,1)S(1)}, bf16[24,1024]{1,0:T(8,128)(2,1)S(1)}, u32[]{:S(2)}, u32[]{:S(2)}) collective-permute-start(bf16[24,1024]{1,0:T(8,128)(2,1)S(1)} %get-tuple-element.53), channel_id=1, source_target_pairs={{0,1},{1,2},{2,3},{3,0},{4,5},{5,6},{6,7},{7,4},{8,9},{9,10},{10,1... | collective-permute-start | bytes 147464 | tf_op jit(solution)/shard_map/ppermute | solution.py:466
  73.0 5.2 %collective-permute-start.9 = (bf16[24,1024]{1,0:T(8,128)(2,1)S(1)}, bf16[24,1024]{1,0:T(8,128)(2,1)S(1)}, u32[]{:S(2)}, u32[]{:S(2)}) collective-permute-start(bf16[24,1024]{1,0:T(8,128)(2,1)S(1)} %get-tuple-element.54), channel_id=1, source_target_pairs={{0,2},{1,3},{2,0},{3,1},{4,6},{5,7},{6,4},{7,5},{8,10},{9,11},{10,... | collective-permute-start | bytes 147464 | tf_op jit(solution)/shard_map/ppermute | solution.py:466
  75.3 3.2 %collective-permute-start.10 = (bf16[24,1024]{1,0:T(8,128)(2,1)S(1)}, bf16[24,1024]{1,0:T(8,128)(2,1)S(1)}, u32[]{:S(2)}, u32[]{:S(2)}) collective-permute-start(bf16[24,1024]{1,0:T(8,128)(2,1)S(1)} %get-tuple-element.55), channel_id=1, source_target_pairs={{0,3},{1,0},{2,1},{3,2},{4,7},{5,4},{6,5},{7,6},{8,11},{9,8},{10,9... | collective-permute-start | bytes 147464 | tf_op jit(solution)/shard_map/ppermute | solution.py:466
  98.7 1.3 copy-start.10
  100.0 24.3 %all-to-all-start.3 = ((bf16[32,8,640]{2,1,0:T(8,128)(2,1)}), bf16[32,8,640]{2,1,0:T(8,128)(2,1)S(1)}, u32[]{:S(2)}, u32[]{:S(2)}) async-start(bf16[32,8,640]{2,1,0:T(8,128)(2,1)} %bitcast.14), calls=%async_computation.3 | async-start | bytes 655360 | tf_op jit(solution)/shard_map/all_to_all | solution.py:481
  105.5 7.2 %collective-permute-start.15 = (bf16[56,1024]{1,0:T(8,128)(2,1)S(1)}, bf16[56,1024]{1,0:T(8,128)(2,1)S(1)}, u32[]{:S(2)}, u32[]{:S(2)}) collective-permute-start(bf16[56,1024]{1,0:T(8,128)(2,1)S(1)} %get-tuple-element.73), channel_id=1, source_target_pairs={{0,2},{1,3},{2,0},{3,1},{4,6},{5,7},{6,4},{7,5},{8,10},{9,11},{10,... | collective-permute-start | bytes 344072 | tf_op jit(solution)/shard_map/ppermute | solution.py:466
  108.2 7.4 %collective-permute-start.14 = (bf16[56,1024]{1,0:T(8,128)(2,1)S(1)}, bf16[56,1024]{1,0:T(8,128)(2,1)S(1)}, u32[]{:S(2)}, u32[]{:S(2)}) collective-permute-start(bf16[56,1024]{1,0:T(8,128)(2,1)S(1)} %get-tuple-element.73), channel_id=1, source_target_pairs={{0,6},{1,7},{2,4},{3,5},{4,2},{5,3},{6,0},{7,1},{8,14},{9,15},{10,... | collective-permute-start | bytes 344072 | tf_op jit(solution)/shard_map/ppermute | solution.py:466
  108.3 9.7 %collective-permute-start.17 = (bf16[56,1024]{1,0:T(8,128)(2,1)S(1)}, bf16[56,1024]{1,0:T(8,128)(2,1)S(1)}, u32[]{:S(2)}, u32[]{:S(2)}) collective-permute-start(bf16[56,1024]{1,0:T(8,128)(2,1)S(1)} %get-tuple-element.74), channel_id=1, source_target_pairs={{0,7},{1,4},{2,5},{3,6},{4,3},{5,0},{6,1},{7,2},{8,15},{9,12},{10,... | collective-permute-start | bytes 344072 | tf_op jit(solution)/shard_map/ppermute | solution.py:466
  111.9 9.0 %collective-permute-start.13 = (bf16[56,1024]{1,0:T(8,128)(2,1)S(1)}, bf16[56,1024]{1,0:T(8,128)(2,1)S(1)}, u32[]{:S(2)}, u32[]{:S(2)}) collective-permute-start(bf16[56,1024]{1,0:T(8,128)(2,1)S(1)} %get-tuple-element.74), channel_id=1, source_target_pairs={{0,3},{1,0},{2,1},{3,2},{4,7},{5,4},{6,5},{7,6},{8,11},{9,8},{10,9... | collective-permute-start | bytes 344072 | tf_op jit(solution)/shard_map/ppermute | solution.py:466
  112.4 8.5 %collective-permute-start.16 = (bf16[56,1024]{1,0:T(8,128)(2,1)S(1)}, bf16[56,1024]{1,0:T(8,128)(2,1)S(1)}, u32[]{:S(2)}, u32[]{:S(2)}) collective-permute-start(bf16[56,1024]{1,0:T(8,128)(2,1)S(1)} %get-tuple-element.75), channel_id=1, source_target_pairs={{0,5},{1,6},{2,7},{3,4},{4,1},{5,2},{6,3},{7,0},{8,13},{9,14},{10,... | collective-permute-start | bytes 344072 | tf_op jit(solution)/shard_map/ppermute | solution.py:466
  112.7 8.2 %collective-permute-start.12 = (bf16[56,1024]{1,0:T(8,128)(2,1)S(1)}, bf16[56,1024]{1,0:T(8,128)(2,1)S(1)}, u32[]{:S(2)}, u32[]{:S(2)}) collective-permute-start(bf16[56,1024]{1,0:T(8,128)(2,1)S(1)} %get-tuple-element.75), channel_id=1, source_target_pairs={{0,1},{1,2},{2,3},{3,0},{4,5},{5,6},{6,7},{7,4},{8,9},{9,10},{10,1... | collective-permute-start | bytes 344072 | tf_op jit(solution)/shard_map/ppermute | solution.py:466
  115.6 8.7 %collective-permute-start.11 = (bf16[56,1024]{1,0:T(8,128)(2,1)S(1)}, bf16[56,1024]{1,0:T(8,128)(2,1)S(1)}, u32[]{:S(2)}, u32[]{:S(2)}) collective-permute-start(bf16[56,1024]{1,0:T(8,128)(2,1)S(1)} %get-tuple-element.60.refs_0_), channel_id=1, source_target_pairs={{0,4},{1,5},{2,6},{3,7},{4,0},{5,1},{6,2},{7,3},{8,12},{9,13},{10,... | collective-permute-start | bytes 344072 | tf_op jit(solution)/shard_map/ppermute | solution.py:466
  127.1 23.7 %all-to-all-start.4 = ((bf16[32,8,640]{2,1,0:T(8,128)(2,1)}), bf16[32,8,640]{2,1,0:T(8,128)(2,1)S(1)}, u32[]{:S(2)}, u32[]{:S(2)}) async-start(bf16[32,8,640]{2,1,0:T(8,128)(2,1)} %mid_x.3), calls=%async_computation.4 | async-start | bytes 655360 | tf_op jit(solution)/shard_map/all_to_all | solution.py:488
  137.9 4.5 %collective-permute-start.18 = (bf16[24,1024]{1,0:T(8,128)(2,1)S(1)}, bf16[24,1024]{1,0:T(8,128)(2,1)S(1)}, u32[]{:S(2)}, u32[]{:S(2)}) collective-permute-start(bf16[24,1024]{1,0:T(8,128)(2,1)S(1)} %get-tuple-element.69), channel_id=1, source_target_pairs={{0,1},{1,2},{2,3},{3,0},{4,5},{5,6},{6,7},{7,4},{8,9},{9,10},{10,1... | collective-permute-start | bytes 147464 | tf_op jit(solution)/shard_map/ppermute | solution.py:466
  138.4 5.2 %collective-permute-start.19 = (bf16[24,1024]{1,0:T(8,128)(2,1)S(1)}, bf16[24,1024]{1,0:T(8,128)(2,1)S(1)}, u32[]{:S(2)}, u32[]{:S(2)}) collective-permute-start(bf16[24,1024]{1,0:T(8,128)(2,1)S(1)} %get-tuple-element.70), channel_id=1, source_target_pairs={{0,2},{1,3},{2,0},{3,1},{4,6},{5,7},{6,4},{7,5},{8,10},{9,11},{10,... | collective-permute-start | bytes 147464 | tf_op jit(solution)/shard_map/ppermute | solution.py:466
  140.8 3.8 %collective-permute-start.20 = (bf16[24,1024]{1,0:T(8,128)(2,1)S(1)}, bf16[24,1024]{1,0:T(8,128)(2,1)S(1)}, u32[]{:S(2)}, u32[]{:S(2)}) collective-permute-start(bf16[24,1024]{1,0:T(8,128)(2,1)S(1)} %get-tuple-element.71), channel_id=1, source_target_pairs={{0,3},{1,0},{2,1},{3,2},{4,7},{5,4},{6,5},{7,6},{8,11},{9,8},{10,9... | collective-permute-start | bytes 147464 | tf_op jit(solution)/shard_map/ppermute | solution.py:466

commit v3 on v2

--- a/solution.py
+++ b/solution.py
@@ -22,6 +22,8 @@
 ROWS = RYP + 32
 GROUP = 16
 WIDE = GROUP * CH
+LAST_GROUPS = (64, 16)
+EARLY = 5
 LINE = 8
 
 
@@ -43,7 +45,6 @@
 
 
 SHIFTS = ((1, 0), (0, 1), (0, 3), (1, 2), (0, 2), (1, 1), (1, 3))
-UNROLL = 4
 QUARTER = 16 * 64
 
 
@@ -100,14 +101,15 @@
 
 
 def fill_kron(bx_ref, kron_ref):
-    lanes = lax.broadcasted_iota(jnp.int32, (CH, WIDE), 1)
-    rows = lax.broadcasted_iota(jnp.int32, (CH, WIDE), 0)
+    wide = kron_ref.shape[1]
+    lanes = lax.broadcasted_iota(jnp.int32, (CH, wide), 1)
+    rows = lax.broadcasted_iota(jnp.int32, (CH, wide), 0)
     eye = (lanes % CH) == rows
-    x = lax.broadcasted_iota(jnp.int32, (128, WIDE), 1) // CH + GROUP * pl.program_id(0)
-    position = lax.broadcasted_iota(jnp.int32, (128, WIDE), 0)
+    x = (lax.broadcasted_iota(jnp.int32, (128, wide), 1) + wide * pl.program_id(0)) // CH
+    position = lax.broadcasted_iota(jnp.int32, (128, wide), 0)
     spread = dot(bx_ref[...], jnp.where(x == position, 1.0, 0.0).astype(BF16))
     for r in range(RX):
-        row = jnp.broadcast_to(spread[r : r + 1, :], (CH, WIDE))
+        row = jnp.broadcast_to(spread[r : r + 1, :], (CH, wide))
         kron_ref[r * CH : (r + 1) * CH, :] = jnp.where(eye, row, 0.0).astype(BF16)
 
 
@@ -122,8 +124,10 @@
     def _():
         acc_ref[...] += part
 
-    zy_ref[0, :RYP] = dot(cy_ref[...], state).astype(BF16)
-    zy_ref[0, RYP:] = wy_ref[0]
+    for q in range(zy_ref.shape[0]):
+        part = state[:, q * QUARTER : (q + 1) * QUARTER]
+        zy_ref[q, :RYP] = dot(cy_ref[...], part).astype(BF16)
+        zy_ref[q, RYP:] = wy_ref[0]
 
     @pl.when(g == pl.num_programs(0) - 1)
     def _():
@@ -182,7 +186,7 @@
     return jnp.concatenate([w * sign, pltpu.roll(w, 64, 1)], axis=0).astype(BF16)
 
 
-def mix(xs_ref, ms_ref, lines, steps, weights):
+def mix(xs_ref, ms_ref, lines, steps, unroll, weights):
     sign = jnp.where(half_mask(CH), 1.0, -1.0)
 
     def product(i, _):
@@ -190,7 +194,7 @@
             rows = pl.ds(pl.multiple_of(mode * lines, lines), lines)
             ms_ref[rows, :] = dot_nt(xs_ref[rows, :].astype(BF16), mode_weights(w, sign))
 
-    lax.fori_loop(0, steps, product, None, unroll=UNROLL)
+    lax.fori_loop(0, steps, product, None, unroll=unroll)
 
 
 def mid_x_kernel(
@@ -214,7 +218,7 @@
         xs_ref[pl.ds(y, MODES, stride=LINE), :] = x
     core = core_ref[0]
     weights = lambda t: [(t * 2 + core, w0_ref[t, 0]), (t * 2 + 1 - core, w1_ref[t, 0])]
-    mix(xs_ref, ms_ref, LINE, 16, weights)
+    mix(xs_ref, ms_ref, LINE, 16, 8, weights)
     cols = []
     for y in range(LINE):
         m = ms_ref[pl.ds(y, MODES, stride=LINE), :]
@@ -291,7 +295,7 @@
             tiles = [packed[j * 8 : (j + 1) * 8, t * 128 : (t + 1) * 128] for t in range(8)]
             w_ref[src, j] = jnp.concatenate(tiles, axis=0).astype(BF16)
     weights = lambda src: [(src * 4 + j, w_ref[src, j]) for j in range(4)]
-    mix(xs_ref, ms_ref, lines, 8, weights)
+    mix(xs_ref, ms_ref, lines, 8, 4, weights)
     for g in range(2):
         cols = []
         for b in range(4):
@@ -330,7 +334,7 @@
     return half + half * jnp.tanh(inner)
 
 
-def last_kernel(more, *refs):
+def last_kernel(more, group, *refs):
     me_ref, yx_ref, bx_ref = refs[:3]
     yy_refs = refs[3:7]
     cy_ref, state_ref, we_ref, wr_ref = refs[7:11]
@@ -352,12 +356,12 @@
 
     fill_kron(bx_ref, kron_ref)
     basis = cy_ref[...].astype(F32).T.astype(BF16)
-    yy = yy_ref[g]
-    for j in range(WIDE // 256):
+    for j in range(group // 4):
         lanes = slice(j * 256, (j + 1) * 256)
         if j % 2 == 0:
             both = slice(j * 256, (j + 2) * 256)
-            total = dot(yx_ref[...], kron_ref[:, both]) + dot(basis, yy[:, both])
+            yy = yy_ref[g * (group // 16) + j // 4, :, j % 4 * 256 : (j % 4 + 2) * 256]
+            total = dot(yx_ref[...], kron_ref[:, both]) + dot(basis, yy)
             total = total.astype(BF16)
             total = jnp.concatenate([total[:, :256], total[:, 256:]], axis=0)
             hidden = gelu(dot(total, we4_ref[...])).astype(BF16)
@@ -371,28 +375,30 @@
             for p in range(2):
                 block = new[h * 128 : (h + 1) * 128, p * 128 : (p + 1) * 128].T
                 x = j * 4 + p * 2
-                t_ref[h, pl.ds(x, CH, stride=GROUP), :] = block[:CH]
-                t_ref[h, pl.ds(x + 1, CH, stride=GROUP), :] = block[CH:]
+                t_ref[h, pl.ds(x, CH, stride=group), :] = block[:CH]
+                t_ref[h, pl.ds(x + 1, CH, stride=group), :] = block[CH:]
     if more:
         coefficients(g, out_ref[...], kron_ref, cy_ref, wy_ref, acc_ref, zx_ref, zy_ref)
     else:
         for h in range(2):
-            part = t_ref[h].reshape(CH, GROUP, 128).astype(BF16)
+            part = t_ref[h].reshape(CH, group, 128).astype(BF16)
             out_ref[:, :, h * 128 : (h + 1) * 128] = part
 
 
 def last_call(layer, more, me, yx, yy, state, we, wr, wy, c):
+    group = LAST_GROUPS[layer]
+    wide = group * CH
     in_specs = [
         pl.BlockSpec(memory_space=pltpu.SMEM),
         pl.BlockSpec((256, RX * CH), lambda g: (0, 0)),
         pl.BlockSpec((16, 128), lambda g: (0, 0)),
         *[pl.BlockSpec((RYP, QUARTER), lambda g: (0, 0))] * 4,
         pl.BlockSpec((RYP, 256), lambda g: (0, 0)),
-        pl.BlockSpec((256, WIDE), lambda g: (0, g)),
+        pl.BlockSpec((256, wide), lambda g: (0, g)),
         pl.BlockSpec((1, CH, HID), lambda g: (layer, 0, 0)),
         pl.BlockSpec((1, CH, HID), lambda g: (layer, 0, 0)),
     ]
-    scratch = [pltpu.VMEM((RX * CH, WIDE), BF16)] + [pltpu.VMEM((256, 1024), BF16)] * 2
+    scratch = [pltpu.VMEM((RX * CH, wide), BF16)] + [pltpu.VMEM((256, 1024), BF16)] * 2
     scratch.append(pltpu.VMEM((4, RYP, QUARTER), BF16))
     args = [me, yx, c["bx"], *yy, c["cy"], state, we, wr]
     if more:
@@ -401,9 +407,9 @@
         )
         args.append(wy)
         out_specs = [
-            pl.BlockSpec((256, WIDE), lambda g: (0, g)),
+            pl.BlockSpec((256, wide), lambda g: (0, g)),
             pl.BlockSpec((256, RX * CH), lambda g: (0, 0)),
-            pl.BlockSpec((1, ROWS, WIDE), lambda g: (g, 0, 0)),
+            pl.BlockSpec((group // 16, ROWS, QUARTER), lambda g: (g, 0, 0)),
         ]
         out_shape = [
             jax.ShapeDtypeStruct((256, 4096), BF16),
@@ -412,13 +418,13 @@
         ]
         scratch.append(pltpu.VMEM((256, RX * CH), F32))
     else:
-        out_specs = [pl.BlockSpec((CH, GROUP, 256), lambda g: (0, g, 0))]
+        out_specs = [pl.BlockSpec((CH, group, 256), lambda g: (0, g, 0))]
         out_shape = [jax.ShapeDtypeStruct((CH, 64, 256), BF16)]
-        scratch.append(pltpu.VMEM((2, CH * GROUP, 128), F32))
+        scratch.append(pltpu.VMEM((2, CH * group, 128), F32))
     return pl.pallas_call(
-        functools.partial(last_kernel, more),
+        functools.partial(last_kernel, more, group),
         name="last",
-        grid=(64 // GROUP,),
+        grid=(64 // group,),
         in_specs=in_specs,
         out_specs=out_specs,
         out_shape=out_shape,
@@ -478,11 +484,14 @@
     state, zx, zy = first_call(state_field[0], wy, c)
     for l in range(LAYERS):
         state = pltpu.with_memory_space_constraint(state, pltpu.HBM)
-        recv = lax.all_to_all(zx.reshape(32, LINE, RX * CH), "gx", 0, 0, tiled=True)
         zs = []
         for flip, step in ((0, 0),) + SHIFTS:
             chunk = lax.dynamic_slice_in_dim(zy, lax.rem(me[0] + step, 4), 1, 0)[0]
             zs.append(permute_y(chunk, flip, step) if flip or step else chunk)
+        if l == 0:
+            zx, early = lax.optimization_barrier((zx, zs[:EARLY]))
+            zs = early + zs[EARLY:]
+        recv = lax.all_to_all(zx.reshape(32, LINE, RX * CH), "gx", 0, 0, tiled=True)
         zs, recv = lax.optimization_barrier((zs, recv))
         send = mid_x(l, core, recv, mine, swapped, c)
         yx = lax.all_to_all(send, "gx", 0, 0, tiled=True).reshape(256, RX * CH)

time: 164 us -> 159 us (0.970)
  Pallas kernels: 42.8 us -> 39 us
    all_to_all x1, waiting for transfers between devices: 7.78 us -> 0.01 us  [body(): lax.all_to_all(own_x, 'gx', 0, 0, axis_index_groups=same_core, tiled=True)]
    all_to_all x2, waiting for transfers between devices: 0.01 us -> 5.18 us  [body(): recv = lax.all_to_all(zx.reshape(32, LINE, RX * CH), 'gx', 0, 0, tiled=True)]
    all_to_all x2, starting transfers between devices: 13 us -> 17.1 us  [body(): recv = lax.all_to_all(zx.reshape(32, LINE, RX * CH), 'gx', 0, 0, tiled=True)]
    all_to_all x2, starting transfers between devices: 20.2 us -> 16.2 us  [body(): yx = lax.all_to_all(send, 'gx', 0, 0, tiled=True).reshape(256, RX * CH)]
    pallas_call x2, Pallas kernels: 27 us -> 23.8 us  [last_call(): pl.pallas_call(functools.partial(last_kernel, more, group), name='last',...]
    ppermute x20, waiting for transfers between devices: 24.9 us -> 26.8 us  [permute_y(): return lax.ppermute(x, 'gy', [(i, moved(i, flip, step)) for i in range(8)])]
    ppermute x20, starting transfers between devices: 25.8 us -> 24 us  [permute_y(): return lax.ppermute(x, 'gy', [(i, moved(i, flip, step)) for i in range(8)])]
  transfers between devices with their start and end apart: 26 -> 26, of which waited for: 16 -> 20; matrix products, arithmetic and copies ran while one was open for 0% -> 0% of each run, Pallas kernels for 6% -> 6%
where the time goes in v3:
time: 159 us; the launch traced here: 158 us
  starting transfers between devices  69.4 us (44%)
  waiting for transfers between devices  44.9 us (28%)
  Pallas kernels  39 us (25%)
  local copies, waits for them, and re-layouts  4.7 us (3%)
    ppermute x20, waiting for transfers between devices, permute_y(): return lax.ppermute(x, 'gy', [(i, moved(i, flip, step)) for i in range(8)])  26.8 us
    ppermute x20, starting transfers between devices, permute_y(): return lax.ppermute(x, 'gy', [(i, moved(i, flip, step)) for i in range(8)])  24 us
    pallas_call x2, Pallas kernels, last_call(): pl.pallas_call(functools.partial(last_kernel, more, group), name='last',...  23.8 us
    all_to_all x2, starting transfers between devices, body(): recv = lax.all_to_all(zx.reshape(32, LINE, RX * CH), 'gx', 0, 0, tiled=True)  17.1 us
    all_to_all x2, starting transfers between devices, body(): yx = lax.all_to_all(send, 'gx', 0, 0, tiled=True).reshape(256, RX * CH)  16.2 us
    all_to_all x2, waiting for transfers between devices, body(): yx = lax.all_to_all(send, 'gx', 0, 0, tiled=True).reshape(256, RX * CH)  12.9 us
    all_to_all x1, starting transfers between devices, body(): lax.all_to_all(own_x, 'gx', 0, 0, axis_index_groups=same_core, tiled=True)  11.7 us
    pallas_call x1, Pallas kernels, first_call(): pl.pallas_call(first_kernel, name='first', grid=(64 // GROUP,), in_specs=...  6.17 us
  transfers between devices with their start and end apart: 26, of which 20 were waited for; matrix products, arithmetic and copies ran while one was open for 0% of the time, Pallas kernels for 6%

profile of v3, /device:TPU:1, one launch (start us, length us, event | category | flops | bytes accessed | tf_op | source)
XLA Modules:
  0.0 158.2 jit_solution(2284045026209620333)
XLA Ops:
  0.0 1.1 copy-done.1
  1.1 0.8 copy-done.2
  1.9 0.9 pack.1
  2.9 11.7 %all-to-all-start.1 = ((bf16[16,2,64,128]{3,2,1,0:T(8,128)(2,1)}), bf16[16,2,64,128]{3,2,1,0:T(8,128)(2,1)S(1)}, u32[]{:S(2)}, u32[]{:S(2)}) async-start(bf16[16,2,64,128]{3,2,1,0:T(8,128)(2,1)} %get-tuple-element.55), calls=%async_computation.1 | async-start | bytes 1048576 | tf_op jit(solution)/shard_map/all_to_all | solution.py:481
  14.7 0.0 copy-start.5
  14.7 6.2 %first.1 = (bf16[256,4096]{1,0:T(8,128)(2,1)S(1)}, bf16[256,640]{1,0:T(8,128)(2,1)}, bf16[4,56,1024]{2,1,0:T(8,128)(2,1)S(1)}) custom-call(bf16[64,64,256]{2,1,0:T(8,128)(2,1)S(1)} %bitcast.27, bf16[16,128]{1,0:T(8,128)(2,1)S(1)} %copy-done.8, bf16[24,256]{1,0:T(8,128)(2,1)S(1)} %copy-done.7, bf16[2,32,1024]{2,1,0:T(8,128)(2,1)S(1)} %get-tuple-element.45.wy_ref.refs_11_), custom_call_target="tpu_custom_call" | custom-call | flops 10000000000 | bytes 1048576 | tf_op jit(solution)/shard_map/first/pallas_call | solution.py:154
  20.9 1.3 copy-done.9
  22.2 2.9 %collective-permute-start.3 = (bf16[56,1024]{1,0:T(8,128)(2,1)S(1)}, bf16[56,1024]{1,0:T(8,128)(2,1)S(1)}, u32[]{:S(2)}, u32[]{:S(2)}) collective-permute-start(bf16[56,1024]{1,0:T(8,128)(2,1)S(1)} %get-tuple-element.89), channel_id=1, source_target_pairs={{0,6},{1,7},{2,4},{3,5},{4,2},{5,3},{6,0},{7,1},{8,14},{9,15},{10,... | collective-permute-start | bytes 344072 | tf_op jit(solution)/shard_map/ppermute | solution.py:472
  25.2 0.9 collective-permute-start.2
  26.0 0.6 collective-permute-start.1
  26.6 1.1 collective-permute-start
  27.7 1.0 collective-permute-done.3.refs_4_
  28.7 1.4 collective-permute-done.2.refs_3_
  30.2 1.1 collective-permute-done.1.refs_2_
  31.3 0.8 collective-permute-done.refs_1_
  32.0 0.0 all-to-all-done.1.w0_ref
  32.0 11.8 %all-to-all-start = ((bf16[32,8,640]{2,1,0:T(8,128)(2,1)}), bf16[32,8,640]{2,1,0:T(8,128)(2,1)S(1)}, u32[]{:S(2)}, u32[]{:S(2)}) async-start(bf16[32,8,640]{2,1,0:T(8,128)(2,1)} %bitcast.7), calls=%async_computation | async-start | bytes 655360 | tf_op jit(solution)/shard_map/all_to_all | solution.py:494
  43.8 0.3 collective-permute-start.7
  44.1 1.1 collective-permute-start.4
  45.3 0.9 collective-permute-start.6
  46.2 1.4 collective-permute-start.5
  47.6 2.5 %collective-permute-done.4.refs_5_ = bf16[56,1024]{1,0:T(8,128)(2,1)S(1)} collective-permute-done((bf16[56,1024]{1,0:T(8,128)(2,1)S(1)}, bf16[56,1024]{1,0:T(8,128)(2,1)S(1)}, u32[]{:S(2)}, u32[]{:S(2)}) %collective-permute-start.4) | collective-permute-done | bytes 114720 | tf_op jit(solution)/shard_map/ppermute | solution.py:472
  50.1 2.1 %collective-permute-done.6.refs_7_ = bf16[56,1024]{1,0:T(8,128)(2,1)S(1)} collective-permute-done((bf16[56,1024]{1,0:T(8,128)(2,1)S(1)}, bf16[56,1024]{1,0:T(8,128)(2,1)S(1)}, u32[]{:S(2)}, u32[]{:S(2)}) %collective-permute-start.6) | collective-permute-done | bytes 114720 | tf_op jit(solution)/shard_map/ppermute | solution.py:472
  52.2 1.7 %collective-permute-done.5.refs_6_ = bf16[56,1024]{1,0:T(8,128)(2,1)S(1)} collective-permute-done((bf16[56,1024]{1,0:T(8,128)(2,1)S(1)}, bf16[56,1024]{1,0:T(8,128)(2,1)S(1)}, u32[]{:S(2)}, u32[]{:S(2)}) %collective-permute-start.5) | collective-permute-done | bytes 114720 | tf_op jit(solution)/shard_map/ppermute | solution.py:472
  54.0 5.2 %all-to-all-done.recv_ref = bf16[32,8,640]{2,1,0:T(8,128)(2,1)S(1)} async-done(((bf16[32,8,640]{2,1,0:T(8,128)(2,1)}), bf16[32,8,640]{2,1,0:T(8,128)(2,1)S(1)}, u32[]{:S(2)}, u32[]{:S(2)}) %all-to-all-start) | async-done | bytes 327712 | tf_op jit(solution)/shard_map/all_to_all | solution.py:494
  59.1 0.0 collective-permute-done.7.w1_ref
  59.1 2.5 %mid_x.2 = bf16[32,8,640]{2,1,0:T(8,128)(2,1)} custom-call(s32[1]{0:T(128)} %bitcast.1.core_ref, bf16[32,8,640]{2,1,0:T(8,128)(2,1)S(1)} %all-to-all-done.recv_ref, bf16[16,2,64,128]{3,2,1,0:T(8,128)(2,1)S(1)} %all-to-all-done.1.w0_ref, bf16[16,2,64,128]{3,2,1,0:T(8,128)(2,1)S(1)} %collective-permute-done.7.w1_ref, bf16[288,256]{1,0:T(8,128)(2,1)S(1)} %copy-done.5), custom_call_target="tpu_custom_call" | custom-call | flops 3000000000 | bytes 1048576 | tf_op jit(solution)/shard_map/mid_x/pallas_call | solution.py:245
  61.6 6.9 %all-to-all-start.2 = ((bf16[32,8,640]{2,1,0:T(8,128)(2,1)}), bf16[32,8,640]{2,1,0:T(8,128)(2,1)S(1)}, u32[]{:S(2)}, u32[]{:S(2)}) async-start(bf16[32,8,640]{2,1,0:T(8,128)(2,1)} %mid_x.2), calls=%async_computation.2 | async-start | bytes 655360 | tf_op jit(solution)/shard_map/all_to_all | solution.py:497
  68.5 0.0 copy-start.3
  68.5 0.0 copy-start.4
  68.5 1.6 mid_y.2
  70.1 0.4 collective-permute-start.8
  70.5 2.4 %collective-permute-start.9 = (bf16[24,1024]{1,0:T(8,128)(2,1)S(1)}, bf16[24,1024]{1,0:T(8,128)(2,1)S(1)}, u32[]{:S(2)}, u32[]{:S(2)}) collective-permute-start(bf16[24,1024]{1,0:T(8,128)(2,1)S(1)} %get-tuple-element.66), channel_id=1, source_target_pairs={{0,2},{1,3},{2,0},{3,1},{4,6},{5,7},{6,4},{7,5},{8,10},{9,11},{10,... | collective-permute-start | bytes 147464 | tf_op jit(solution)/shard_map/ppermute | solution.py:472
  72.8 0.8 collective-permute-start.10
  73.6 1.0 collective-permute-done.8.refs_4_
  74.6 1.0 collective-permute-done.9.refs_5_
  75.6 0.9 collective-permute-done.10.refs_6_
  76.5 6.4 %all-to-all-done.2 = bf16[32,8,640]{2,1,0:T(8,128)(2,1)S(1)} async-done(((bf16[32,8,640]{2,1,0:T(8,128)(2,1)}), bf16[32,8,640]{2,1,0:T(8,128)(2,1)S(1)}, u32[]{:S(2)}, u32[]{:S(2)}) %all-to-all-start.2) | async-done | bytes 327712 | tf_op jit(solution)/shard_map/all_to_all | solution.py:497
  82.9 11.1 %last.2 = (bf16[256,4096]{1,0:T(8,128)(2,1)S(1)}, bf16[256,640]{1,0:T(8,128)(2,1)}, bf16[4,56,1024]{2,1,0:T(8,128)(2,1)S(1)}) custom-call(s32[1]{0:T(128)} %bitcast.me_ref.refs_0_, bf16[256,640]{1,0:T(8,128)(2,1)S(1)} %bitcast.25, bf16[16,128]{1,0:T(8,128)(2,1)S(1)} %copy-done.8, bf16[24,1024]{1,0:T(8,128)(2,1)S(1)} %get-tuple-element.64.refs_3_, ...), custom_call_target="tpu_custom_call" | custom-call | flops 12000000000 | bytes 1048576 | tf_op jit(solution)/shard_map/last/pallas_call | solution.py:424
  94.1 1.3 copy-done.10
  95.4 5.3 %all-to-all-start.3 = ((bf16[32,8,640]{2,1,0:T(8,128)(2,1)}), bf16[32,8,640]{2,1,0:T(8,128)(2,1)S(1)}, u32[]{:S(2)}, u32[]{:S(2)}) async-start(bf16[32,8,640]{2,1,0:T(8,128)(2,1)} %bitcast.14), calls=%async_computation.3 | async-start | bytes 655360 | tf_op jit(solution)/shard_map/all_to_all | solution.py:494
  100.8 1.5 collective-permute-start.15
  102.3 1.7 %collective-permute-start.14 = (bf16[56,1024]{1,0:T(8,128)(2,1)S(1)}, bf16[56,1024]{1,0:T(8,128)(2,1)S(1)}, u32[]{:S(2)}, u32[]{:S(2)}) collective-permute-start(bf16[56,1024]{1,0:T(8,128)(2,1)S(1)} %get-tuple-element.85), channel_id=1, source_target_pairs={{0,6},{1,7},{2,4},{3,5},{4,2},{5,3},{6,0},{7,1},{8,14},{9,15},{10,... | collective-permute-start | bytes 344072 | tf_op jit(solution)/shard_map/ppermute | solution.py:472
  104.0 2.3 %collective-permute-start.17 = (bf16[56,1024]{1,0:T(8,128)(2,1)S(1)}, bf16[56,1024]{1,0:T(8,128)(2,1)S(1)}, u32[]{:S(2)}, u32[]{:S(2)}) collective-permute-start(bf16[56,1024]{1,0:T(8,128)(2,1)S(1)} %get-tuple-element.86), channel_id=1, source_target_pairs={{0,7},{1,4},{2,5},{3,6},{4,3},{5,0},{6,1},{7,2},{8,15},{9,12},{10,... | collective-permute-start | bytes 344072 | tf_op jit(solution)/shard_map/ppermute | solution.py:472
  106.3 0.2 collective-permute-start.13
  106.4 1.4 collective-permute-start.16
  107.8 2.3 %collective-permute-done.14.refs_4_ = bf16[56,1024]{1,0:T(8,128)(2,1)S(1)} collective-permute-done((bf16[56,1024]{1,0:T(8,128)(2,1)S(1)}, bf16[56,1024]{1,0:T(8,128)(2,1)S(1)}, u32[]{:S(2)}, u32[]{:S(2)}) %collective-permute-start.14) | collective-permute-done | bytes 114720 | tf_op jit(solution)/shard_map/ppermute | solution.py:472
  110.1 1.1 collective-permute-start.11
  111.2 3.3 %collective-permute-done.17.refs_7_ = bf16[56,1024]{1,0:T(8,128)(2,1)S(1)} collective-permute-done((bf16[56,1024]{1,0:T(8,128)(2,1)S(1)}, bf16[56,1024]{1,0:T(8,128)(2,1)S(1)}, u32[]{:S(2)}, u32[]{:S(2)}) %collective-permute-start.17) | collective-permute-done | bytes 114720 | tf_op jit(solution)/shard_map/ppermute | solution.py:472
  114.5 1.3 collective-permute-done.13.refs_3_
  115.8 0.0 collective-permute-done.12.refs_2_
  115.8 3.3 %collective-permute-done.11.refs_1_ = bf16[56,1024]{1,0:T(8,128)(2,1)S(1)} collective-permute-done((bf16[56,1024]{1,0:T(8,128)(2,1)S(1)}, bf16[56,1024]{1,0:T(8,128)(2,1)S(1)}, u32[]{:S(2)}, u32[]{:S(2)}) %collective-permute-start.11) | collective-permute-done | bytes 114720 | tf_op jit(solution)/shard_map/ppermute | solution.py:472
  119.2 0.0 all-to-all-done.3.recv_ref
  119.2 2.5 %mid_x.3 = bf16[32,8,640]{2,1,0:T(8,128)(2,1)} custom-call(s32[1]{0:T(128)} %bitcast.1.core_ref, bf16[32,8,640]{2,1,0:T(8,128)(2,1)S(1)} %all-to-all-done.3.recv_ref, bf16[16,2,64,128]{3,2,1,0:T(8,128)(2,1)S(1)} %all-to-all-done.1.w0_ref, bf16[16,2,64,128]{3,2,1,0:T(8,128)(2,1)S(1)} %collective-permute-done.7.w1_ref, bf16[288,256]{1,0:T(8,128)(2,1)S(1)} %copy-done.5), custom_call_target="tpu_custom_call" | custom-call | flops 3000000000 | bytes 1048576 | tf_op jit(solution)/shard_map/mid_x/pallas_call | solution.py:245
  121.6 9.4 %all-to-all-start.4 = ((bf16[32,8,640]{2,1,0:T(8,128)(2,1)}), bf16[32,8,640]{2,1,0:T(8,128)(2,1)S(1)}, u32[]{:S(2)}, u32[]{:S(2)}) async-start(bf16[32,8,640]{2,1,0:T(8,128)(2,1)} %mid_x.3), calls=%async_computation.4 | async-start | bytes 655360 | tf_op jit(solution)/shard_map/all_to_all | solution.py:497
  131.0 1.6 mid_y.3
  132.6 0.4 collective-permute-start.18
  132.9 2.4 %collective-permute-start.19 = (bf16[24,1024]{1,0:T(8,128)(2,1)S(1)}, bf16[24,1024]{1,0:T(8,128)(2,1)S(1)}, u32[]{:S(2)}, u32[]{:S(2)}) collective-permute-start(bf16[24,1024]{1,0:T(8,128)(2,1)S(1)} %get-tuple-element.82), channel_id=1, source_target_pairs={{0,2},{1,3},{2,0},{3,1},{4,6},{5,7},{6,4},{7,5},{8,10},{9,11},{10,... | collective-permute-start | bytes 147464 | tf_op jit(solution)/shard_map/ppermute | solution.py:472
  135.3 0.7 collective-permute-start.20
  136.0 1.1 collective-permute-done.18.refs_4_
  137.1 1.0 collective-permute-done.19.refs_5_
  138.1 0.9 collective-permute-done.20.refs_6_
  139.0 6.5 %all-to-all-done.4 = bf16[32,8,640]{2,1,0:T(8,128)(2,1)S(1)} async-done(((bf16[32,8,640]{2,1,0:T(8,128)(2,1)}), bf16[32,8,640]{2,1,0:T(8,128)(2,1)S(1)}, u32[]{:S(2)}, u32[]{:S(2)}) %all-to-all-start.4) | async-done | bytes 327712 | tf_op jit(solution)/shard_map/all_to_all | solution.py:497
  145.4 12.7 %last.3 = bf16[64,64,256]{2,1,0:T(8,128)(2,1)} custom-call(s32[1]{0:T(128)} %bitcast.me_ref.refs_0_, bf16[256,640]{1,0:T(8,128)(2,1)S(1)} %bitcast.26, bf16[16,128]{1,0:T(8,128)(2,1)S(1)} %copy-done.8, bf16[24,1024]{1,0:T(8,128)(2,1)S(1)} %get-tuple-element.80.refs_3_, bf16[24,1024]{1,0:T(8,128)(2,1)S(1)} %collective-permute-done.18.refs_4_, ...), custom_call_target="tpu_custom_call" | custom-call | flops 12000000000 | bytes 1048576 | tf_op jit(solution)/shard_map/last/pallas_call | solution.py:424
  (20 shorter events, 0.1 us)
Async XLA Ops:
  0.0 14.7 %copy-start.8 = (bf16[16,128]{1,0:T(8,128)(2,1)S(1)}, bf16[16,128]{1,0:T(8,128)(2,1)}, u32[]{:S(2)}) copy-start(bf16[16,128]{1,0:T(8,128)(2,1)} %constant.40.clone.bx_ref.refs_2_) | copy-start | bytes 12292
  0.0 14.7 %copy-start = (bf16[1,64,64,256]{3,2,1,0:T(8,128)(2,1)S(1)}, bf16[1,64,64,256]{3,2,1,0:T(8,128)(2,1)}, u32[]{:S(2)}) copy-start(bf16[1,64,64,256]{3,2,1,0:T(8,128)(2,1)} %param.9) | copy-start | bytes 6291460
  0.0 1.1 copy-start.1
  1.1 0.8 copy-start.2
  1.9 12.7 %copy-start.7 = (bf16[24,256]{1,0:T(8,128)(2,1)S(1)}, bf16[24,256]{1,0:T(8,128)(2,1)}, u32[]{:S(2)}) copy-start(bf16[24,256]{1,0:T(8,128)(2,1)} %constant.39.clone.cy_ref.refs_7_) | copy-start | bytes 36868
  2.9 29.2 %all-to-all-start.1 = ((bf16[16,2,64,128]{3,2,1,0:T(8,128)(2,1)}), bf16[16,2,64,128]{3,2,1,0:T(8,128)(2,1)S(1)}, u32[]{:S(2)}, u32[]{:S(2)}) async-start(bf16[16,2,64,128]{3,2,1,0:T(8,128)(2,1)} %get-tuple-element.55), calls=%async_computation.1 | async-start | bytes 1048576 | tf_op jit(solution)/shard_map/all_to_all | solution.py:481
  14.7 44.4 %copy-start.5 = (bf16[288,256]{1,0:T(8,128)(2,1)S(1)}, bf16[288,256]{1,0:T(8,128)(2,1)}, u32[]{:S(2)}) copy-start(bf16[288,256]{1,0:T(8,128)(2,1)} %constant.37.clone.tab_ref) | copy-start | bytes 442372
  20.9 1.3 copy-start.9
  22.2 6.5 %collective-permute-start.3 = (bf16[56,1024]{1,0:T(8,128)(2,1)S(1)}, bf16[56,1024]{1,0:T(8,128)(2,1)S(1)}, u32[]{:S(2)}, u32[]{:S(2)}) collective-permute-start(bf16[56,1024]{1,0:T(8,128)(2,1)S(1)} %get-tuple-element.89), channel_id=1, source_target_pairs={{0,6},{1,7},{2,4},{3,5},{4,2},{5,3},{6,0},{7,1},{8,14},{9,15},{10,... | collective-permute-start | bytes 344072 | tf_op jit(solution)/shard_map/ppermute | solution.py:472
  25.2 5.0 %collective-permute-start.2 = (bf16[56,1024]{1,0:T(8,128)(2,1)S(1)}, bf16[56,1024]{1,0:T(8,128)(2,1)S(1)}, u32[]{:S(2)}, u32[]{:S(2)}) collective-permute-start(bf16[56,1024]{1,0:T(8,128)(2,1)S(1)} %get-tuple-element.90), channel_id=1, source_target_pairs={{0,3},{1,0},{2,1},{3,2},{4,7},{5,4},{6,5},{7,6},{8,11},{9,8},{10,9... | collective-permute-start | bytes 344072 | tf_op jit(solution)/shard_map/ppermute | solution.py:472
  26.0 5.2 %collective-permute-start.1 = (bf16[56,1024]{1,0:T(8,128)(2,1)S(1)}, bf16[56,1024]{1,0:T(8,128)(2,1)S(1)}, u32[]{:S(2)}, u32[]{:S(2)}) collective-permute-start(bf16[56,1024]{1,0:T(8,128)(2,1)S(1)} %get-tuple-element.91), channel_id=1, source_target_pairs={{0,1},{1,2},{2,3},{3,0},{4,5},{5,6},{6,7},{7,4},{8,9},{9,10},{10,1... | collective-permute-start | bytes 344072 | tf_op jit(solution)/shard_map/ppermute | solution.py:472
  26.6 5.4 %collective-permute-start = (bf16[56,1024]{1,0:T(8,128)(2,1)S(1)}, bf16[56,1024]{1,0:T(8,128)(2,1)S(1)}, u32[]{:S(2)}, u32[]{:S(2)}) collective-permute-start(bf16[56,1024]{1,0:T(8,128)(2,1)S(1)} %get-tuple-element.56.refs_0_), channel_id=1, source_target_pairs={{0,4},{1,5},{2,6},{3,7},{4,0},{5,1},{6,2},{7,3},{8,12},{9,13},{10,... | collective-permute-start | bytes 344072 | tf_op jit(solution)/shard_map/ppermute | solution.py:472
  32.0 27.1 %all-to-all-start = ((bf16[32,8,640]{2,1,0:T(8,128)(2,1)}), bf16[32,8,640]{2,1,0:T(8,128)(2,1)S(1)}, u32[]{:S(2)}, u32[]{:S(2)}) async-start(bf16[32,8,640]{2,1,0:T(8,128)(2,1)} %bitcast.7), calls=%async_computation | async-start | bytes 655360 | tf_op jit(solution)/shard_map/all_to_all | solution.py:494
  43.8 15.3 %collective-permute-start.7 = (bf16[16,2,64,128]{3,2,1,0:T(8,128)(2,1)S(1)}, bf16[16,2,64,128]{3,2,1,0:T(8,128)(2,1)S(1)}, u32[]{:S(2)}, u32[]{:S(2)}) collective-permute-start(bf16[16,2,64,128]{3,2,1,0:T(8,128)(2,1)S(1)} %all-to-all-done.1.w0_ref), channel_id=1, source_target_pairs={{0,8},{8,0},{16,24},{24,16},{32,40},{40,32},{48,56},{56,48},{64,72... | collective-permute-start | bytes 1572872 | tf_op jit(solution)/shard_map/ppermute | solution.py:468
  44.1 6.0 %collective-permute-start.4 = (bf16[56,1024]{1,0:T(8,128)(2,1)S(1)}, bf16[56,1024]{1,0:T(8,128)(2,1)S(1)}, u32[]{:S(2)}, u32[]{:S(2)}) collective-permute-start(bf16[56,1024]{1,0:T(8,128)(2,1)S(1)} %get-tuple-element.89), channel_id=1, source_target_pairs={{0,2},{1,3},{2,0},{3,1},{4,6},{5,7},{6,4},{7,5},{8,10},{9,11},{10,... | collective-permute-start | bytes 344072 | tf_op jit(solution)/shard_map/ppermute | solution.py:472
  45.3 6.9 %collective-permute-start.6 = (bf16[56,1024]{1,0:T(8,128)(2,1)S(1)}, bf16[56,1024]{1,0:T(8,128)(2,1)S(1)}, u32[]{:S(2)}, u32[]{:S(2)}) collective-permute-start(bf16[56,1024]{1,0:T(8,128)(2,1)S(1)} %get-tuple-element.90), channel_id=1, source_target_pairs={{0,7},{1,4},{2,5},{3,6},{4,3},{5,0},{6,1},{7,2},{8,15},{9,12},{10,... | collective-permute-start | bytes 344072 | tf_op jit(solution)/shard_map/ppermute | solution.py:472
  46.2 7.7 %collective-permute-start.5 = (bf16[56,1024]{1,0:T(8,128)(2,1)S(1)}, bf16[56,1024]{1,0:T(8,128)(2,1)S(1)}, u32[]{:S(2)}, u32[]{:S(2)}) collective-permute-start(bf16[56,1024]{1,0:T(8,128)(2,1)S(1)} %get-tuple-element.91), channel_id=1, source_target_pairs={{0,5},{1,6},{2,7},{3,4},{4,1},{5,2},{6,3},{7,0},{8,13},{9,14},{10,... | collective-permute-start | bytes 344072 | tf_op jit(solution)/shard_map/ppermute | solution.py:472
  59.1 9.3 %copy-start.6 = (bf16[2,8,24,128]{3,2,1,0:T(8,128)(2,1)S(1)}, bf16[2,8,24,128]{3,2,1,0:T(8,128)(2,1)}, u32[]{:S(2)}) copy-start(bf16[2,8,24,128]{3,2,1,0:T(8,128)(2,1)} %constant.38.clone.refs_8_) | copy-start | bytes 294916
  61.6 21.3 %all-to-all-start.2 = ((bf16[32,8,640]{2,1,0:T(8,128)(2,1)}), bf16[32,8,640]{2,1,0:T(8,128)(2,1)S(1)}, u32[]{:S(2)}, u32[]{:S(2)}) async-start(bf16[32,8,640]{2,1,0:T(8,128)(2,1)} %mid_x.2), calls=%async_computation.2 | async-start | bytes 655360 | tf_op jit(solution)/shard_map/all_to_all | solution.py:497
  68.5 14.5 %copy-start.3 = (bf16[2,64,256]{2,1,0:T(8,128)(2,1)S(1)}, bf16[2,64,256]{2,1,0:T(8,128)(2,1)}, u32[]{:S(2)}) copy-start(bf16[2,64,256]{2,1,0:T(8,128)(2,1)} %refs_9_.3) | copy-start | bytes 196612
  68.5 14.5 %copy-start.4 = (bf16[2,256,64]{1,2,0:T(8,128)(2,1)S(1)}, bf16[2,256,64]{1,2,0:T(8,128)(2,1)}, u32[]{:S(2)}) copy-start(bf16[2,256,64]{1,2,0:T(8,128)(2,1)} %param.13) | copy-start | bytes 196612
  70.1 4.5 %collective-permute-start.8 = (bf16[24,1024]{1,0:T(8,128)(2,1)S(1)}, bf16[24,1024]{1,0:T(8,128)(2,1)S(1)}, u32[]{:S(2)}, u32[]{:S(2)}) collective-permute-start(bf16[24,1024]{1,0:T(8,128)(2,1)S(1)} %get-tuple-element.65), channel_id=1, source_target_pairs={{0,1},{1,2},{2,3},{3,0},{4,5},{5,6},{6,7},{7,4},{8,9},{9,10},{10,1... | collective-permute-start | bytes 147464 | tf_op jit(solution)/shard_map/ppermute | solution.py:472
  70.5 5.2 %collective-permute-start.9 = (bf16[24,1024]{1,0:T(8,128)(2,1)S(1)}, bf16[24,1024]{1,0:T(8,128)(2,1)S(1)}, u32[]{:S(2)}, u32[]{:S(2)}) collective-permute-start(bf16[24,1024]{1,0:T(8,128)(2,1)S(1)} %get-tuple-element.66), channel_id=1, source_target_pairs={{0,2},{1,3},{2,0},{3,1},{4,6},{5,7},{6,4},{7,5},{8,10},{9,11},{10,... | collective-permute-start | bytes 147464 | tf_op jit(solution)/shard_map/ppermute | solution.py:472
  72.8 3.7 %collective-permute-start.10 = (bf16[24,1024]{1,0:T(8,128)(2,1)S(1)}, bf16[24,1024]{1,0:T(8,128)(2,1)S(1)}, u32[]{:S(2)}, u32[]{:S(2)}) collective-permute-start(bf16[24,1024]{1,0:T(8,128)(2,1)S(1)} %get-tuple-element.67), channel_id=1, source_target_pairs={{0,3},{1,0},{2,1},{3,2},{4,7},{5,4},{6,5},{7,6},{8,11},{9,8},{10,9... | collective-permute-start | bytes 147464 | tf_op jit(solution)/shard_map/ppermute | solution.py:472
  94.1 1.3 copy-start.10
  95.4 23.8 %all-to-all-start.3 = ((bf16[32,8,640]{2,1,0:T(8,128)(2,1)}), bf16[32,8,640]{2,1,0:T(8,128)(2,1)S(1)}, u32[]{:S(2)}, u32[]{:S(2)}) async-start(bf16[32,8,640]{2,1,0:T(8,128)(2,1)} %bitcast.14), calls=%async_computation.3 | async-start | bytes 655360 | tf_op jit(solution)/shard_map/all_to_all | solution.py:494
  100.8 7.0 %collective-permute-start.15 = (bf16[56,1024]{1,0:T(8,128)(2,1)S(1)}, bf16[56,1024]{1,0:T(8,128)(2,1)S(1)}, u32[]{:S(2)}, u32[]{:S(2)}) collective-permute-start(bf16[56,1024]{1,0:T(8,128)(2,1)S(1)} %get-tuple-element.85), channel_id=1, source_target_pairs={{0,2},{1,3},{2,0},{3,1},{4,6},{5,7},{6,4},{7,5},{8,10},{9,11},{10,... | collective-permute-start | bytes 344072 | tf_op jit(solution)/shard_map/ppermute | solution.py:472
  102.3 7.8 %collective-permute-start.14 = (bf16[56,1024]{1,0:T(8,128)(2,1)S(1)}, bf16[56,1024]{1,0:T(8,128)(2,1)S(1)}, u32[]{:S(2)}, u32[]{:S(2)}) collective-permute-start(bf16[56,1024]{1,0:T(8,128)(2,1)S(1)} %get-tuple-element.85), channel_id=1, source_target_pairs={{0,6},{1,7},{2,4},{3,5},{4,2},{5,3},{6,0},{7,1},{8,14},{9,15},{10,... | collective-permute-start | bytes 344072 | tf_op jit(solution)/shard_map/ppermute | solution.py:472
  104.0 10.5 %collective-permute-start.17 = (bf16[56,1024]{1,0:T(8,128)(2,1)S(1)}, bf16[56,1024]{1,0:T(8,128)(2,1)S(1)}, u32[]{:S(2)}, u32[]{:S(2)}) collective-permute-start(bf16[56,1024]{1,0:T(8,128)(2,1)S(1)} %get-tuple-element.86), channel_id=1, source_target_pairs={{0,7},{1,4},{2,5},{3,6},{4,3},{5,0},{6,1},{7,2},{8,15},{9,12},{10,... | collective-permute-start | bytes 344072 | tf_op jit(solution)/shard_map/ppermute | solution.py:472
  106.3 9.5 %collective-permute-start.13 = (bf16[56,1024]{1,0:T(8,128)(2,1)S(1)}, bf16[56,1024]{1,0:T(8,128)(2,1)S(1)}, u32[]{:S(2)}, u32[]{:S(2)}) collective-permute-start(bf16[56,1024]{1,0:T(8,128)(2,1)S(1)} %get-tuple-element.86), channel_id=1, source_target_pairs={{0,3},{1,0},{2,1},{3,2},{4,7},{5,4},{6,5},{7,6},{8,11},{9,8},{10,9... | collective-permute-start | bytes 344072 | tf_op jit(solution)/shard_map/ppermute | solution.py:472
  106.4 9.4 %collective-permute-start.16 = (bf16[56,1024]{1,0:T(8,128)(2,1)S(1)}, bf16[56,1024]{1,0:T(8,128)(2,1)S(1)}, u32[]{:S(2)}, u32[]{:S(2)}) collective-permute-start(bf16[56,1024]{1,0:T(8,128)(2,1)S(1)} %get-tuple-element.87), channel_id=1, source_target_pairs={{0,5},{1,6},{2,7},{3,4},{4,1},{5,2},{6,3},{7,0},{8,13},{9,14},{10,... | collective-permute-start | bytes 344072 | tf_op jit(solution)/shard_map/ppermute | solution.py:472
  107.8 8.0 %collective-permute-start.12 = (bf16[56,1024]{1,0:T(8,128)(2,1)S(1)}, bf16[56,1024]{1,0:T(8,128)(2,1)S(1)}, u32[]{:S(2)}, u32[]{:S(2)}) collective-permute-start(bf16[56,1024]{1,0:T(8,128)(2,1)S(1)} %get-tuple-element.87), channel_id=1, source_target_pairs={{0,1},{1,2},{2,3},{3,0},{4,5},{5,6},{6,7},{7,4},{8,9},{9,10},{10,1... | collective-permute-start | bytes 344072 | tf_op jit(solution)/shard_map/ppermute | solution.py:472
  110.1 9.1 %collective-permute-start.11 = (bf16[56,1024]{1,0:T(8,128)(2,1)S(1)}, bf16[56,1024]{1,0:T(8,128)(2,1)S(1)}, u32[]{:S(2)}, u32[]{:S(2)}) collective-permute-start(bf16[56,1024]{1,0:T(8,128)(2,1)S(1)} %get-tuple-element.72.refs_0_), channel_id=1, source_target_pairs={{0,4},{1,5},{2,6},{3,7},{4,0},{5,1},{6,2},{7,3},{8,12},{9,13},{10,... | collective-permute-start | bytes 344072 | tf_op jit(solution)/shard_map/ppermute | solution.py:472
  121.6 23.8 %all-to-all-start.4 = ((bf16[32,8,640]{2,1,0:T(8,128)(2,1)}), bf16[32,8,640]{2,1,0:T(8,128)(2,1)S(1)}, u32[]{:S(2)}, u32[]{:S(2)}) async-start(bf16[32,8,640]{2,1,0:T(8,128)(2,1)} %mid_x.3), calls=%async_computation.4 | async-start | bytes 655360 | tf_op jit(solution)/shard_map/all_to_all | solution.py:497
  132.6 4.5 %collective-permute-start.18 = (bf16[24,1024]{1,0:T(8,128)(2,1)S(1)}, bf16[24,1024]{1,0:T(8,128)(2,1)S(1)}, u32[]{:S(2)}, u32[]{:S(2)}) collective-permute-start(bf16[24,1024]{1,0:T(8,128)(2,1)S(1)} %get-tuple-element.81), channel_id=1, source_target_pairs={{0,1},{1,2},{2,3},{3,0},{4,5},{5,6},{6,7},{7,4},{8,9},{9,10},{10,1... | collective-permute-start | bytes 147464 | tf_op jit(solution)/shard_map/ppermute | solution.py:472
  132.9 5.1 %collective-permute-start.19 = (bf16[24,1024]{1,0:T(8,128)(2,1)S(1)}, bf16[24,1024]{1,0:T(8,128)(2,1)S(1)}, u32[]{:S(2)}, u32[]{:S(2)}) collective-permute-start(bf16[24,1024]{1,0:T(8,128)(2,1)S(1)} %get-tuple-element.82), channel_id=1, source_target_pairs={{0,2},{1,3},{2,0},{3,1},{4,6},{5,7},{6,4},{7,5},{8,10},{9,11},{10,... | collective-permute-start | bytes 147464 | tf_op jit(solution)/shard_map/ppermute | solution.py:472
  135.3 3.7 %collective-permute-start.20 = (bf16[24,1024]{1,0:T(8,128)(2,1)S(1)}, bf16[24,1024]{1,0:T(8,128)(2,1)S(1)}, u32[]{:S(2)}, u32[]{:S(2)}) collective-permute-start(bf16[24,1024]{1,0:T(8,128)(2,1)S(1)} %get-tuple-element.83), channel_id=1, source_target_pairs={{0,3},{1,0},{2,1},{3,2},{4,7},{5,4},{6,5},{7,6},{8,11},{9,8},{10,9... | collective-permute-start | bytes 147464 | tf_op jit(solution)/shard_map/ppermute | solution.py:472

commit v4 on v3

--- a/solution.py
+++ b/solution.py
@@ -434,34 +434,38 @@
     )(*args)
 
 
-def pack_kernel(wx_ref, wy_ref, x_ref, y_ref):
-    def join(parts):
-        return jnp.concatenate([part.astype(F32) for part in parts], axis=1)
-
+def join(parts):
+    return jnp.concatenate([part.astype(F32) for part in parts], axis=1)
+
+
+def pack_x_kernel(w_ref, out_ref):
     for layer in range(LAYERS):
-        own = join([wx_ref[layer, 0, i] for i in range(2)]).astype(BF16)
+        own = join([w_ref[layer, 0, i] for i in range(2)]).astype(BF16)
         for i in range(16):
-            x_ref[i, layer] = own
+            out_ref[i, layer] = own
+
+
+def pack_y_kernel(w_ref, out_ref):
+    for layer in range(LAYERS):
         rows = []
         for j in range(4):
-            own = join([wy_ref[layer, j, i] for i in range(2)])
+            own = join([w_ref[layer, j, i] for i in range(2)])
             rows.append(join([own[t * 8 : (t + 1) * 8] for t in range(8)]))
-        y_ref[layer] = jnp.concatenate(rows, axis=0).astype(BF16)
-
-
-def pack_call(spectral_x, spectral_y):
-    shapes = (16, LAYERS, CH, 128), (LAYERS, ROWS - RYP, QUARTER)
-    out_shape = [jax.ShapeDtypeStruct(shape, BF16) for shape in shapes]
+        out_ref[layer] = jnp.concatenate(rows, axis=0).astype(BF16)
+
+
+def pack_call(kernel, name, weights, shape):
+    out_shape = jax.ShapeDtypeStruct(shape, BF16)
     return pl.pallas_call(
-        pack_kernel,
-        name="pack",
+        kernel,
+        name=name,
         grid=(1,),
-        in_specs=[whole(spectral_x), whole(spectral_y)],
-        out_specs=[whole(a) for a in out_shape],
+        in_specs=[whole(weights)],
+        out_specs=whole(out_shape),
         out_shape=out_shape,
         compiler_params=params(16),
-        cost_estimate=estimate(2),
-    )(spectral_x, spectral_y)
+        cost_estimate=estimate(1),
+    )(weights)
 
 
 def swap_cores(x):
@@ -476,7 +480,9 @@
     c = {name: jnp.asarray(value) for name, value in make_constants().items()}
     core = lax.rem(lax.axis_index("gx"), 2).reshape(1).astype(jnp.int32)
     me = lax.axis_index("gy").reshape(1).astype(jnp.int32)
-    own_x, wy = pack_call(spectral_x, spectral_y)
+    own_x = pack_call(pack_x_kernel, "pack_x", spectral_x, (16, LAYERS, CH, 128))
+    own_x, spectral_y = lax.optimization_barrier((own_x, spectral_y))
+    wy = pack_call(pack_y_kernel, "pack_y", spectral_y, (LAYERS, ROWS - RYP, QUARTER))
     same_core = [list(range(s, 32, 2)) for s in range(2)]
     mine = lax.all_to_all(own_x, "gx", 0, 0, axis_index_groups=same_core, tiled=True)
     swapped = swap_cores(mine)

time: 159 us -> 159 us (level)
  no operation moved by 1% of the time
where the time goes in v4:
time: 159 us
  starting transfers between devices  69.9 us (44%)
  waiting for transfers between devices  44.4 us (28%)
  Pallas kernels  39.1 us (25%)
  local copies, waits for them, and re-layouts  5.05 us (3%)
    ppermute x20, waiting for transfers between devices, permute_y(): return lax.ppermute(x, 'gy', [(i, moved(i, flip, step)) for i in range(8)])  26.3 us
    ppermute x20, starting transfers between devices, permute_y(): return lax.ppermute(x, 'gy', [(i, moved(i, flip, step)) for i in range(8)])  24 us
    pallas_call x2, Pallas kernels, last_call(): pl.pallas_call(functools.partial(last_kernel, more, group), name='last',...  23.8 us
    all_to_all x2, starting transfers between devices, body(): recv = lax.all_to_all(zx.reshape(32, LINE, RX * CH), 'gx', 0, 0, tiled=True)  17.7 us
    all_to_all x2, starting transfers between devices, body(): yx = lax.all_to_all(send, 'gx', 0, 0, tiled=True).reshape(256, RX * CH)  16.2 us
    all_to_all x2, waiting for transfers between devices, body(): yx = lax.all_to_all(send, 'gx', 0, 0, tiled=True).reshape(256, RX * CH)  12.9 us
    all_to_all x1, starting transfers between devices, body(): lax.all_to_all(own_x, 'gx', 0, 0, axis_index_groups=same_core, tiled=True)  11.7 us
    pallas_call x1, Pallas kernels, first_call(): pl.pallas_call(first_kernel, name='first', grid=(64 // GROUP,), in_specs=...  6.16 us
  transfers between devices with their start and end apart: 26, of which 20 were waited for; matrix products, arithmetic and copies ran while one was open for 0% of the time, Pallas kernels for 6%

profile of v4, /device:TPU:1, one launch (start us, length us, event | category | flops | bytes accessed | tf_op | source)
XLA Modules:
  0.0 158.6 jit_solution(5199722171191369297)
XLA Ops:
  0.0 0.9 copy-done.2
  0.9 0.9 pack_x.1
  1.8 11.7 %all-to-all-start.1 = ((bf16[16,2,64,128]{3,2,1,0:T(8,128)(2,1)}), bf16[16,2,64,128]{3,2,1,0:T(8,128)(2,1)S(1)}, u32[]{:S(2)}, u32[]{:S(2)}) async-start(bf16[16,2,64,128]{3,2,1,0:T(8,128)(2,1)} %pack_x.1), calls=%async_computation.1 | async-start | bytes 1048576 | tf_op jit(solution)/shard_map/all_to_all | solution.py:487
  13.6 0.0 copy-start
  13.6 0.0 copy-start.7
  13.6 0.0 copy-start.8
  13.6 0.1 pack_y.1.wy_ref.refs_11_
  13.8 1.4 copy-done
  15.2 6.2 %first.1 = (bf16[256,4096]{1,0:T(8,128)(2,1)S(1)}, bf16[256,640]{1,0:T(8,128)(2,1)}, bf16[4,56,1024]{2,1,0:T(8,128)(2,1)S(1)}) custom-call(bf16[64,64,256]{2,1,0:T(8,128)(2,1)S(1)} %bitcast.27, bf16[16,128]{1,0:T(8,128)(2,1)S(1)} %copy-done.8, bf16[24,256]{1,0:T(8,128)(2,1)S(1)} %copy-done.7, bf16[2,32,1024]{2,1,0:T(8,128)(2,1)S(1)} %pack_y.1.wy_ref.refs_11_), custom_call_target="tpu_custom_call" | custom-call | flops 10000000000 | bytes 1048576 | tf_op jit(solution)/shard_map/first/pallas_call | solution.py:154
  21.3 1.3 copy-done.9
  22.7 2.9 %collective-permute-start.3 = (bf16[56,1024]{1,0:T(8,128)(2,1)S(1)}, bf16[56,1024]{1,0:T(8,128)(2,1)S(1)}, u32[]{:S(2)}, u32[]{:S(2)}) collective-permute-start(bf16[56,1024]{1,0:T(8,128)(2,1)S(1)} %get-tuple-element.89), channel_id=1, source_target_pairs={{0,6},{1,7},{2,4},{3,5},{4,2},{5,3},{6,0},{7,1},{8,14},{9,15},{10,... | collective-permute-start | bytes 344072 | tf_op jit(solution)/shard_map/ppermute | solution.py:476
  25.6 0.9 collective-permute-start.2
  26.5 0.6 collective-permute-start.1
  27.1 1.1 collective-permute-start
  28.2 1.0 collective-permute-done.3.refs_4_
  29.2 1.5 collective-permute-done.2.refs_3_
  30.6 0.8 collective-permute-done.1.refs_2_
  31.4 0.5 collective-permute-done.refs_1_
  31.9 0.0 all-to-all-done.1.w0_ref
  31.9 12.4 %all-to-all-start = ((bf16[32,8,640]{2,1,0:T(8,128)(2,1)}), bf16[32,8,640]{2,1,0:T(8,128)(2,1)S(1)}, u32[]{:S(2)}, u32[]{:S(2)}) async-start(bf16[32,8,640]{2,1,0:T(8,128)(2,1)} %bitcast.7), calls=%async_computation | async-start | bytes 655360 | tf_op jit(solution)/shard_map/all_to_all | solution.py:500
  44.3 0.3 collective-permute-start.7
  44.6 1.0 collective-permute-start.4
  45.7 1.1 collective-permute-start.6
  46.7 1.3 collective-permute-start.5
  48.0 2.6 %collective-permute-done.4.refs_5_ = bf16[56,1024]{1,0:T(8,128)(2,1)S(1)} collective-permute-done((bf16[56,1024]{1,0:T(8,128)(2,1)S(1)}, bf16[56,1024]{1,0:T(8,128)(2,1)S(1)}, u32[]{:S(2)}, u32[]{:S(2)}) %collective-permute-start.4) | collective-permute-done | bytes 114720 | tf_op jit(solution)/shard_map/ppermute | solution.py:476
  50.6 2.1 %collective-permute-done.6.refs_7_ = bf16[56,1024]{1,0:T(8,128)(2,1)S(1)} collective-permute-done((bf16[56,1024]{1,0:T(8,128)(2,1)S(1)}, bf16[56,1024]{1,0:T(8,128)(2,1)S(1)}, u32[]{:S(2)}, u32[]{:S(2)}) %collective-permute-start.6) | collective-permute-done | bytes 114720 | tf_op jit(solution)/shard_map/ppermute | solution.py:476
  52.7 1.8 %collective-permute-done.5.refs_6_ = bf16[56,1024]{1,0:T(8,128)(2,1)S(1)} collective-permute-done((bf16[56,1024]{1,0:T(8,128)(2,1)S(1)}, bf16[56,1024]{1,0:T(8,128)(2,1)S(1)}, u32[]{:S(2)}, u32[]{:S(2)}) %collective-permute-start.5) | collective-permute-done | bytes 114720 | tf_op jit(solution)/shard_map/ppermute | solution.py:476
  54.5 5.2 %all-to-all-done.recv_ref = bf16[32,8,640]{2,1,0:T(8,128)(2,1)S(1)} async-done(((bf16[32,8,640]{2,1,0:T(8,128)(2,1)}), bf16[32,8,640]{2,1,0:T(8,128)(2,1)S(1)}, u32[]{:S(2)}, u32[]{:S(2)}) %all-to-all-start) | async-done | bytes 327712 | tf_op jit(solution)/shard_map/all_to_all | solution.py:500
  59.6 2.4 %mid_x.2 = bf16[32,8,640]{2,1,0:T(8,128)(2,1)} custom-call(s32[1]{0:T(128)} %bitcast.1.core_ref, bf16[32,8,640]{2,1,0:T(8,128)(2,1)S(1)} %all-to-all-done.recv_ref, bf16[16,2,64,128]{3,2,1,0:T(8,128)(2,1)S(1)} %all-to-all-done.1.w0_ref, bf16[16,2,64,128]{3,2,1,0:T(8,128)(2,1)S(1)} %collective-permute-done.7.w1_ref, bf16[288,256]{1,0:T(8,128)(2,1)S(1)} %copy-done.5), custom_call_target="tpu_custom_call" | custom-call | flops 3000000000 | bytes 1048576 | tf_op jit(solution)/shard_map/mid_x/pallas_call | solution.py:245
  62.1 6.9 %all-to-all-start.2 = ((bf16[32,8,640]{2,1,0:T(8,128)(2,1)}), bf16[32,8,640]{2,1,0:T(8,128)(2,1)S(1)}, u32[]{:S(2)}, u32[]{:S(2)}) async-start(bf16[32,8,640]{2,1,0:T(8,128)(2,1)} %mid_x.2), calls=%async_computation.2 | async-start | bytes 655360 | tf_op jit(solution)/shard_map/all_to_all | solution.py:503
  69.0 0.0 copy-start.3
  69.0 0.0 copy-start.4
  69.0 1.6 mid_y.2
  70.6 0.4 collective-permute-start.8
  71.0 2.4 %collective-permute-start.9 = (bf16[24,1024]{1,0:T(8,128)(2,1)S(1)}, bf16[24,1024]{1,0:T(8,128)(2,1)S(1)}, u32[]{:S(2)}, u32[]{:S(2)}) collective-permute-start(bf16[24,1024]{1,0:T(8,128)(2,1)S(1)} %get-tuple-element.66), channel_id=1, source_target_pairs={{0,2},{1,3},{2,0},{3,1},{4,6},{5,7},{6,4},{7,5},{8,10},{9,11},{10,... | collective-permute-start | bytes 147464 | tf_op jit(solution)/shard_map/ppermute | solution.py:476
  73.3 0.8 collective-permute-start.10
  74.1 0.9 collective-permute-done.8.refs_4_
  75.1 1.1 collective-permute-done.9.refs_5_
  76.1 0.9 collective-permute-done.10.refs_6_
  77.0 6.4 %all-to-all-done.2 = bf16[32,8,640]{2,1,0:T(8,128)(2,1)S(1)} async-done(((bf16[32,8,640]{2,1,0:T(8,128)(2,1)}), bf16[32,8,640]{2,1,0:T(8,128)(2,1)S(1)}, u32[]{:S(2)}, u32[]{:S(2)}) %all-to-all-start.2) | async-done | bytes 327712 | tf_op jit(solution)/shard_map/all_to_all | solution.py:503
  83.4 11.1 %last.2 = (bf16[256,4096]{1,0:T(8,128)(2,1)S(1)}, bf16[256,640]{1,0:T(8,128)(2,1)}, bf16[4,56,1024]{2,1,0:T(8,128)(2,1)S(1)}) custom-call(s32[1]{0:T(128)} %bitcast.me_ref.refs_0_, bf16[256,640]{1,0:T(8,128)(2,1)S(1)} %bitcast.25, bf16[16,128]{1,0:T(8,128)(2,1)S(1)} %copy-done.8, bf16[24,1024]{1,0:T(8,128)(2,1)S(1)} %get-tuple-element.64.refs_3_, ...), custom_call_target="tpu_custom_call" | custom-call | flops 12000000000 | bytes 1048576 | tf_op jit(solution)/shard_map/last/pallas_call | solution.py:424
  94.6 1.3 copy-done.10
  95.9 5.3 %all-to-all-start.3 = ((bf16[32,8,640]{2,1,0:T(8,128)(2,1)}), bf16[32,8,640]{2,1,0:T(8,128)(2,1)S(1)}, u32[]{:S(2)}, u32[]{:S(2)}) async-start(bf16[32,8,640]{2,1,0:T(8,128)(2,1)} %bitcast.14), calls=%async_computation.3 | async-start | bytes 655360 | tf_op jit(solution)/shard_map/all_to_all | solution.py:500
  101.3 1.5 collective-permute-start.15
  102.8 1.7 %collective-permute-start.14 = (bf16[56,1024]{1,0:T(8,128)(2,1)S(1)}, bf16[56,1024]{1,0:T(8,128)(2,1)S(1)}, u32[]{:S(2)}, u32[]{:S(2)}) collective-permute-start(bf16[56,1024]{1,0:T(8,128)(2,1)S(1)} %get-tuple-element.85), channel_id=1, source_target_pairs={{0,6},{1,7},{2,4},{3,5},{4,2},{5,3},{6,0},{7,1},{8,14},{9,15},{10,... | collective-permute-start | bytes 344072 | tf_op jit(solution)/shard_map/ppermute | solution.py:476
  104.5 2.3 %collective-permute-start.17 = (bf16[56,1024]{1,0:T(8,128)(2,1)S(1)}, bf16[56,1024]{1,0:T(8,128)(2,1)S(1)}, u32[]{:S(2)}, u32[]{:S(2)}) collective-permute-start(bf16[56,1024]{1,0:T(8,128)(2,1)S(1)} %get-tuple-element.86), channel_id=1, source_target_pairs={{0,7},{1,4},{2,5},{3,6},{4,3},{5,0},{6,1},{7,2},{8,15},{9,12},{10,... | collective-permute-start | bytes 344072 | tf_op jit(solution)/shard_map/ppermute | solution.py:476
  106.7 0.2 collective-permute-start.13
  107.0 1.3 collective-permute-start.16
  108.3 2.2 %collective-permute-done.14.refs_4_ = bf16[56,1024]{1,0:T(8,128)(2,1)S(1)} collective-permute-done((bf16[56,1024]{1,0:T(8,128)(2,1)S(1)}, bf16[56,1024]{1,0:T(8,128)(2,1)S(1)}, u32[]{:S(2)}, u32[]{:S(2)}) %collective-permute-start.14) | collective-permute-done | bytes 114720 | tf_op jit(solution)/shard_map/ppermute | solution.py:476
  110.5 1.1 collective-permute-start.11
  111.7 3.3 %collective-permute-done.17.refs_7_ = bf16[56,1024]{1,0:T(8,128)(2,1)S(1)} collective-permute-done((bf16[56,1024]{1,0:T(8,128)(2,1)S(1)}, bf16[56,1024]{1,0:T(8,128)(2,1)S(1)}, u32[]{:S(2)}, u32[]{:S(2)}) %collective-permute-start.17) | collective-permute-done | bytes 114720 | tf_op jit(solution)/shard_map/ppermute | solution.py:476
  115.0 1.3 collective-permute-done.13.refs_3_
  116.3 3.3 %collective-permute-done.11.refs_1_ = bf16[56,1024]{1,0:T(8,128)(2,1)S(1)} collective-permute-done((bf16[56,1024]{1,0:T(8,128)(2,1)S(1)}, bf16[56,1024]{1,0:T(8,128)(2,1)S(1)}, u32[]{:S(2)}, u32[]{:S(2)}) %collective-permute-start.11) | collective-permute-done | bytes 114720 | tf_op jit(solution)/shard_map/ppermute | solution.py:476
  119.6 2.5 %mid_x.3 = bf16[32,8,640]{2,1,0:T(8,128)(2,1)} custom-call(s32[1]{0:T(128)} %bitcast.1.core_ref, bf16[32,8,640]{2,1,0:T(8,128)(2,1)S(1)} %all-to-all-done.3.recv_ref, bf16[16,2,64,128]{3,2,1,0:T(8,128)(2,1)S(1)} %all-to-all-done.1.w0_ref, bf16[16,2,64,128]{3,2,1,0:T(8,128)(2,1)S(1)} %collective-permute-done.7.w1_ref, bf16[288,256]{1,0:T(8,128)(2,1)S(1)} %copy-done.5), custom_call_target="tpu_custom_call" | custom-call | flops 3000000000 | bytes 1048576 | tf_op jit(solution)/shard_map/mid_x/pallas_call | solution.py:245
  122.1 9.4 %all-to-all-start.4 = ((bf16[32,8,640]{2,1,0:T(8,128)(2,1)}), bf16[32,8,640]{2,1,0:T(8,128)(2,1)S(1)}, u32[]{:S(2)}, u32[]{:S(2)}) async-start(bf16[32,8,640]{2,1,0:T(8,128)(2,1)} %mid_x.3), calls=%async_computation.4 | async-start | bytes 655360 | tf_op jit(solution)/shard_map/all_to_all | solution.py:503
  131.5 1.6 mid_y.3
  133.0 0.3 collective-permute-start.18
  133.4 2.4 %collective-permute-start.19 = (bf16[24,1024]{1,0:T(8,128)(2,1)S(1)}, bf16[24,1024]{1,0:T(8,128)(2,1)S(1)}, u32[]{:S(2)}, u32[]{:S(2)}) collective-permute-start(bf16[24,1024]{1,0:T(8,128)(2,1)S(1)} %get-tuple-element.82), channel_id=1, source_target_pairs={{0,2},{1,3},{2,0},{3,1},{4,6},{5,7},{6,4},{7,5},{8,10},{9,11},{10,... | collective-permute-start | bytes 147464 | tf_op jit(solution)/shard_map/ppermute | solution.py:476
  135.8 0.6 collective-permute-start.20
  136.4 1.1 collective-permute-done.18.refs_4_
  137.6 1.0 collective-permute-done.19.refs_5_
  138.5 0.9 collective-permute-done.20.refs_6_
  139.4 6.5 %all-to-all-done.4 = bf16[32,8,640]{2,1,0:T(8,128)(2,1)S(1)} async-done(((bf16[32,8,640]{2,1,0:T(8,128)(2,1)}), bf16[32,8,640]{2,1,0:T(8,128)(2,1)S(1)}, u32[]{:S(2)}, u32[]{:S(2)}) %all-to-all-start.4) | async-done | bytes 327712 | tf_op jit(solution)/shard_map/all_to_all | solution.py:503
  145.9 12.7 %last.3 = bf16[64,64,256]{2,1,0:T(8,128)(2,1)} custom-call(s32[1]{0:T(128)} %bitcast.me_ref.refs_0_, bf16[256,640]{1,0:T(8,128)(2,1)S(1)} %bitcast.26, bf16[16,128]{1,0:T(8,128)(2,1)S(1)} %copy-done.8, bf16[24,1024]{1,0:T(8,128)(2,1)S(1)} %get-tuple-element.80.refs_3_, bf16[24,1024]{1,0:T(8,128)(2,1)S(1)} %collective-permute-done.18.refs_4_, ...), custom_call_target="tpu_custom_call" | custom-call | flops 12000000000 | bytes 1048576 | tf_op jit(solution)/shard_map/last/pallas_call | solution.py:424
  (21 shorter events, 0.1 us)
Async XLA Ops:
  0.0 13.6 %copy-start.1 = (bf16[2,4,2,64,64]{4,3,2,1,0:T(8,128)(2,1)S(1)}, bf16[2,4,2,64,64]{4,3,2,1,0:T(8,128)(2,1)}, u32[]{:S(2)}) copy-start(bf16[2,4,2,64,64]{4,3,2,1,0:T(8,128)(2,1)} %w_ref.2) | copy-start | bytes 393220
  0.0 0.9 copy-start.2
  1.8 30.1 %all-to-all-start.1 = ((bf16[16,2,64,128]{3,2,1,0:T(8,128)(2,1)}), bf16[16,2,64,128]{3,2,1,0:T(8,128)(2,1)S(1)}, u32[]{:S(2)}, u32[]{:S(2)}) async-start(bf16[16,2,64,128]{3,2,1,0:T(8,128)(2,1)} %pack_x.1), calls=%async_computation.1 | async-start | bytes 1048576 | tf_op jit(solution)/shard_map/all_to_all | solution.py:487
  13.6 1.6 %copy-start = (bf16[1,64,64,256]{3,2,1,0:T(8,128)(2,1)S(1)}, bf16[1,64,64,256]{3,2,1,0:T(8,128)(2,1)}, u32[]{:S(2)}) copy-start(bf16[1,64,64,256]{3,2,1,0:T(8,128)(2,1)} %param.9) | copy-start | bytes 6291460
  13.6 1.6 copy-start.7
  13.6 1.6 copy-start.8
  15.2 44.5 %copy-start.5 = (bf16[288,256]{1,0:T(8,128)(2,1)S(1)}, bf16[288,256]{1,0:T(8,128)(2,1)}, u32[]{:S(2)}) copy-start(bf16[288,256]{1,0:T(8,128)(2,1)} %constant.37.clone.tab_ref) | copy-start | bytes 442372
  21.3 1.3 copy-start.9
  22.7 6.5 %collective-permute-start.3 = (bf16[56,1024]{1,0:T(8,128)(2,1)S(1)}, bf16[56,1024]{1,0:T(8,128)(2,1)S(1)}, u32[]{:S(2)}, u32[]{:S(2)}) collective-permute-start(bf16[56,1024]{1,0:T(8,128)(2,1)S(1)} %get-tuple-element.89), channel_id=1, source_target_pairs={{0,6},{1,7},{2,4},{3,5},{4,2},{5,3},{6,0},{7,1},{8,14},{9,15},{10,... | collective-permute-start | bytes 344072 | tf_op jit(solution)/shard_map/ppermute | solution.py:476
  25.6 5.0 %collective-permute-start.2 = (bf16[56,1024]{1,0:T(8,128)(2,1)S(1)}, bf16[56,1024]{1,0:T(8,128)(2,1)S(1)}, u32[]{:S(2)}, u32[]{:S(2)}) collective-permute-start(bf16[56,1024]{1,0:T(8,128)(2,1)S(1)} %get-tuple-element.90), channel_id=1, source_target_pairs={{0,3},{1,0},{2,1},{3,2},{4,7},{5,4},{6,5},{7,6},{8,11},{9,8},{10,9... | collective-permute-start | bytes 344072 | tf_op jit(solution)/shard_map/ppermute | solution.py:476
  26.5 4.9 %collective-permute-start.1 = (bf16[56,1024]{1,0:T(8,128)(2,1)S(1)}, bf16[56,1024]{1,0:T(8,128)(2,1)S(1)}, u32[]{:S(2)}, u32[]{:S(2)}) collective-permute-start(bf16[56,1024]{1,0:T(8,128)(2,1)S(1)} %get-tuple-element.91), channel_id=1, source_target_pairs={{0,1},{1,2},{2,3},{3,0},{4,5},{5,6},{6,7},{7,4},{8,9},{9,10},{10,1... | collective-permute-start | bytes 344072 | tf_op jit(solution)/shard_map/ppermute | solution.py:476
  27.1 4.8 %collective-permute-start = (bf16[56,1024]{1,0:T(8,128)(2,1)S(1)}, bf16[56,1024]{1,0:T(8,128)(2,1)S(1)}, u32[]{:S(2)}, u32[]{:S(2)}) collective-permute-start(bf16[56,1024]{1,0:T(8,128)(2,1)S(1)} %get-tuple-element.56.refs_0_), channel_id=1, source_target_pairs={{0,4},{1,5},{2,6},{3,7},{4,0},{5,1},{6,2},{7,3},{8,12},{9,13},{10,... | collective-permute-start | bytes 344072 | tf_op jit(solution)/shard_map/ppermute | solution.py:476
  31.9 27.7 %all-to-all-start = ((bf16[32,8,640]{2,1,0:T(8,128)(2,1)}), bf16[32,8,640]{2,1,0:T(8,128)(2,1)S(1)}, u32[]{:S(2)}, u32[]{:S(2)}) async-start(bf16[32,8,640]{2,1,0:T(8,128)(2,1)} %bitcast.7), calls=%async_computation | async-start | bytes 655360 | tf_op jit(solution)/shard_map/all_to_all | solution.py:500
  44.3 15.3 %collective-permute-start.7 = (bf16[16,2,64,128]{3,2,1,0:T(8,128)(2,1)S(1)}, bf16[16,2,64,128]{3,2,1,0:T(8,128)(2,1)S(1)}, u32[]{:S(2)}, u32[]{:S(2)}) collective-permute-start(bf16[16,2,64,128]{3,2,1,0:T(8,128)(2,1)S(1)} %all-to-all-done.1.w0_ref), channel_id=1, source_target_pairs={{0,8},{8,0},{16,24},{24,16},{32,40},{40,32},{48,56},{56,48},{64,72... | collective-permute-start | bytes 1572872 | tf_op jit(solution)/shard_map/ppermute | solution.py:472
  44.6 6.0 %collective-permute-start.4 = (bf16[56,1024]{1,0:T(8,128)(2,1)S(1)}, bf16[56,1024]{1,0:T(8,128)(2,1)S(1)}, u32[]{:S(2)}, u32[]{:S(2)}) collective-permute-start(bf16[56,1024]{1,0:T(8,128)(2,1)S(1)} %get-tuple-element.89), channel_id=1, source_target_pairs={{0,2},{1,3},{2,0},{3,1},{4,6},{5,7},{6,4},{7,5},{8,10},{9,11},{10,... | collective-permute-start | bytes 344072 | tf_op jit(solution)/shard_map/ppermute | solution.py:476
  45.7 7.0 %collective-permute-start.6 = (bf16[56,1024]{1,0:T(8,128)(2,1)S(1)}, bf16[56,1024]{1,0:T(8,128)(2,1)S(1)}, u32[]{:S(2)}, u32[]{:S(2)}) collective-permute-start(bf16[56,1024]{1,0:T(8,128)(2,1)S(1)} %get-tuple-element.90), channel_id=1, source_target_pairs={{0,7},{1,4},{2,5},{3,6},{4,3},{5,0},{6,1},{7,2},{8,15},{9,12},{10,... | collective-permute-start | bytes 344072 | tf_op jit(solution)/shard_map/ppermute | solution.py:476
  46.7 7.7 %collective-permute-start.5 = (bf16[56,1024]{1,0:T(8,128)(2,1)S(1)}, bf16[56,1024]{1,0:T(8,128)(2,1)S(1)}, u32[]{:S(2)}, u32[]{:S(2)}) collective-permute-start(bf16[56,1024]{1,0:T(8,128)(2,1)S(1)} %get-tuple-element.91), channel_id=1, source_target_pairs={{0,5},{1,6},{2,7},{3,4},{4,1},{5,2},{6,3},{7,0},{8,13},{9,14},{10,... | collective-permute-start | bytes 344072 | tf_op jit(solution)/shard_map/ppermute | solution.py:476
  59.6 9.3 %copy-start.6 = (bf16[2,8,24,128]{3,2,1,0:T(8,128)(2,1)S(1)}, bf16[2,8,24,128]{3,2,1,0:T(8,128)(2,1)}, u32[]{:S(2)}) copy-start(bf16[2,8,24,128]{3,2,1,0:T(8,128)(2,1)} %constant.38.clone.refs_8_) | copy-start | bytes 294916
  62.1 21.3 %all-to-all-start.2 = ((bf16[32,8,640]{2,1,0:T(8,128)(2,1)}), bf16[32,8,640]{2,1,0:T(8,128)(2,1)S(1)}, u32[]{:S(2)}, u32[]{:S(2)}) async-start(bf16[32,8,640]{2,1,0:T(8,128)(2,1)} %mid_x.2), calls=%async_computation.2 | async-start | bytes 655360 | tf_op jit(solution)/shard_map/all_to_all | solution.py:503
  69.0 14.5 %copy-start.3 = (bf16[2,64,256]{2,1,0:T(8,128)(2,1)S(1)}, bf16[2,64,256]{2,1,0:T(8,128)(2,1)}, u32[]{:S(2)}) copy-start(bf16[2,64,256]{2,1,0:T(8,128)(2,1)} %refs_9_.3) | copy-start | bytes 196612
  69.0 14.5 %copy-start.4 = (bf16[2,256,64]{1,2,0:T(8,128)(2,1)S(1)}, bf16[2,256,64]{1,2,0:T(8,128)(2,1)}, u32[]{:S(2)}) copy-start(bf16[2,256,64]{1,2,0:T(8,128)(2,1)} %param.13) | copy-start | bytes 196612
  70.6 4.5 %collective-permute-start.8 = (bf16[24,1024]{1,0:T(8,128)(2,1)S(1)}, bf16[24,1024]{1,0:T(8,128)(2,1)S(1)}, u32[]{:S(2)}, u32[]{:S(2)}) collective-permute-start(bf16[24,1024]{1,0:T(8,128)(2,1)S(1)} %get-tuple-element.65), channel_id=1, source_target_pairs={{0,1},{1,2},{2,3},{3,0},{4,5},{5,6},{6,7},{7,4},{8,9},{9,10},{10,1... | collective-permute-start | bytes 147464 | tf_op jit(solution)/shard_map/ppermute | solution.py:476
  71.0 5.2 %collective-permute-start.9 = (bf16[24,1024]{1,0:T(8,128)(2,1)S(1)}, bf16[24,1024]{1,0:T(8,128)(2,1)S(1)}, u32[]{:S(2)}, u32[]{:S(2)}) collective-permute-start(bf16[24,1024]{1,0:T(8,128)(2,1)S(1)} %get-tuple-element.66), channel_id=1, source_target_pairs={{0,2},{1,3},{2,0},{3,1},{4,6},{5,7},{6,4},{7,5},{8,10},{9,11},{10,... | collective-permute-start | bytes 147464 | tf_op jit(solution)/shard_map/ppermute | solution.py:476
  73.3 3.7 %collective-permute-start.10 = (bf16[24,1024]{1,0:T(8,128)(2,1)S(1)}, bf16[24,1024]{1,0:T(8,128)(2,1)S(1)}, u32[]{:S(2)}, u32[]{:S(2)}) collective-permute-start(bf16[24,1024]{1,0:T(8,128)(2,1)S(1)} %get-tuple-element.67), channel_id=1, source_target_pairs={{0,3},{1,0},{2,1},{3,2},{4,7},{5,4},{6,5},{7,6},{8,11},{9,8},{10,9... | collective-permute-start | bytes 147464 | tf_op jit(solution)/shard_map/ppermute | solution.py:476
  94.6 1.3 copy-start.10
  95.9 23.8 %all-to-all-start.3 = ((bf16[32,8,640]{2,1,0:T(8,128)(2,1)}), bf16[32,8,640]{2,1,0:T(8,128)(2,1)S(1)}, u32[]{:S(2)}, u32[]{:S(2)}) async-start(bf16[32,8,640]{2,1,0:T(8,128)(2,1)} %bitcast.14), calls=%async_computation.3 | async-start | bytes 655360 | tf_op jit(solution)/shard_map/all_to_all | solution.py:500
  101.3 7.0 %collective-permute-start.15 = (bf16[56,1024]{1,0:T(8,128)(2,1)S(1)}, bf16[56,1024]{1,0:T(8,128)(2,1)S(1)}, u32[]{:S(2)}, u32[]{:S(2)}) collective-permute-start(bf16[56,1024]{1,0:T(8,128)(2,1)S(1)} %get-tuple-element.85), channel_id=1, source_target_pairs={{0,2},{1,3},{2,0},{3,1},{4,6},{5,7},{6,4},{7,5},{8,10},{9,11},{10,... | collective-permute-start | bytes 344072 | tf_op jit(solution)/shard_map/ppermute | solution.py:476
  102.8 7.8 %collective-permute-start.14 = (bf16[56,1024]{1,0:T(8,128)(2,1)S(1)}, bf16[56,1024]{1,0:T(8,128)(2,1)S(1)}, u32[]{:S(2)}, u32[]{:S(2)}) collective-permute-start(bf16[56,1024]{1,0:T(8,128)(2,1)S(1)} %get-tuple-element.85), channel_id=1, source_target_pairs={{0,6},{1,7},{2,4},{3,5},{4,2},{5,3},{6,0},{7,1},{8,14},{9,15},{10,... | collective-permute-start | bytes 344072 | tf_op jit(solution)/shard_map/ppermute | solution.py:476
  104.5 10.5 %collective-permute-start.17 = (bf16[56,1024]{1,0:T(8,128)(2,1)S(1)}, bf16[56,1024]{1,0:T(8,128)(2,1)S(1)}, u32[]{:S(2)}, u32[]{:S(2)}) collective-permute-start(bf16[56,1024]{1,0:T(8,128)(2,1)S(1)} %get-tuple-element.86), channel_id=1, source_target_pairs={{0,7},{1,4},{2,5},{3,6},{4,3},{5,0},{6,1},{7,2},{8,15},{9,12},{10,... | collective-permute-start | bytes 344072 | tf_op jit(solution)/shard_map/ppermute | solution.py:476
  106.7 9.5 %collective-permute-start.13 = (bf16[56,1024]{1,0:T(8,128)(2,1)S(1)}, bf16[56,1024]{1,0:T(8,128)(2,1)S(1)}, u32[]{:S(2)}, u32[]{:S(2)}) collective-permute-start(bf16[56,1024]{1,0:T(8,128)(2,1)S(1)} %get-tuple-element.86), channel_id=1, source_target_pairs={{0,3},{1,0},{2,1},{3,2},{4,7},{5,4},{6,5},{7,6},{8,11},{9,8},{10,9... | collective-permute-start | bytes 344072 | tf_op jit(solution)/shard_map/ppermute | solution.py:476
  107.0 9.3 %collective-permute-start.16 = (bf16[56,1024]{1,0:T(8,128)(2,1)S(1)}, bf16[56,1024]{1,0:T(8,128)(2,1)S(1)}, u32[]{:S(2)}, u32[]{:S(2)}) collective-permute-start(bf16[56,1024]{1,0:T(8,128)(2,1)S(1)} %get-tuple-element.87), channel_id=1, source_target_pairs={{0,5},{1,6},{2,7},{3,4},{4,1},{5,2},{6,3},{7,0},{8,13},{9,14},{10,... | collective-permute-start | bytes 344072 | tf_op jit(solution)/shard_map/ppermute | solution.py:476
  108.3 8.0 %collective-permute-start.12 = (bf16[56,1024]{1,0:T(8,128)(2,1)S(1)}, bf16[56,1024]{1,0:T(8,128)(2,1)S(1)}, u32[]{:S(2)}, u32[]{:S(2)}) collective-permute-start(bf16[56,1024]{1,0:T(8,128)(2,1)S(1)} %get-tuple-element.87), channel_id=1, source_target_pairs={{0,1},{1,2},{2,3},{3,0},{4,5},{5,6},{6,7},{7,4},{8,9},{9,10},{10,1... | collective-permute-start | bytes 344072 | tf_op jit(solution)/shard_map/ppermute | solution.py:476
  110.5 9.1 %collective-permute-start.11 = (bf16[56,1024]{1,0:T(8,128)(2,1)S(1)}, bf16[56,1024]{1,0:T(8,128)(2,1)S(1)}, u32[]{:S(2)}, u32[]{:S(2)}) collective-permute-start(bf16[56,1024]{1,0:T(8,128)(2,1)S(1)} %get-tuple-element.72.refs_0_), channel_id=1, source_target_pairs={{0,4},{1,5},{2,6},{3,7},{4,0},{5,1},{6,2},{7,3},{8,12},{9,13},{10,... | collective-permute-start | bytes 344072 | tf_op jit(solution)/shard_map/ppermute | solution.py:476
  122.1 23.8 %all-to-all-start.4 = ((bf16[32,8,640]{2,1,0:T(8,128)(2,1)}), bf16[32,8,640]{2,1,0:T(8,128)(2,1)S(1)}, u32[]{:S(2)}, u32[]{:S(2)}) async-start(bf16[32,8,640]{2,1,0:T(8,128)(2,1)} %mid_x.3), calls=%async_computation.4 | async-start | bytes 655360 | tf_op jit(solution)/shard_map/all_to_all | solution.py:503
  133.0 4.5 %collective-permute-start.18 = (bf16[24,1024]{1,0:T(8,128)(2,1)S(1)}, bf16[24,1024]{1,0:T(8,128)(2,1)S(1)}, u32[]{:S(2)}, u32[]{:S(2)}) collective-permute-start(bf16[24,1024]{1,0:T(8,128)(2,1)S(1)} %get-tuple-element.81), channel_id=1, source_target_pairs={{0,1},{1,2},{2,3},{3,0},{4,5},{5,6},{6,7},{7,4},{8,9},{9,10},{10,1... | collective-permute-start | bytes 147464 | tf_op jit(solution)/shard_map/ppermute | solution.py:476
  133.4 5.1 %collective-permute-start.19 = (bf16[24,1024]{1,0:T(8,128)(2,1)S(1)}, bf16[24,1024]{1,0:T(8,128)(2,1)S(1)}, u32[]{:S(2)}, u32[]{:S(2)}) collective-permute-start(bf16[24,1024]{1,0:T(8,128)(2,1)S(1)} %get-tuple-element.82), channel_id=1, source_target_pairs={{0,2},{1,3},{2,0},{3,1},{4,6},{5,7},{6,4},{7,5},{8,10},{9,11},{10,... | collective-permute-start | bytes 147464 | tf_op jit(solution)/shard_map/ppermute | solution.py:476
  135.8 3.7 %collective-permute-start.20 = (bf16[24,1024]{1,0:T(8,128)(2,1)S(1)}, bf16[24,1024]{1,0:T(8,128)(2,1)S(1)}, u32[]{:S(2)}, u32[]{:S(2)}) collective-permute-start(bf16[24,1024]{1,0:T(8,128)(2,1)S(1)} %get-tuple-element.83), channel_id=1, source_target_pairs={{0,3},{1,0},{2,1},{3,2},{4,7},{5,4},{6,5},{7,6},{8,11},{9,8},{10,9... | collective-permute-start | bytes 147464 | tf_op jit(solution)/shard_map/ppermute | solution.py:476

commit v5 on v4

--- a/solution.py
+++ b/solution.py
@@ -23,7 +23,6 @@
 GROUP = 16
 WIDE = GROUP * CH
 LAST_GROUPS = (64, 16)
-EARLY = 5
 LINE = 8
 
 
@@ -494,9 +493,6 @@
         for flip, step in ((0, 0),) + SHIFTS:
             chunk = lax.dynamic_slice_in_dim(zy, lax.rem(me[0] + step, 4), 1, 0)[0]
             zs.append(permute_y(chunk, flip, step) if flip or step else chunk)
-        if l == 0:
-            zx, early = lax.optimization_barrier((zx, zs[:EARLY]))
-            zs = early + zs[EARLY:]
         recv = lax.all_to_all(zx.reshape(32, LINE, RX * CH), "gx", 0, 0, tiled=True)
         zs, recv = lax.optimization_barrier((zs, recv))
         send = mid_x(l, core, recv, mine, swapped, c)

time: 159 us -> 159 us (level)
    all_to_all x1, waiting for transfers between devices: 0.01 us -> 6.15 us  [body(): lax.all_to_all(own_x, 'gx', 0, 0, axis_index_groups=same_core, tiled=True)]
    all_to_all x2, waiting for transfers between devices: 5.16 us -> 0.01 us  [body(): recv = lax.all_to_all(zx.reshape(32, LINE, RX * CH), 'gx', 0, 0, tiled=True)]
    all_to_all x2, starting transfers between devices: 17.7 us -> 12.9 us  [body(): recv = lax.all_to_all(zx.reshape(32, LINE, RX * CH), 'gx', 0, 0, tiled=True)]
    all_to_all x2, starting transfers between devices: 16.2 us -> 20.2 us  [body(): yx = lax.all_to_all(send, 'gx', 0, 0, tiled=True).reshape(256, RX * CH)]
    ppermute x20, starting transfers between devices: 24 us -> 25.9 us  [permute_y(): return lax.ppermute(x, 'gy', [(i, moved(i, flip, step)) for i in range(8)])]
  transfers between devices with their start and end apart: 26 -> 26, of which waited for: 20 -> 16; matrix products, arithmetic and copies ran while one was open for 0% -> 0% of each run, Pallas kernels for 6% -> 6%
where the time goes in v5:
time: 159 us
  starting transfers between devices  71 us (45%)
  waiting for transfers between devices  43.2 us (27%)
  Pallas kernels  39.1 us (25%)
  local copies, waits for them, and re-layouts  5.11 us (3%)
    ppermute x20, starting transfers between devices, permute_y(): return lax.ppermute(x, 'gy', [(i, moved(i, flip, step)) for i in range(8)])  25.9 us
    ppermute x20, waiting for transfers between devices, permute_y(): return lax.ppermute(x, 'gy', [(i, moved(i, flip, step)) for i in range(8)])  24.9 us
    pallas_call x2, Pallas kernels, last_call(): pl.pallas_call(functools.partial(last_kernel, more, group), name='last',...  23.8 us
    all_to_all x2, starting transfers between devices, body(): yx = lax.all_to_all(send, 'gx', 0, 0, tiled=True).reshape(256, RX * CH)  20.2 us
    all_to_all x2, starting transfers between devices, body(): recv = lax.all_to_all(zx.reshape(32, LINE, RX * CH), 'gx', 0, 0, tiled=True)  12.9 us
    all_to_all x2, waiting for transfers between devices, body(): yx = lax.all_to_all(send, 'gx', 0, 0, tiled=True).reshape(256, RX * CH)  12.1 us
    all_to_all x1, starting transfers between devices, body(): lax.all_to_all(own_x, 'gx', 0, 0, axis_index_groups=same_core, tiled=True)  11.7 us
    pallas_call x1, Pallas kernels, first_call(): pl.pallas_call(first_kernel, name='first', grid=(64 // GROUP,), in_specs=...  6.16 us
  transfers between devices with their start and end apart: 26, of which 16 were waited for; matrix products, arithmetic and copies ran while one was open for 0% of the time, Pallas kernels for 6%

profile of v5, /device:TPU:1, one launch (start us, length us, event | category | flops | bytes accessed | tf_op | source)
XLA Modules:
  0.0 158.6 jit_solution(479945922299074112)
XLA Ops:
  0.0 0.9 copy-done.2
  0.9 0.9 pack_x.1
  1.8 11.7 %all-to-all-start.1 = ((bf16[16,2,64,128]{3,2,1,0:T(8,128)(2,1)}), bf16[16,2,64,128]{3,2,1,0:T(8,128)(2,1)S(1)}, u32[]{:S(2)}, u32[]{:S(2)}) async-start(bf16[16,2,64,128]{3,2,1,0:T(8,128)(2,1)} %pack_x.1), calls=%async_computation.1 | async-start | bytes 1048576 | tf_op jit(solution)/shard_map/all_to_all | solution.py:486
  13.6 0.0 copy-start
  13.6 0.0 copy-start.7
  13.6 0.0 copy-start.8
  13.6 0.1 pack_y.1.wy_ref.refs_11_
  13.7 1.4 copy-done
  15.2 6.2 %first.1 = (bf16[256,4096]{1,0:T(8,128)(2,1)S(1)}, bf16[256,640]{1,0:T(8,128)(2,1)}, bf16[4,56,1024]{2,1,0:T(8,128)(2,1)S(1)}) custom-call(bf16[64,64,256]{2,1,0:T(8,128)(2,1)S(1)} %bitcast.27, bf16[16,128]{1,0:T(8,128)(2,1)S(1)} %copy-done.8, bf16[24,256]{1,0:T(8,128)(2,1)S(1)} %copy-done.7, bf16[2,32,1024]{2,1,0:T(8,128)(2,1)S(1)} %pack_y.1.wy_ref.refs_11_), custom_call_target="tpu_custom_call" | custom-call | flops 10000000000 | bytes 1048576 | tf_op jit(solution)/shard_map/first/pallas_call | solution.py:153
  21.3 1.3 copy-done.9
  22.7 6.2 %all-to-all-done.1.w0_ref = bf16[16,2,64,128]{3,2,1,0:T(8,128)(2,1)S(1)} async-done(((bf16[16,2,64,128]{3,2,1,0:T(8,128)(2,1)}), bf16[16,2,64,128]{3,2,1,0:T(8,128)(2,1)S(1)}, u32[]{:S(2)}, u32[]{:S(2)}) %all-to-all-start.1) | async-done | bytes 524320 | tf_op jit(solution)/shard_map/all_to_all | solution.py:486
  28.8 7.5 %all-to-all-start = ((bf16[32,8,640]{2,1,0:T(8,128)(2,1)}), bf16[32,8,640]{2,1,0:T(8,128)(2,1)S(1)}, u32[]{:S(2)}, u32[]{:S(2)}) async-start(bf16[32,8,640]{2,1,0:T(8,128)(2,1)} %bitcast.7), calls=%async_computation | async-start | bytes 655360 | tf_op jit(solution)/shard_map/all_to_all | solution.py:496
  36.3 0.3 collective-permute-start.7
  36.7 2.8 %collective-permute-start.4 = (bf16[56,1024]{1,0:T(8,128)(2,1)S(1)}, bf16[56,1024]{1,0:T(8,128)(2,1)S(1)}, u32[]{:S(2)}, u32[]{:S(2)}) collective-permute-start(bf16[56,1024]{1,0:T(8,128)(2,1)S(1)} %get-tuple-element.77), channel_id=1, source_target_pairs={{0,2},{1,3},{2,0},{3,1},{4,6},{5,7},{6,4},{7,5},{8,10},{9,11},{10,... | collective-permute-start | bytes 344072 | tf_op jit(solution)/shard_map/ppermute | solution.py:475
  39.5 0.3 collective-permute-start.3
  39.9 3.3 %collective-permute-start.6 = (bf16[56,1024]{1,0:T(8,128)(2,1)S(1)}, bf16[56,1024]{1,0:T(8,128)(2,1)S(1)}, u32[]{:S(2)}, u32[]{:S(2)}) collective-permute-start(bf16[56,1024]{1,0:T(8,128)(2,1)S(1)} %get-tuple-element.78), channel_id=1, source_target_pairs={{0,7},{1,4},{2,5},{3,6},{4,3},{5,0},{6,1},{7,2},{8,15},{9,12},{10,... | collective-permute-start | bytes 344072 | tf_op jit(solution)/shard_map/ppermute | solution.py:475
  43.1 0.5 collective-permute-start.2
  43.7 1.0 collective-permute-start.5
  44.7 1.9 %collective-permute-done.3.refs_4_ = bf16[56,1024]{1,0:T(8,128)(2,1)S(1)} collective-permute-done((bf16[56,1024]{1,0:T(8,128)(2,1)S(1)}, bf16[56,1024]{1,0:T(8,128)(2,1)S(1)}, u32[]{:S(2)}, u32[]{:S(2)}) %collective-permute-start.3) | collective-permute-done | bytes 114720 | tf_op jit(solution)/shard_map/ppermute | solution.py:475
  46.6 0.7 collective-permute-start.1
  47.3 3.8 %collective-permute-done.6.refs_7_ = bf16[56,1024]{1,0:T(8,128)(2,1)S(1)} collective-permute-done((bf16[56,1024]{1,0:T(8,128)(2,1)S(1)}, bf16[56,1024]{1,0:T(8,128)(2,1)S(1)}, u32[]{:S(2)}, u32[]{:S(2)}) %collective-permute-start.6) | collective-permute-done | bytes 114720 | tf_op jit(solution)/shard_map/ppermute | solution.py:475
  51.1 0.6 collective-permute-start
  51.7 0.8 collective-permute-done.2.refs_3_
  52.5 0.0 collective-permute-done.1.refs_2_
  52.5 2.5 %collective-permute-done.refs_1_ = bf16[56,1024]{1,0:T(8,128)(2,1)S(1)} collective-permute-done((bf16[56,1024]{1,0:T(8,128)(2,1)S(1)}, bf16[56,1024]{1,0:T(8,128)(2,1)S(1)}, u32[]{:S(2)}, u32[]{:S(2)}) %collective-permute-start) | collective-permute-done | bytes 114720 | tf_op jit(solution)/shard_map/ppermute | solution.py:475
  55.0 0.0 copy-start.6
  55.1 2.4 %mid_x.2 = bf16[32,8,640]{2,1,0:T(8,128)(2,1)} custom-call(s32[1]{0:T(128)} %bitcast.1.core_ref, bf16[32,8,640]{2,1,0:T(8,128)(2,1)S(1)} %all-to-all-done.recv_ref, bf16[16,2,64,128]{3,2,1,0:T(8,128)(2,1)S(1)} %all-to-all-done.1.w0_ref, bf16[16,2,64,128]{3,2,1,0:T(8,128)(2,1)S(1)} %collective-permute-done.7.w1_ref, bf16[288,256]{1,0:T(8,128)(2,1)S(1)} %copy-done.5), custom_call_target="tpu_custom_call" | custom-call | flops 3000000000 | bytes 1048576 | tf_op jit(solution)/shard_map/mid_x/pallas_call | solution.py:244
  57.5 11.0 %all-to-all-start.2 = ((bf16[32,8,640]{2,1,0:T(8,128)(2,1)}), bf16[32,8,640]{2,1,0:T(8,128)(2,1)S(1)}, u32[]{:S(2)}, u32[]{:S(2)}) async-start(bf16[32,8,640]{2,1,0:T(8,128)(2,1)} %mid_x.2), calls=%async_computation.2 | async-start | bytes 655360 | tf_op jit(solution)/shard_map/all_to_all | solution.py:499
  68.5 0.0 copy-start.3
  68.5 0.0 copy-start.4
  68.5 1.6 mid_y.2
  70.1 1.5 collective-permute-start.8
  71.6 2.3 %collective-permute-start.9 = (bf16[24,1024]{1,0:T(8,128)(2,1)S(1)}, bf16[24,1024]{1,0:T(8,128)(2,1)S(1)}, u32[]{:S(2)}, u32[]{:S(2)}) collective-permute-start(bf16[24,1024]{1,0:T(8,128)(2,1)S(1)} %get-tuple-element.54), channel_id=1, source_target_pairs={{0,2},{1,3},{2,0},{3,1},{4,6},{5,7},{6,4},{7,5},{8,10},{9,11},{10,... | collective-permute-start | bytes 147464 | tf_op jit(solution)/shard_map/ppermute | solution.py:475
  73.9 1.1 collective-permute-start.10
  75.0 0.0 collective-permute-done.8.refs_4_
  75.0 1.9 %collective-permute-done.9.refs_5_ = bf16[24,1024]{1,0:T(8,128)(2,1)S(1)} collective-permute-done((bf16[24,1024]{1,0:T(8,128)(2,1)S(1)}, bf16[24,1024]{1,0:T(8,128)(2,1)S(1)}, u32[]{:S(2)}, u32[]{:S(2)}) %collective-permute-start.9) | collective-permute-done | bytes 49184 | tf_op jit(solution)/shard_map/ppermute | solution.py:475
  76.9 0.3 collective-permute-done.10.refs_6_
  77.1 5.8 %all-to-all-done.2 = bf16[32,8,640]{2,1,0:T(8,128)(2,1)S(1)} async-done(((bf16[32,8,640]{2,1,0:T(8,128)(2,1)}), bf16[32,8,640]{2,1,0:T(8,128)(2,1)S(1)}, u32[]{:S(2)}, u32[]{:S(2)}) %all-to-all-start.2) | async-done | bytes 327712 | tf_op jit(solution)/shard_map/all_to_all | solution.py:499
  82.9 11.1 %last.2 = (bf16[256,4096]{1,0:T(8,128)(2,1)S(1)}, bf16[256,640]{1,0:T(8,128)(2,1)}, bf16[4,56,1024]{2,1,0:T(8,128)(2,1)S(1)}) custom-call(s32[1]{0:T(128)} %bitcast.me_ref.refs_0_, bf16[256,640]{1,0:T(8,128)(2,1)S(1)} %bitcast.25, bf16[16,128]{1,0:T(8,128)(2,1)S(1)} %copy-done.8, bf16[24,1024]{1,0:T(8,128)(2,1)S(1)} %get-tuple-element.52.refs_3_, ...), custom_call_target="tpu_custom_call" | custom-call | flops 12000000000 | bytes 1048576 | tf_op jit(solution)/shard_map/last/pallas_call | solution.py:423
  94.1 1.3 copy-done.10
  95.4 5.4 %all-to-all-start.3 = ((bf16[32,8,640]{2,1,0:T(8,128)(2,1)}), bf16[32,8,640]{2,1,0:T(8,128)(2,1)S(1)}, u32[]{:S(2)}, u32[]{:S(2)}) async-start(bf16[32,8,640]{2,1,0:T(8,128)(2,1)} %bitcast.14), calls=%async_computation.3 | async-start | bytes 655360 | tf_op jit(solution)/shard_map/all_to_all | solution.py:496
  100.9 2.7 %collective-permute-start.15 = (bf16[56,1024]{1,0:T(8,128)(2,1)S(1)}, bf16[56,1024]{1,0:T(8,128)(2,1)S(1)}, u32[]{:S(2)}, u32[]{:S(2)}) collective-permute-start(bf16[56,1024]{1,0:T(8,128)(2,1)S(1)} %get-tuple-element.73), channel_id=1, source_target_pairs={{0,2},{1,3},{2,0},{3,1},{4,6},{5,7},{6,4},{7,5},{8,10},{9,11},{10,... | collective-permute-start | bytes 344072 | tf_op jit(solution)/shard_map/ppermute | solution.py:475
  103.6 0.1 collective-permute-start.14
  103.7 3.6 %collective-permute-start.17 = (bf16[56,1024]{1,0:T(8,128)(2,1)S(1)}, bf16[56,1024]{1,0:T(8,128)(2,1)S(1)}, u32[]{:S(2)}, u32[]{:S(2)}) collective-permute-start(bf16[56,1024]{1,0:T(8,128)(2,1)S(1)} %get-tuple-element.74), channel_id=1, source_target_pairs={{0,7},{1,4},{2,5},{3,6},{4,3},{5,0},{6,1},{7,2},{8,15},{9,12},{10,... | collective-permute-start | bytes 344072 | tf_op jit(solution)/shard_map/ppermute | solution.py:475
  107.3 0.4 collective-permute-start.13
  107.8 0.3 collective-permute-start.16
  108.1 0.0 collective-permute-done.15.refs_5_
  108.1 0.7 collective-permute-start.12
  108.8 2.2 %collective-permute-done.14.refs_4_ = bf16[56,1024]{1,0:T(8,128)(2,1)S(1)} collective-permute-done((bf16[56,1024]{1,0:T(8,128)(2,1)S(1)}, bf16[56,1024]{1,0:T(8,128)(2,1)S(1)}, u32[]{:S(2)}, u32[]{:S(2)}) %collective-permute-start.14) | collective-permute-done | bytes 114720 | tf_op jit(solution)/shard_map/ppermute | solution.py:475
  111.0 0.2 collective-permute-start.11
  111.3 2.1 %collective-permute-done.17.refs_7_ = bf16[56,1024]{1,0:T(8,128)(2,1)S(1)} collective-permute-done((bf16[56,1024]{1,0:T(8,128)(2,1)S(1)}, bf16[56,1024]{1,0:T(8,128)(2,1)S(1)}, u32[]{:S(2)}, u32[]{:S(2)}) %collective-permute-start.17) | collective-permute-done | bytes 114720 | tf_op jit(solution)/shard_map/ppermute | solution.py:475
  113.4 2.9 %collective-permute-done.13.refs_3_ = bf16[56,1024]{1,0:T(8,128)(2,1)S(1)} collective-permute-done((bf16[56,1024]{1,0:T(8,128)(2,1)S(1)}, bf16[56,1024]{1,0:T(8,128)(2,1)S(1)}, u32[]{:S(2)}, u32[]{:S(2)}) %collective-permute-start.13) | collective-permute-done | bytes 114720 | tf_op jit(solution)/shard_map/ppermute | solution.py:475
  116.3 3.4 %collective-permute-done.11.refs_1_ = bf16[56,1024]{1,0:T(8,128)(2,1)S(1)} collective-permute-done((bf16[56,1024]{1,0:T(8,128)(2,1)S(1)}, bf16[56,1024]{1,0:T(8,128)(2,1)S(1)}, u32[]{:S(2)}, u32[]{:S(2)}) %collective-permute-start.11) | collective-permute-done | bytes 114720 | tf_op jit(solution)/shard_map/ppermute | solution.py:475
  119.7 2.5 %mid_x.3 = bf16[32,8,640]{2,1,0:T(8,128)(2,1)} custom-call(s32[1]{0:T(128)} %bitcast.1.core_ref, bf16[32,8,640]{2,1,0:T(8,128)(2,1)S(1)} %all-to-all-done.3.recv_ref, bf16[16,2,64,128]{3,2,1,0:T(8,128)(2,1)S(1)} %all-to-all-done.1.w0_ref, bf16[16,2,64,128]{3,2,1,0:T(8,128)(2,1)S(1)} %collective-permute-done.7.w1_ref, bf16[288,256]{1,0:T(8,128)(2,1)S(1)} %copy-done.5), custom_call_target="tpu_custom_call" | custom-call | flops 3000000000 | bytes 1048576 | tf_op jit(solution)/shard_map/mid_x/pallas_call | solution.py:244
  122.2 9.2 %all-to-all-start.4 = ((bf16[32,8,640]{2,1,0:T(8,128)(2,1)}), bf16[32,8,640]{2,1,0:T(8,128)(2,1)S(1)}, u32[]{:S(2)}, u32[]{:S(2)}) async-start(bf16[32,8,640]{2,1,0:T(8,128)(2,1)} %mid_x.3), calls=%async_computation.4 | async-start | bytes 655360 | tf_op jit(solution)/shard_map/all_to_all | solution.py:499
  131.4 1.6 mid_y.3
  133.0 0.5 collective-permute-start.18
  133.4 2.4 %collective-permute-start.19 = (bf16[24,1024]{1,0:T(8,128)(2,1)S(1)}, bf16[24,1024]{1,0:T(8,128)(2,1)S(1)}, u32[]{:S(2)}, u32[]{:S(2)}) collective-permute-start(bf16[24,1024]{1,0:T(8,128)(2,1)S(1)} %get-tuple-element.70), channel_id=1, source_target_pairs={{0,2},{1,3},{2,0},{3,1},{4,6},{5,7},{6,4},{7,5},{8,10},{9,11},{10,... | collective-permute-start | bytes 147464 | tf_op jit(solution)/shard_map/ppermute | solution.py:475
  135.8 0.7 collective-permute-start.20
  136.6 0.9 collective-permute-done.18.refs_4_
  137.5 1.1 collective-permute-done.19.refs_5_
  138.6 1.0 collective-permute-done.20.refs_6_
  139.6 6.3 %all-to-all-done.4 = bf16[32,8,640]{2,1,0:T(8,128)(2,1)S(1)} async-done(((bf16[32,8,640]{2,1,0:T(8,128)(2,1)}), bf16[32,8,640]{2,1,0:T(8,128)(2,1)S(1)}, u32[]{:S(2)}, u32[]{:S(2)}) %all-to-all-start.4) | async-done | bytes 327712 | tf_op jit(solution)/shard_map/all_to_all | solution.py:499
  145.9 12.7 %last.3 = bf16[64,64,256]{2,1,0:T(8,128)(2,1)} custom-call(s32[1]{0:T(128)} %bitcast.me_ref.refs_0_, bf16[256,640]{1,0:T(8,128)(2,1)S(1)} %bitcast.26, bf16[16,128]{1,0:T(8,128)(2,1)S(1)} %copy-done.8, bf16[24,1024]{1,0:T(8,128)(2,1)S(1)} %get-tuple-element.68.refs_3_, bf16[24,1024]{1,0:T(8,128)(2,1)S(1)} %collective-permute-done.18.refs_4_, ...), custom_call_target="tpu_custom_call" | custom-call | flops 12000000000 | bytes 1048576 | tf_op jit(solution)/shard_map/last/pallas_call | solution.py:423
  (21 shorter events, 0.1 us)
Async XLA Ops:
  0.0 13.6 %copy-start.1 = (bf16[2,4,2,64,64]{4,3,2,1,0:T(8,128)(2,1)S(1)}, bf16[2,4,2,64,64]{4,3,2,1,0:T(8,128)(2,1)}, u32[]{:S(2)}) copy-start(bf16[2,4,2,64,64]{4,3,2,1,0:T(8,128)(2,1)} %w_ref.2) | copy-start | bytes 393220
  0.0 0.9 copy-start.2
  1.8 27.0 %all-to-all-start.1 = ((bf16[16,2,64,128]{3,2,1,0:T(8,128)(2,1)}), bf16[16,2,64,128]{3,2,1,0:T(8,128)(2,1)S(1)}, u32[]{:S(2)}, u32[]{:S(2)}) async-start(bf16[16,2,64,128]{3,2,1,0:T(8,128)(2,1)} %pack_x.1), calls=%async_computation.1 | async-start | bytes 1048576 | tf_op jit(solution)/shard_map/all_to_all | solution.py:486
  13.6 1.6 %copy-start = (bf16[1,64,64,256]{3,2,1,0:T(8,128)(2,1)S(1)}, bf16[1,64,64,256]{3,2,1,0:T(8,128)(2,1)}, u32[]{:S(2)}) copy-start(bf16[1,64,64,256]{3,2,1,0:T(8,128)(2,1)} %param.9) | copy-start | bytes 6291460
  13.6 1.6 copy-start.7
  13.6 1.6 copy-start.8
  15.2 39.9 %copy-start.5 = (bf16[288,256]{1,0:T(8,128)(2,1)S(1)}, bf16[288,256]{1,0:T(8,128)(2,1)}, u32[]{:S(2)}) copy-start(bf16[288,256]{1,0:T(8,128)(2,1)} %constant.37.clone.tab_ref) | copy-start | bytes 442372
  21.3 1.3 copy-start.9
  28.8 26.2 %all-to-all-start = ((bf16[32,8,640]{2,1,0:T(8,128)(2,1)}), bf16[32,8,640]{2,1,0:T(8,128)(2,1)S(1)}, u32[]{:S(2)}, u32[]{:S(2)}) async-start(bf16[32,8,640]{2,1,0:T(8,128)(2,1)} %bitcast.7), calls=%async_computation | async-start | bytes 655360 | tf_op jit(solution)/shard_map/all_to_all | solution.py:496
  36.3 18.7 %collective-permute-start.7 = (bf16[16,2,64,128]{3,2,1,0:T(8,128)(2,1)S(1)}, bf16[16,2,64,128]{3,2,1,0:T(8,128)(2,1)S(1)}, u32[]{:S(2)}, u32[]{:S(2)}) collective-permute-start(bf16[16,2,64,128]{3,2,1,0:T(8,128)(2,1)S(1)} %all-to-all-done.1.w0_ref), channel_id=1, source_target_pairs={{0,8},{8,0},{16,24},{24,16},{32,40},{40,32},{48,56},{56,48},{64,72... | collective-permute-start | bytes 1572872 | tf_op jit(solution)/shard_map/ppermute | solution.py:471
  36.7 7.0 %collective-permute-start.4 = (bf16[56,1024]{1,0:T(8,128)(2,1)S(1)}, bf16[56,1024]{1,0:T(8,128)(2,1)S(1)}, u32[]{:S(2)}, u32[]{:S(2)}) collective-permute-start(bf16[56,1024]{1,0:T(8,128)(2,1)S(1)} %get-tuple-element.77), channel_id=1, source_target_pairs={{0,2},{1,3},{2,0},{3,1},{4,6},{5,7},{6,4},{7,5},{8,10},{9,11},{10,... | collective-permute-start | bytes 344072 | tf_op jit(solution)/shard_map/ppermute | solution.py:475
  39.5 7.1 %collective-permute-start.3 = (bf16[56,1024]{1,0:T(8,128)(2,1)S(1)}, bf16[56,1024]{1,0:T(8,128)(2,1)S(1)}, u32[]{:S(2)}, u32[]{:S(2)}) collective-permute-start(bf16[56,1024]{1,0:T(8,128)(2,1)S(1)} %get-tuple-element.77), channel_id=1, source_target_pairs={{0,6},{1,7},{2,4},{3,5},{4,2},{5,3},{6,0},{7,1},{8,14},{9,15},{10,... | collective-permute-start | bytes 344072 | tf_op jit(solution)/shard_map/ppermute | solution.py:475
  39.9 11.2 %collective-permute-start.6 = (bf16[56,1024]{1,0:T(8,128)(2,1)S(1)}, bf16[56,1024]{1,0:T(8,128)(2,1)S(1)}, u32[]{:S(2)}, u32[]{:S(2)}) collective-permute-start(bf16[56,1024]{1,0:T(8,128)(2,1)S(1)} %get-tuple-element.78), channel_id=1, source_target_pairs={{0,7},{1,4},{2,5},{3,6},{4,3},{5,0},{6,1},{7,2},{8,15},{9,12},{10,... | collective-permute-start | bytes 344072 | tf_op jit(solution)/shard_map/ppermute | solution.py:475
  43.1 9.4 %collective-permute-start.2 = (bf16[56,1024]{1,0:T(8,128)(2,1)S(1)}, bf16[56,1024]{1,0:T(8,128)(2,1)S(1)}, u32[]{:S(2)}, u32[]{:S(2)}) collective-permute-start(bf16[56,1024]{1,0:T(8,128)(2,1)S(1)} %get-tuple-element.78), channel_id=1, source_target_pairs={{0,3},{1,0},{2,1},{3,2},{4,7},{5,4},{6,5},{7,6},{8,11},{9,8},{10,9... | collective-permute-start | bytes 344072 | tf_op jit(solution)/shard_map/ppermute | solution.py:475
  43.7 8.8 %collective-permute-start.5 = (bf16[56,1024]{1,0:T(8,128)(2,1)S(1)}, bf16[56,1024]{1,0:T(8,128)(2,1)S(1)}, u32[]{:S(2)}, u32[]{:S(2)}) collective-permute-start(bf16[56,1024]{1,0:T(8,128)(2,1)S(1)} %get-tuple-element.79), channel_id=1, source_target_pairs={{0,5},{1,6},{2,7},{3,4},{4,1},{5,2},{6,3},{7,0},{8,13},{9,14},{10,... | collective-permute-start | bytes 344072 | tf_op jit(solution)/shard_map/ppermute | solution.py:475
  46.6 5.9 %collective-permute-start.1 = (bf16[56,1024]{1,0:T(8,128)(2,1)S(1)}, bf16[56,1024]{1,0:T(8,128)(2,1)S(1)}, u32[]{:S(2)}, u32[]{:S(2)}) collective-permute-start(bf16[56,1024]{1,0:T(8,128)(2,1)S(1)} %get-tuple-element.79), channel_id=1, source_target_pairs={{0,1},{1,2},{2,3},{3,0},{4,5},{5,6},{6,7},{7,4},{8,9},{9,10},{10,1... | collective-permute-start | bytes 344072 | tf_op jit(solution)/shard_map/ppermute | solution.py:475
  51.1 3.9 %collective-permute-start = (bf16[56,1024]{1,0:T(8,128)(2,1)S(1)}, bf16[56,1024]{1,0:T(8,128)(2,1)S(1)}, u32[]{:S(2)}, u32[]{:S(2)}) collective-permute-start(bf16[56,1024]{1,0:T(8,128)(2,1)S(1)} %get-tuple-element.44.refs_0_), channel_id=1, source_target_pairs={{0,4},{1,5},{2,6},{3,7},{4,0},{5,1},{6,2},{7,3},{8,12},{9,13},{10,... | collective-permute-start | bytes 344072 | tf_op jit(solution)/shard_map/ppermute | solution.py:475
  55.0 13.4 %copy-start.6 = (bf16[2,8,24,128]{3,2,1,0:T(8,128)(2,1)S(1)}, bf16[2,8,24,128]{3,2,1,0:T(8,128)(2,1)}, u32[]{:S(2)}) copy-start(bf16[2,8,24,128]{3,2,1,0:T(8,128)(2,1)} %constant.38.clone.refs_8_) | copy-start | bytes 294916
  57.5 25.4 %all-to-all-start.2 = ((bf16[32,8,640]{2,1,0:T(8,128)(2,1)}), bf16[32,8,640]{2,1,0:T(8,128)(2,1)S(1)}, u32[]{:S(2)}, u32[]{:S(2)}) async-start(bf16[32,8,640]{2,1,0:T(8,128)(2,1)} %mid_x.2), calls=%async_computation.2 | async-start | bytes 655360 | tf_op jit(solution)/shard_map/all_to_all | solution.py:499
  68.5 14.5 %copy-start.3 = (bf16[2,64,256]{2,1,0:T(8,128)(2,1)S(1)}, bf16[2,64,256]{2,1,0:T(8,128)(2,1)}, u32[]{:S(2)}) copy-start(bf16[2,64,256]{2,1,0:T(8,128)(2,1)} %refs_9_.3) | copy-start | bytes 196612
  68.5 14.5 %copy-start.4 = (bf16[2,256,64]{1,2,0:T(8,128)(2,1)S(1)}, bf16[2,256,64]{1,2,0:T(8,128)(2,1)}, u32[]{:S(2)}) copy-start(bf16[2,256,64]{1,2,0:T(8,128)(2,1)} %param.13) | copy-start | bytes 196612
  70.1 4.9 %collective-permute-start.8 = (bf16[24,1024]{1,0:T(8,128)(2,1)S(1)}, bf16[24,1024]{1,0:T(8,128)(2,1)S(1)}, u32[]{:S(2)}, u32[]{:S(2)}) collective-permute-start(bf16[24,1024]{1,0:T(8,128)(2,1)S(1)} %get-tuple-element.53), channel_id=1, source_target_pairs={{0,1},{1,2},{2,3},{3,0},{4,5},{5,6},{6,7},{7,4},{8,9},{9,10},{10,1... | collective-permute-start | bytes 147464 | tf_op jit(solution)/shard_map/ppermute | solution.py:475
  71.6 5.3 %collective-permute-start.9 = (bf16[24,1024]{1,0:T(8,128)(2,1)S(1)}, bf16[24,1024]{1,0:T(8,128)(2,1)S(1)}, u32[]{:S(2)}, u32[]{:S(2)}) collective-permute-start(bf16[24,1024]{1,0:T(8,128)(2,1)S(1)} %get-tuple-element.54), channel_id=1, source_target_pairs={{0,2},{1,3},{2,0},{3,1},{4,6},{5,7},{6,4},{7,5},{8,10},{9,11},{10,... | collective-permute-start | bytes 147464 | tf_op jit(solution)/shard_map/ppermute | solution.py:475
  73.9 3.2 %collective-permute-start.10 = (bf16[24,1024]{1,0:T(8,128)(2,1)S(1)}, bf16[24,1024]{1,0:T(8,128)(2,1)S(1)}, u32[]{:S(2)}, u32[]{:S(2)}) collective-permute-start(bf16[24,1024]{1,0:T(8,128)(2,1)S(1)} %get-tuple-element.55), channel_id=1, source_target_pairs={{0,3},{1,0},{2,1},{3,2},{4,7},{5,4},{6,5},{7,6},{8,11},{9,8},{10,9... | collective-permute-start | bytes 147464 | tf_op jit(solution)/shard_map/ppermute | solution.py:475
  94.1 1.3 copy-start.10
  95.4 24.3 %all-to-all-start.3 = ((bf16[32,8,640]{2,1,0:T(8,128)(2,1)}), bf16[32,8,640]{2,1,0:T(8,128)(2,1)S(1)}, u32[]{:S(2)}, u32[]{:S(2)}) async-start(bf16[32,8,640]{2,1,0:T(8,128)(2,1)} %bitcast.14), calls=%async_computation.3 | async-start | bytes 655360 | tf_op jit(solution)/shard_map/all_to_all | solution.py:496
  100.9 7.2 %collective-permute-start.15 = (bf16[56,1024]{1,0:T(8,128)(2,1)S(1)}, bf16[56,1024]{1,0:T(8,128)(2,1)S(1)}, u32[]{:S(2)}, u32[]{:S(2)}) collective-permute-start(bf16[56,1024]{1,0:T(8,128)(2,1)S(1)} %get-tuple-element.73), channel_id=1, source_target_pairs={{0,2},{1,3},{2,0},{3,1},{4,6},{5,7},{6,4},{7,5},{8,10},{9,11},{10,... | collective-permute-start | bytes 344072 | tf_op jit(solution)/shard_map/ppermute | solution.py:475
  103.6 7.4 %collective-permute-start.14 = (bf16[56,1024]{1,0:T(8,128)(2,1)S(1)}, bf16[56,1024]{1,0:T(8,128)(2,1)S(1)}, u32[]{:S(2)}, u32[]{:S(2)}) collective-permute-start(bf16[56,1024]{1,0:T(8,128)(2,1)S(1)} %get-tuple-element.73), channel_id=1, source_target_pairs={{0,6},{1,7},{2,4},{3,5},{4,2},{5,3},{6,0},{7,1},{8,14},{9,15},{10,... | collective-permute-start | bytes 344072 | tf_op jit(solution)/shard_map/ppermute | solution.py:475
  103.7 9.7 %collective-permute-start.17 = (bf16[56,1024]{1,0:T(8,128)(2,1)S(1)}, bf16[56,1024]{1,0:T(8,128)(2,1)S(1)}, u32[]{:S(2)}, u32[]{:S(2)}) collective-permute-start(bf16[56,1024]{1,0:T(8,128)(2,1)S(1)} %get-tuple-element.74), channel_id=1, source_target_pairs={{0,7},{1,4},{2,5},{3,6},{4,3},{5,0},{6,1},{7,2},{8,15},{9,12},{10,... | collective-permute-start | bytes 344072 | tf_op jit(solution)/shard_map/ppermute | solution.py:475
  107.3 9.0 %collective-permute-start.13 = (bf16[56,1024]{1,0:T(8,128)(2,1)S(1)}, bf16[56,1024]{1,0:T(8,128)(2,1)S(1)}, u32[]{:S(2)}, u32[]{:S(2)}) collective-permute-start(bf16[56,1024]{1,0:T(8,128)(2,1)S(1)} %get-tuple-element.74), channel_id=1, source_target_pairs={{0,3},{1,0},{2,1},{3,2},{4,7},{5,4},{6,5},{7,6},{8,11},{9,8},{10,9... | collective-permute-start | bytes 344072 | tf_op jit(solution)/shard_map/ppermute | solution.py:475
  107.8 8.5 %collective-permute-start.16 = (bf16[56,1024]{1,0:T(8,128)(2,1)S(1)}, bf16[56,1024]{1,0:T(8,128)(2,1)S(1)}, u32[]{:S(2)}, u32[]{:S(2)}) collective-permute-start(bf16[56,1024]{1,0:T(8,128)(2,1)S(1)} %get-tuple-element.75), channel_id=1, source_target_pairs={{0,5},{1,6},{2,7},{3,4},{4,1},{5,2},{6,3},{7,0},{8,13},{9,14},{10,... | collective-permute-start | bytes 344072 | tf_op jit(solution)/shard_map/ppermute | solution.py:475
  108.1 8.2 %collective-permute-start.12 = (bf16[56,1024]{1,0:T(8,128)(2,1)S(1)}, bf16[56,1024]{1,0:T(8,128)(2,1)S(1)}, u32[]{:S(2)}, u32[]{:S(2)}) collective-permute-start(bf16[56,1024]{1,0:T(8,128)(2,1)S(1)} %get-tuple-element.75), channel_id=1, source_target_pairs={{0,1},{1,2},{2,3},{3,0},{4,5},{5,6},{6,7},{7,4},{8,9},{9,10},{10,1... | collective-permute-start | bytes 344072 | tf_op jit(solution)/shard_map/ppermute | solution.py:475
  111.0 8.7 %collective-permute-start.11 = (bf16[56,1024]{1,0:T(8,128)(2,1)S(1)}, bf16[56,1024]{1,0:T(8,128)(2,1)S(1)}, u32[]{:S(2)}, u32[]{:S(2)}) collective-permute-start(bf16[56,1024]{1,0:T(8,128)(2,1)S(1)} %get-tuple-element.60.refs_0_), channel_id=1, source_target_pairs={{0,4},{1,5},{2,6},{3,7},{4,0},{5,1},{6,2},{7,3},{8,12},{9,13},{10,... | collective-permute-start | bytes 344072 | tf_op jit(solution)/shard_map/ppermute | solution.py:475
  122.2 23.7 %all-to-all-start.4 = ((bf16[32,8,640]{2,1,0:T(8,128)(2,1)}), bf16[32,8,640]{2,1,0:T(8,128)(2,1)S(1)}, u32[]{:S(2)}, u32[]{:S(2)}) async-start(bf16[32,8,640]{2,1,0:T(8,128)(2,1)} %mid_x.3), calls=%async_computation.4 | async-start | bytes 655360 | tf_op jit(solution)/shard_map/all_to_all | solution.py:499
  133.0 4.5 %collective-permute-start.18 = (bf16[24,1024]{1,0:T(8,128)(2,1)S(1)}, bf16[24,1024]{1,0:T(8,128)(2,1)S(1)}, u32[]{:S(2)}, u32[]{:S(2)}) collective-permute-start(bf16[24,1024]{1,0:T(8,128)(2,1)S(1)} %get-tuple-element.69), channel_id=1, source_target_pairs={{0,1},{1,2},{2,3},{3,0},{4,5},{5,6},{6,7},{7,4},{8,9},{9,10},{10,1... | collective-permute-start | bytes 147464 | tf_op jit(solution)/shard_map/ppermute | solution.py:475
  133.4 5.2 %collective-permute-start.19 = (bf16[24,1024]{1,0:T(8,128)(2,1)S(1)}, bf16[24,1024]{1,0:T(8,128)(2,1)S(1)}, u32[]{:S(2)}, u32[]{:S(2)}) collective-permute-start(bf16[24,1024]{1,0:T(8,128)(2,1)S(1)} %get-tuple-element.70), channel_id=1, source_target_pairs={{0,2},{1,3},{2,0},{3,1},{4,6},{5,7},{6,4},{7,5},{8,10},{9,11},{10,... | collective-permute-start | bytes 147464 | tf_op jit(solution)/shard_map/ppermute | solution.py:475
  135.8 3.8 %collective-permute-start.20 = (bf16[24,1024]{1,0:T(8,128)(2,1)S(1)}, bf16[24,1024]{1,0:T(8,128)(2,1)S(1)}, u32[]{:S(2)}, u32[]{:S(2)}) collective-permute-start(bf16[24,1024]{1,0:T(8,128)(2,1)S(1)} %get-tuple-element.71), channel_id=1, source_target_pairs={{0,3},{1,0},{2,1},{3,2},{4,7},{5,4},{6,5},{7,6},{8,11},{9,8},{10,9... | collective-permute-start | bytes 147464 | tf_op jit(solution)/shard_map/ppermute | solution.py:475
